TPU v7x, 32 devices: a whole 2x2x4 slice. The times are simulated.
32 devices in a mesh: doc: 8 (over z, y), term: 4 (over x, core).
Axes of the slice: x: 2, y: 2, z: 4, core: 2. Of those that a mesh axis runs over, the one named last changes fastest.
Arguments:
- tfidf: bfloat16 [4096, 8192], P('term', 'doc'), may hold values from 50 to 1000
- pattern: int32 [32, 64], P('term', 'doc'), may hold values 0 or 1
- factor_w: bfloat16 [4096, 256], P('term'), may hold values from 0.29882812 to 3
- factor_h: bfloat16 [256, 8192], P(None, 'doc'), may hold values from 0.29882812 to 3
Outputs:
- updated_w: bfloat16 [4096, 256], P('term')
- updated_h: bfloat16 [256, 8192], P(None, 'doc')
All inputs are finite; a program needn't handle non-finite values. No bound on the sum of `pattern` on one device may be relied on, other than what follows from the above.
Results may differ from a plain program's by a relative error of at most 0.0004.
The roundings to bfloat16 on the way count: a program that leaves them out, or rounds other values in their place, can miss the bound.
Values may be sent and summed in bfloat16 or wider, within the bound.
No kernel may reach another device: no remote copies, remote signals or barrier semaphores. Data moves between devices by JAX's collectives and lax.ppermute only.
A program may use at most 64 MiB of HBM per device.

v0:
```python
import jax
import jax.numpy as jnp
from jax import lax
from jax.sharding import PartitionSpec as P

BLOCK = 128


def expand(pattern):
    block_rows, block_cols = pattern.shape
    spread = jnp.broadcast_to(pattern[:, None, :, None], (block_rows, BLOCK, block_cols, BLOCK))
    return spread.reshape(block_rows * BLOCK, block_cols * BLOCK)


def contract_first(operand_one, operand_two):
    return lax.dot_general(
        operand_one, operand_two, (((0,), (0,)), ((), ())), preferred_element_type=jnp.float32
    )


def contract_last(operand_one, operand_two):
    return lax.dot_general(
        operand_one, operand_two, (((1,), (1,)), ((), ())), preferred_element_type=jnp.float32
    )


def on_device(tfidf, pattern, factor_w, factor_h):
    masked = tfidf * expand(pattern).astype(jnp.bfloat16)
    gram_part = contract_first(factor_w, factor_w)
    numer_part = contract_first(factor_w, masked)
    gram_w = lax.psum(gram_part, "term")
    numerator = lax.psum_scatter(numer_part, "term", scatter_dimension=1, tiled=True)
    share_width = numerator.shape[1]
    old_share = lax.dynamic_slice_in_dim(
        factor_h, lax.axis_index("term") * share_width, share_width, 1
    )
    denominator = jnp.dot(
        gram_w.astype(jnp.bfloat16), old_share, preferred_element_type=jnp.float32
    )
    h_part = (old_share.astype(jnp.float32) * numerator / denominator).astype(jnp.bfloat16)
    new_h = lax.all_gather(h_part, "term", axis=1, tiled=True)
    gram_h_part = contract_last(new_h, new_h)
    term_topic, gram_h = lax.psum((contract_last(masked, new_h), gram_h_part), "doc")
    denominator = jnp.dot(factor_w, gram_h.astype(jnp.bfloat16), preferred_element_type=jnp.float32)
    new_w = (factor_w.astype(jnp.float32) * term_topic / denominator).astype(jnp.bfloat16)
    return (new_w, new_h)


def solution(mesh):
    placed = (P("term", "doc"), P("term", "doc"), P("term", None), P(None, "doc"))
    return jax.shard_map(
        on_device,
        mesh=mesh,
        in_specs=placed,
        out_specs=(P("term", None), P(None, "doc")),
        check_vma=False,
    )
```

profile of v0, /device:TPU:0, one launch (start us, length us, event | category | flops | bytes accessed | tf_op | source)
XLA Modules:
  0.0 143.6 jit_solution(14670027527547338195)
XLA Ops:
  7.2 0.0 copy-start
  7.2 0.0 copy-start.1
  7.2 0.0 reduce-scatter.2.cloned.1.call-start
  7.2 0.8 convert_element_type.26
  8.0 0.3 broadcast_in_dim.2
  8.4 0.0 copy-start.2
  8.4 1.3 copy-done.2
  9.7 0.0 copy-done.1
  9.7 3.5 %convolution_bitcast_fusion = f32[256,1024]{0,1:T(8,128)} fusion(bf16[1024,256]{1,0:T(8,128)(2,1)S(1)} %copy-done.1, bf16[1024,1024]{1,0:T(8,128)(2,1)} %param.4, bf16[128,8,8,128]{3,2,1,0:T(8,128)(2,1)S(1)} %bitcast.24), kind=kOutput, calls=%fused_computation.1 | convolution fusion | flops 537919488 | bytes 5767168 | tf_op jit(solution)/shard_map/dot_general | solution.py:16
  13.2 0.0 reduce-scatter.2.cloned.1.call-update
  13.3 0.0 all-reduce.4.cloned.1.call-start
  13.4 0.1 copy.12
  13.5 0.3 fusion.6
  13.8 16.3 %all-reduce.5 = bf16[256,256]{1,0:T(8,128)(2,1)S(1)} all-reduce(f32[256,256]{1,0:T(8,128)S(1)} %fusion.6), channel_id=1, replica_groups=mesh['doc'=8,'term'=4] {'term'}, use_global_device_ids=true, to_apply=%region_1.0 | all-reduce | flops 65536 | bytes 393216 | tf_op jit(solution)/shard_map/psum | solution.py:31
  30.1 10.8 %reduce-scatter.2.cloned.1.call-done = f32[256,256]{0,1:T(8,128)} async-done(((f32[256,1024]{0,1:T(8,128)}), f32[256,256]{0,1:T(8,128)}) %reduce-scatter.2.cloned.1.call-update) | async-done | bytes 262160 | tf_op jit(solution)/shard_map/reduce_scatter | solution.py:32
  40.9 1.2 fusion.2
  42.1 6.6 %all_gather.3 = bf16[256,1024]{0,1:T(8,128)(2,1)S(1)} all-gather(bf16[256,256]{0,1:T(8,128)(2,1)S(1)} %fusion.2), channel_id=1, replica_groups=mesh['doc'=8,'term'=4] {'term'}, dimensions={1}, use_global_device_ids=true | all-gather | bytes 655360 | tf_op jit(solution)/shard_map/all_gather | solution.py:41
  48.7 3.9 %fusion.3 = f32[1024,256]{1,0:T(8,128)} fusion(bf16[256,1024]{0,1:T(8,128)(2,1)S(1)} %all_gather.3, bf16[1024,1024]{1,0:T(8,128)(2,1)} %param.4, bf16[128,8,8,128]{3,2,1,0:T(8,128)(2,1)} %bitcast.25), kind=kOutput, calls=%fused_computation.7 | convolution fusion | flops 537919488 | bytes 5767168 | tf_op jit(solution)/shard_map/dot_general | solution.py:22
  52.6 0.0 all-reduce.4.cloned.1.call-update
  52.6 1.0 copy.9
  53.6 0.3 fusion.7
  54.0 41.6 %all-reduce.6 = bf16[256,256]{1,0:T(8,128)(2,1)S(1)} all-reduce(f32[256,256]{1,0:T(8,128)S(1)} %fusion.7), channel_id=1, replica_groups=mesh['doc'=8,'term'=4] {'doc'}, use_global_device_ids=true, to_apply=%region_3.0 | all-reduce | flops 65536 | bytes 393216 | tf_op jit(solution)/shard_map/psum | solution.py:43
  95.6 38.9 %all-reduce.4.cloned.1.call-done = f32[1024,256]{1,0:T(8,128)} async-done(((f32[1024,256]{1,0:T(8,128)}), f32[1024,256]{1,0:T(8,128)}) %all-reduce.4.cloned.1.call-update) | async-done | bytes 1048592 | tf_op jit(solution)/shard_map/psum | solution.py:43
  134.5 2.3 %fusion.1 = bf16[1024,256]{1,0:T(8,128)(2,1)} fusion(bf16[1024,256]{1,0:T(8,128)(2,1)S(1)} %copy-done.1, f32[1024,256]{1,0:T(8,128)} %all-reduce.4.cloned.1.call-done, bf16[256,256]{1,0:T(8,128)(2,1)S(1)} %all-reduce.6), kind=kOutput, calls=%fused_computation.4 | convolution fusion | flops 135266304 | bytes 2228224 | tf_op jit(solution)/shard_map/dot_general | solution.py:44
  (2 shorter events, 0.0 us)
Async XLA Ops:
  7.2 6.2 %copy-start = (bf16[256,1024]{1,0:T(8,128)(2,1)S(1)}, bf16[256,1024]{1,0:T(8,128)(2,1)}, u32[]{:S(2)}) copy-start(bf16[256,1024]{1,0:T(8,128)(2,1)} %param.7) | copy-start | bytes 1572868
  7.2 2.5 %copy-start.1 = (bf16[1024,256]{1,0:T(8,128)(2,1)S(1)}, bf16[1024,256]{1,0:T(8,128)(2,1)}, u32[]{:S(2)}) copy-start(bf16[1024,256]{1,0:T(8,128)(2,1)} %param.6) | copy-start | bytes 1572868
  7.2 33.7 %reduce-scatter.2.cloned.1.call-start = ((), (), s32[]{:S(2)}) async-start(), calls=%async_computation.1 | async-start | bytes 1310720 | tf_op jit(solution)/shard_map/reduce_scatter | solution.py:32
  8.4 1.4 copy-start.2
  13.3 121.2 %all-reduce.4.cloned.1.call-start = ((), (), s32[]{:S(2)}) async-start(), calls=%async_computation.2 | async-start | bytes 2097152 | tf_op jit(solution)/shard_map/psum | solution.py:43
Sparse Core Ops, SparseCore 0:
  13.4 27.4 reduce-scatter.1
  52.8 81.6 all-reduce.3
where the time goes:
time: 144 us
  blocking collectives  64.4 us (45%)
  waiting for transfers between devices  49.8 us (35%)
  between operations  14.1 us (10%)
  matrix products  11.6 us (8%)
  local copies, waits for them, and re-layouts  2.82 us (2%)
    psum x1, blocking collectives, on_device(): lax.psum((contract_last(masked, new_h), gram_h_part), 'doc')  41.6 us
    psum x1, waiting for transfers between devices, on_device(): lax.psum((contract_last(masked, new_h), gram_h_part), 'doc')  38.9 us
    psum x1, blocking collectives, on_device(): gram_w = lax.psum(gram_part, 'term')  16.3 us
    reduce_scatter x1, waiting for transfers between devices, on_device(): lax.psum_scatter(numer_part, 'term', scatter_dimension=1, tiled=True)  10.8 us
    all_gather x1, blocking collectives, on_device(): new_h = lax.all_gather(h_part, 'term', axis=1, tiled=True)  6.58 us
    dot_general x2, matrix products, contract_last(): lax.dot_general(operand_one, operand_two, (((1,), (1,)), ((), ())), prefe...  4.26 us
    dot_general x2, matrix products, contract_first(): lax.dot_general(operand_one, operand_two, (((0,), (0,)), ((), ())), prefe...  3.86 us
  transfers between devices with their start and end apart: 2, of which 2 were waited for; matrix products, arithmetic and copies ran while one was open for 1% of the time, Pallas kernels for 0%

commit v1 on v0

v1 whole, which is shorter than its diff:
```python
import functools

import jax
import jax.numpy as jnp
from jax import lax
from jax.experimental import pallas as pl
from jax.experimental.pallas import tpu as pltpu
from jax.sharding import PartitionSpec as P


BLOCK = 128
F32 = jnp.float32
BF16 = jnp.bfloat16
VMEM = pl.BlockSpec(memory_space=pltpu.VMEM)
HBM = pl.BlockSpec(memory_space=pltpu.HBM)
PIECES = 4
LIMIT = 50 << 20


def nt(a, b):
    return lax.dot_general(a, b, (((1,), (1,)), ((), ())), preferred_element_type=F32)


def nn(a, b):
    return lax.dot_general(a, b, (((1,), (0,)), ((), ())), preferred_element_type=F32)


def call(body, out, args, hbm=(), scratch=(), flops=1 << 20, moved=1 << 20, limit=24 << 20):
    return pl.pallas_call(
        body,
        out_shape=out,
        in_specs=[HBM if i in hbm else VMEM for i in range(len(args))],
        out_specs=jax.tree.map(lambda _: VMEM, out),
        scratch_shapes=list(scratch),
        compiler_params=pltpu.CompilerParams(vmem_limit_bytes=limit),
        cost_estimate=pl.CostEstimate(flops=flops, bytes_accessed=moved, transcendentals=0),
    )(*args)


def like(*shape, dtype=F32):
    return jax.ShapeDtypeStruct(shape, dtype)


def core_index():
    return lax.axis_index("term") & 1


def doc_bit(bit):
    return (lax.axis_index("doc") >> bit) & 1


def pack(gram, core):
    k = gram.shape[0]
    h, q = k // 2, k // 4
    e = q // 2
    if core == 0:
        diag, off = gram[:h, :h], gram[:q, h:]
    else:
        diag, off = gram[h:, h:], gram[q:h, h:]
    top = jnp.concatenate([diag[:q], diag[q:]], axis=1)
    low = jnp.concatenate([off[:e], off[e:]], axis=1)
    return jnp.concatenate([top, low], axis=0)


def unpack(one, two):
    k = one.shape[1]
    h, q = k // 2, k // 4
    e = q // 2

    def parts(p):
        diag = jnp.concatenate([p[:q, :h], p[:q, h:]], axis=0)
        off = jnp.concatenate([p[q : q + e, :h], p[q : q + e, h:]], axis=0)
        return diag, off

    diag_one, off_one = parts(one)
    diag_two, off_two = parts(two)
    off = jnp.concatenate([off_one, off_two], axis=0)
    upper = jnp.concatenate([diag_one, off], axis=1)
    lower = jnp.concatenate([off.T, diag_two], axis=1)
    return jnp.concatenate([upper, lower], axis=0)


def pick(core, one, two):
    return jnp.where(core == 0, one, two)


def mask_rows(pattern, half, cols):
    blocks = cols // BLOCK
    lane = lax.broadcasted_iota(jnp.int32, (pattern.shape[0], cols), 1) // BLOCK
    mask = jnp.zeros((pattern.shape[0], cols), F32)
    for c in range(blocks):
        column = pick(half, pattern[:, c : c + 1], pattern[:, blocks + c : blocks + c + 1])
        mask = jnp.where(lane == c, column.astype(F32), mask)
    return mask


def masked_piece(tile_ref, mask, piece, rows):
    out = []
    for r in range(rows // BLOCK):
        first = piece * rows + r * BLOCK
        line = mask[first // BLOCK : first // BLOCK + 1, :].astype(BF16)
        out.append(tile_ref[first : first + BLOCK, :] * line)
    return jnp.concatenate(out, axis=0)


def load_body(m, w, wt, send, keep, own, other, w_all, sems):
    core = core_index()
    terms, cols = own.shape
    k = w.shape[1]
    rows = terms // PIECES
    columns = lambda side: pl.ds(pl.multiple_of(side * cols, cols), cols)
    copies = []
    for i in range(PIECES):
        part = pl.ds(i * rows, rows)
        copies.append(pltpu.make_async_copy(w.at[part, :], w_all.at[part, :], sems.at[i]))
    copies.append(pltpu.make_async_copy(m.at[:, columns(1 - core)], other, sems.at[PIECES]))
    copies.append(pltpu.make_async_copy(m.at[:, columns(core)], own, sems.at[PIECES + 1]))
    for copy in copies:
        copy.start()
    gram = jnp.zeros((k, k), F32)
    for i in range(PIECES):
        part = slice(i * rows, (i + 1) * rows)
        copies[i].wait()
        piece = w_all[part, :]
        flipped = piece.T
        wt[:, part] = flipped
        gram += nn(flipped, piece)
    one, two = pack(gram, 0), pack(gram, 1)
    send[...] = pick(core, two, one)
    keep[...] = pick(core, one, two)
    for copy in copies[PIECES:]:
        copy.wait()


def half_h_body(h, out):
    cols = out.shape[1]
    out[...] = h[:, pl.ds(pl.multiple_of(core_index() * cols, cols), cols)]


def numer_body(half, pattern, wt, *refs, other):
    out, masked = refs[-2:]
    side = 1 - core_index() if other else core_index()
    terms, cols = half.shape
    rows = terms // PIECES
    mask = mask_rows(pattern[...], side, cols)
    for i in range(PIECES):
        part = slice(i * rows, (i + 1) * rows)
        tile = masked_piece(half, mask, i, rows)
        masked[part, :] = tile
        product = nn(wt[:, part], tile)
        if i == 0:
            out[...] = product
        else:
            out[...] += product


def add_body(a, b, out):
    out[...] = a[...] + b[...]


def round_add_body(a, b, out):
    out[...] = (a[...] + b[...]).astype(BF16)


def new_h_body(mine, other, gram_mine, gram_other, h, out):
    core = core_index()
    a, b = gram_mine[...], gram_other[...]
    gram = unpack(pick(core, a, b), pick(core, b, a))
    old = h[...]
    total = mine[...] + other[...]
    out[...] = (old.astype(F32) * total / nn(gram, old)).astype(BF16)


def first_w_body(masked, h, out):
    step = masked.shape[0] // 2
    for r in range(2):
        part = slice(r * step, (r + 1) * step)
        out[part, :] = nt(masked[part, :], h[...])


def split_rows(parts, outs, gram, merged):
    size = parts[0][0].shape[0]
    for side in range(2):
        if merged:
            outs[side][:size, :] = parts[0][side]
            outs[side][size : 2 * size, :] = parts[1][side]
            outs[side][2 * size :, :] = gram
        else:
            outs[side][:size, :] = parts[0][side]
            outs[side][size:, :] = gram
            outs[2 + side][...] = parts[1][side]


def second_w_body(masked, part, h, h_own, *outs, bits, merged):
    rows, cols = masked.shape
    core = core_index()
    size = rows // 4
    new_h = outs[-1]

    def piece(start_block):
        start = pl.multiple_of(start_block * size, size)
        return part[pl.ds(start, size), :] + nt(masked[pl.ds(start, size), :], h[...])

    bit_a, bit_b = doc_bit(bits[0]), doc_bit(bits[1])
    gram = nt(h[...], h[...]) + nt(h_own[...], h_own[...])
    mine = pick(core, pack(gram, 0), pack(gram, 1))
    parts = ((piece(1 - bit_a), piece(bit_a)), (piece(3 - bit_b), piece(2 + bit_b)))
    split_rows(parts, outs, mine, merged)
    new_h[:, pl.ds(pl.multiple_of((1 - core) * cols, cols), cols)] = h[...]
    new_h[:, pl.ds(pl.multiple_of(core * cols, cols), cols)] = h_own[...]


def arrived(refs, merged, size):
    if merged:
        total = refs[0][...] + refs[1][...]
        return total[:size], total[size : 2 * size], total[2 * size :]
    a = refs[0][...] + refs[1][...]
    return a[:size], refs[2][...] + refs[3][...], a[size:]


def halve_body(*refs, size, bits, was_merged, merged):
    given = 2 if was_merged else 4
    a, b, gram = arrived(refs[:given], was_merged, size)
    half = size // 2
    parts = []
    for bit, x in ((doc_bit(bits[0]), a), (doc_bit(bits[1]), b)):
        low, high = x[:half], x[half:]
        parts.append((pick(bit, high, low), pick(bit, low, high)))
    split_rows(parts, refs[given:], gram, merged)


def gram_h_body(*refs, size, merged):
    refs[-1][...] = arrived(refs[:-1], merged, size)[2].astype(BF16)


def new_w_body(gram_mine, gram_other, wa, wb, *refs, size, merged):
    core = core_index()
    one, two = gram_mine[...], gram_other[...]
    gram = unpack(pick(core, one, two), pick(core, two, one))
    a, b, _ = arrived(refs[:-1], merged, size)
    out = refs[-1]
    for first, old_ref, total in ((0, wa, a), (size, wb, b)):
        old = old_ref[...]
        out[first : first + size, :] = (old.astype(F32) * total / nn(old, gram)).astype(BF16)


def swap(x, axis, size, bit):
    return lax.ppermute(x, axis, [(i, i ^ (1 << bit)) for i in range(size)])


def join(bit, mine, other):
    return jnp.concatenate([jnp.where(bit == 0, mine, other), jnp.where(bit == 0, other, mine)], axis=0)


def on_device(m, pattern, w, h, *, n_doc, n_term):
    return update(m, pattern, w, h, n_doc, n_term)


def update(m, pattern, w, h, n_doc, n_term):
    terms, docs = m.shape
    k = w.shape[1]
    half = docs // 2
    pk = 3 * k // 8
    bits = n_doc.bit_length() - 1
    term_bits = n_term.bit_length() - 1
    order = [tuple(pair) for pair in zip(range(bits), [1, 0] + list(range(2, bits)))]
    same = [one == two for one, two in order]

    def over_term(x, bit):
        return swap(x, "term", n_term, bit)

    def over_doc(x, bit):
        return swap(x, "doc", n_doc, bit)

    flops = terms * docs * k
    moved = 2 * terms * docs

    side = like(terms, half, dtype=BF16)
    wt, g_send, g_keep, own, other = call(
        load_body,
        (like(k, terms, dtype=BF16), like(pk, k), like(pk, k), side, side),
        (m, w),
        hbm=(0, 1),
        scratch=(pltpu.VMEM((terms, k), BF16), pltpu.SemaphoreType.DMA((PIECES + 2,))),
        limit=LIMIT,
    )
    g_got = over_term(g_send, 0)

    def numer(half_m, is_other, *after):
        body = functools.partial(numer_body, other=is_other)
        return call(body, (like(k, half), side), (half_m, pattern, wt, *after), flops=flops, moved=moved)

    n_send, masked_other = numer(other, True)
    n_got = over_term(n_send, 0)
    g_sum = call(add_body, like(pk, k), (g_keep, g_got))
    for bit in range(1, term_bits - 1):
        g_sum = g_sum + over_term(g_sum, bit)
    g_far = over_term(g_sum, term_bits - 1)
    n_keep, masked_own = numer(own, False, g_sum)
    h_old = call(half_h_body, like(k, half, dtype=BF16), (h,))
    n_sum = call(add_body, like(k, half), (n_keep, n_got))
    for bit in range(1, term_bits - 1):
        n_sum = n_sum + over_term(n_sum, bit)
    n_far = over_term(n_sum, term_bits - 1)
    g_mine = call(round_add_body, like(pk, k, dtype=BF16), (g_sum, g_far))
    g_other = over_term(g_mine, 0)
    h_own = call(new_h_body, like(k, half, dtype=BF16), (n_sum, n_far, g_mine, g_other, h_old))
    h_other = over_term(h_own, 0)

    part = call(first_w_body, like(terms, k), (masked_own, h_own), flops=flops, moved=moved)
    size = terms // 4

    def pieces(rows, merged):
        if merged:
            return (like(2 * rows + pk, k),) * 2
        return (like(rows + pk, k),) * 2 + (like(rows, k),) * 2

    *state, new_h = call(
        functools.partial(second_w_body, bits=order[0], merged=same[0]),
        pieces(size, same[0]) + (like(k, docs, dtype=BF16),),
        (masked_other, part, h_other, h_own),
        flops=flops,
        moved=moved,
    )
    for step in range(bits):
        got = [over_doc(state[2 * i], order[step][i]) for i in range(len(state) // 2)]
        refs = []
        for i, x in enumerate(got):
            refs += [state[2 * i + 1], x]
        if step == bits - 1:
            break
        body = functools.partial(
            halve_body, size=size, bits=order[step + 1], was_merged=same[step], merged=same[step + 1]
        )
        size //= 2
        state = call(body, pieces(size, same[step + 1]), refs)
    merged = same[bits - 1]
    g_mine = call(functools.partial(gram_h_body, size=size, merged=merged), like(pk, k, dtype=BF16), refs)
    g_other = over_term(g_mine, 0)
    old = []
    for stream in range(2):
        start = jnp.int32(stream * (terms // 2))
        for step in range(bits):
            start += doc_bit(order[step][stream]) * (terms // 2 >> (step + 1))
        old.append(lax.dynamic_slice_in_dim(w, start, size, 0))
    both = call(
        functools.partial(new_w_body, size=size, merged=merged),
        like(2 * size, k, dtype=BF16),
        (g_mine, g_other, *old, *refs),
    )
    for step in reversed(range(bits)):
        if same[step]:
            got = over_doc(both, order[step][0])
            w_a, w_b = [
                join(doc_bit(order[step][0]), both[i * size : (i + 1) * size], got[i * size : (i + 1) * size])
                for i in range(2)
            ]
        else:
            w_a, w_b = both[:size], both[size:]
            w_a, w_b = [
                join(doc_bit(bit), x, over_doc(x, bit)) for x, bit in zip((w_a, w_b), order[step])
            ]
        size *= 2
        both = jnp.concatenate([w_a, w_b], axis=0)
    return both, new_h


def solution(mesh):
    sizes = dict(mesh.shape)
    return jax.shard_map(
        functools.partial(on_device, n_doc=sizes["doc"], n_term=sizes["term"]),
        mesh=mesh,
        in_specs=(P("term", "doc"), P("term", "doc"), P("term", None), P(None, "doc")),
        out_specs=(P("term", None), P(None, "doc")),
        check_vma=False,
    )
```

time: 144 us -> 79.9 us (0.55)
  blocking collectives: 64.4 us -> 0 us
  starting transfers between devices: 0.08 us -> 19.6 us
  between operations: 14.1 us -> 0.82 us
  matrix products: 11.6 us -> 0 us
  Pallas kernels: 0 us -> 5.97 us
    psum x2 -> x0, blocking collectives: 57.8 us -> none  [the longest x1 41.6 us: on_device(): lax.psum((contract_last(masked, new_h), gram_h_part), 'doc')]
    ppermute x0 -> x17, waiting for transfers between devices: none -> 50.4 us  [swap(): return lax.ppermute(x, axis, [(i, i ^ 1 << bit) for i in range(size)])]
    psum x1 -> x0, waiting for transfers between devices: 38.9 us -> none  [on_device(): lax.psum((contract_last(masked, new_h), gram_h_part), 'doc')]
    ppermute x0 -> x17, starting transfers between devices: none -> 19.6 us  [swap(): return lax.ppermute(x, axis, [(i, i ^ 1 << bit) for i in range(size)])]
    dot_general x6 -> x0, matrix products: 11.6 us -> none  [the longest x2 4.26 us: contract_last(): lax.dot_general(operand_one, operand_two, (((1,), (1,)), ((), ())), prefe...]
    reduce_scatter x1 -> x0, waiting for transfers between devices: 10.8 us -> none  [on_device(): lax.psum_scatter(numer_part, 'term', scatter_dimension=1, tiled=True)]
    all_gather x1 -> x0, blocking collectives: 6.58 us -> none  [on_device(): new_h = lax.all_gather(h_part, 'term', axis=1, tiled=True)]
    pallas_call x0 -> x14, Pallas kernels: none -> 5.97 us  [call(): pl.pallas_call(body, out_shape=out, in_specs=[HBM if i in hbm else VMEM f...]
  transfers between devices with their start and end apart: 2 -> 17, of which waited for: 2 -> 15; matrix products, arithmetic and copies ran while one was open for 1% -> 1% of each run, Pallas kernels for 0% -> 1%
where the time goes in v1:
time: 79.9 us; the launch traced here: 79.7 us
  waiting for transfers between devices  50.4 us (63%)
  starting transfers between devices  19.6 us (25%)
  Pallas kernels  5.97 us (7%)
  local copies, waits for them, and re-layouts  1.83 us (2%)
  other arithmetic  1.01 us (1%)
  between operations  0.82 us (1%)
    ppermute x17, waiting for transfers between devices, swap(): return lax.ppermute(x, axis, [(i, i ^ 1 << bit) for i in range(size)])  50.4 us
    ppermute x17, starting transfers between devices, swap(): return lax.ppermute(x, axis, [(i, i ^ 1 << bit) for i in range(size)])  19.6 us
    pallas_call x14, Pallas kernels, call(): pl.pallas_call(body, out_shape=out, in_specs=[HBM if i in hbm else VMEM f...  5.97 us
  transfers between devices with their start and end apart: 17, of which 15 were waited for; matrix products, arithmetic and copies ran while one was open for 1% of the time, Pallas kernels for 1%

profile of v1, /device:TPU:0, one launch (start us, length us, event | category | flops | bytes accessed | tf_op | source)
XLA Modules:
  0.0 79.7 jit_solution(1714715367927173974)
XLA Ops:
  0.6 1.0 %copy-done = bf16[1024,256]{1,0:T(8,128)(2,1)S(1)} copy-done((bf16[1024,256]{1,0:T(8,128)(2,1)S(1)}, bf16[1024,256]{1,0:T(8,128)(2,1)}, u32[]{:S(2)}) %copy-start) | copy-done | bytes 524312
  1.7 2.2 %shard_map.59 = (bf16[256,1024]{1,0:T(8,128)(2,1)S(1)}, f32[96,256]{1,0:T(8,128)S(1)}, f32[96,256]{1,0:T(8,128)S(1)}, bf16[1024,512]{1,0:T(8,128)(2,1)S(1)}, bf16[1024,512]{1,0:T(8,128)(2,1)S(1)}) custom-call(bf16[1024,1024]{1,0:T(8,128)(2,1)} %m.1, bf16[1024,256]{1,0:T(8,128)(2,1)S(1)} %copy-done), custom_call_target="tpu_custom_call" | custom-call | flops 1048576 | bytes 1048576 | tf_op jit(solution)/shard_map/pallas_call | solution.py:29
  5.2 1.6 %collective-permute-done.b = f32[96,256]{1,0:T(8,128)S(1)} collective-permute-done((f32[96,256]{1,0:T(8,128)S(1)}, f32[96,256]{1,0:T(8,128)S(1)}, u32[]{:S(2)}, u32[]{:S(2)}) %collective-permute-start) | collective-permute-done | bytes 98336 | tf_op jit(solution)/shard_map/ppermute | solution.py:248
  7.5 2.9 %collective-permute-start.2 = (f32[256,512]{1,0:T(8,128)S(1)}, f32[256,512]{1,0:T(8,128)S(1)}, u32[]{:S(2)}, u32[]{:S(2)}) collective-permute-start(f32[256,512]{1,0:T(8,128)S(1)} %shard_map.63.mine), channel_id=1, source_target_pairs={{0,2},{1,3},{2,0},{3,1},{4,6},{5,7},{6,4},{7,5},{8,10},{9,11},{10,... | collective-permute-start | bytes 1572872 | tf_op jit(solution)/shard_map/ppermute | solution.py:248
  10.5 14.3 %collective-permute-done.3.b = f32[96,256]{1,0:T(8,128)S(1)} collective-permute-done((f32[96,256]{1,0:T(8,128)S(1)}, f32[96,256]{1,0:T(8,128)S(1)}, u32[]{:S(2)}, u32[]{:S(2)}) %collective-permute-start.3) | collective-permute-done | bytes 98336 | tf_op jit(solution)/shard_map/ppermute | solution.py:248
  24.9 1.2 %collective-permute-done.4.gram_other = bf16[96,256]{1,0:T(8,128)(2,1)S(1)} collective-permute-done((bf16[96,256]{1,0:T(8,128)(2,1)S(1)}, bf16[96,256]{1,0:T(8,128)(2,1)S(1)}, u32[]{:S(2)}, u32[]{:S(2)}) %collective-permute-start.4) | collective-permute-done | bytes 49184 | tf_op jit(solution)/shard_map/ppermute | solution.py:248
  27.0 0.9 %collective-permute-done.5.h = bf16[256,512]{1,0:T(8,128)(2,1)S(1)} collective-permute-done((bf16[256,512]{1,0:T(8,128)(2,1)S(1)}, bf16[256,512]{1,0:T(8,128)(2,1)S(1)}, u32[]{:S(2)}, u32[]{:S(2)}) %collective-permute-start.5) | collective-permute-done | bytes 262176 | tf_op jit(solution)/shard_map/ppermute | solution.py:248
  27.9 1.4 %shard_map.68 = (f32[352,256]{1,0:T(8,128)S(1)}, f32[352,256]{1,0:T(8,128)S(1)}, f32[256,256]{1,0:T(8,128)S(1)}, f32[256,256]{1,0:T(8,128)S(1)}, bf16[256,1024]{1,0:T(8,128)(2,1)}) custom-call(bf16[1024,512]{1,0:T(8,128)(2,1)S(1)} %get-tuple-element.24.masked, f32[1024,256]{1,0:T(8,128)S(1)} %shard_map.67.part, ...), custom_call_target="tpu_custom_call" | custom-call | flops 268435456 | bytes 2097152 | tf_op jit(solution)/shard_map/pallas_call | solution.py:29
  29.3 1.8 %collective-permute-start.6 = (f32[352,256]{1,0:T(8,128)S(1)}, f32[352,256]{1,0:T(8,128)S(1)}, u32[]{:S(2)}, u32[]{:S(2)}) collective-permute-start(f32[352,256]{1,0:T(8,128)S(1)} %get-tuple-element.32), channel_id=1, source_target_pairs={{0,4},{4,0},{8,12},{12,8},{16,20},{20,16},{24,28},{28,24},{1,5},{5... | collective-permute-start | bytes 1081352 | tf_op jit(solution)/shard_map/ppermute | solution.py:248
  31.0 1.6 %collective-permute-start.7 = (f32[256,256]{1,0:T(8,128)S(1)}, f32[256,256]{1,0:T(8,128)S(1)}, u32[]{:S(2)}, u32[]{:S(2)}) collective-permute-start(f32[256,256]{1,0:T(8,128)S(1)} %get-tuple-element.34), channel_id=1, source_target_pairs={{0,8},{4,12},{8,0},{12,4},{16,24},{20,28},{24,16},{28,20},{1,9},{5... | collective-permute-start | bytes 786440 | tf_op jit(solution)/shard_map/ppermute | solution.py:248
  32.6 6.5 %collective-permute-done.7.refs_3_ = f32[256,256]{1,0:T(8,128)S(1)} collective-permute-done((f32[256,256]{1,0:T(8,128)S(1)}, f32[256,256]{1,0:T(8,128)S(1)}, u32[]{:S(2)}, u32[]{:S(2)}) %collective-permute-start.7) | collective-permute-done | bytes 262176 | tf_op jit(solution)/shard_map/ppermute | solution.py:248
  39.9 1.9 %collective-permute-start.8 = (f32[224,256]{1,0:T(8,128)S(1)}, f32[224,256]{1,0:T(8,128)S(1)}, u32[]{:S(2)}, u32[]{:S(2)}) collective-permute-start(f32[224,256]{1,0:T(8,128)S(1)} %get-tuple-element.36), channel_id=1, source_target_pairs={{0,8},{4,12},{8,0},{12,4},{16,24},{20,28},{24,16},{28,20},{1,9},{5... | collective-permute-start | bytes 688136 | tf_op jit(solution)/shard_map/ppermute | solution.py:248
  41.7 1.5 %collective-permute-start.9 = (f32[128,256]{1,0:T(8,128)S(1)}, f32[128,256]{1,0:T(8,128)S(1)}, u32[]{:S(2)}, u32[]{:S(2)}) collective-permute-start(f32[128,256]{1,0:T(8,128)S(1)} %get-tuple-element.38), channel_id=1, source_target_pairs={{0,4},{4,0},{8,12},{12,8},{16,20},{20,16},{24,28},{28,24},{1,5},{5... | collective-permute-start | bytes 393224 | tf_op jit(solution)/shard_map/ppermute | solution.py:248
  43.2 3.4 %collective-permute-done.9.refs_3_ = f32[128,256]{1,0:T(8,128)S(1)} collective-permute-done((f32[128,256]{1,0:T(8,128)S(1)}, f32[128,256]{1,0:T(8,128)S(1)}, u32[]{:S(2)}, u32[]{:S(2)}) %collective-permute-start.9) | collective-permute-done | bytes 131104 | tf_op jit(solution)/shard_map/ppermute | solution.py:248
  46.8 2.8 %collective-permute-start.10 = (f32[224,256]{1,0:T(8,128)S(1)}, f32[224,256]{1,0:T(8,128)S(1)}, u32[]{:S(2)}, u32[]{:S(2)}) collective-permute-start(f32[224,256]{1,0:T(8,128)S(1)} %get-tuple-element.40), channel_id=1, source_target_pairs={{0,16},{4,20},{8,24},{12,28},{16,0},{20,4},{24,8},{28,12},{1,17},{... | collective-permute-start | bytes 688136 | tf_op jit(solution)/shard_map/ppermute | solution.py:248
  49.7 9.1 %collective-permute-done.10.refs_1_ = f32[224,256]{1,0:T(8,128)S(1)} collective-permute-done((f32[224,256]{1,0:T(8,128)S(1)}, f32[224,256]{1,0:T(8,128)S(1)}, u32[]{:S(2)}, u32[]{:S(2)}) %collective-permute-start.10) | collective-permute-done | bytes 229408 | tf_op jit(solution)/shard_map/ppermute | solution.py:248
  58.9 0.8 constant_dynamic-slice_fusion
  60.4 6.6 %collective-permute-done.12 = bf16[128,256]{1,0:T(8,128)(2,1)S(1)} collective-permute-done((bf16[128,256]{1,0:T(8,128)(2,1)S(1)}, bf16[128,256]{1,0:T(8,128)(2,1)S(1)}, u32[]{:S(2)}, u32[]{:S(2)}) %collective-permute-start.12) | collective-permute-done | bytes 65568 | tf_op jit(solution)/shard_map/ppermute | solution.py:248
  67.1 1.6 %collective-permute-start.15 = (bf16[128,256]{1,0:T(8,128)(2,1)S(1)}, bf16[128,256]{1,0:T(8,128)(2,1)S(1)}, u32[]{:S(2)}, u32[]{:S(2)}) collective-permute-start(bf16[128,256]{1,0:T(8,128)(2,1)S(1)} %pad_maximum_fusion.4), channel_id=1, source_target_pairs={{0,4},{4,0},{8,12},{12,8},{16,20},{20,16},{24,28},{28,24},{1,5},{5... | collective-permute-start | bytes 196616 | tf_op jit(solution)/shard_map/ppermute | solution.py:248
  68.7 2.6 %collective-permute-done.13 = bf16[128,256]{1,0:T(8,128)(2,1)S(1)} collective-permute-done((bf16[128,256]{1,0:T(8,128)(2,1)S(1)}, bf16[128,256]{1,0:T(8,128)(2,1)S(1)}, u32[]{:S(2)}, u32[]{:S(2)}) %collective-permute-start.13) | collective-permute-done | bytes 65568 | tf_op jit(solution)/shard_map/ppermute | solution.py:248
  71.5 1.6 %collective-permute-start.14 = (bf16[256,256]{1,0:T(8,128)(2,1)S(1)}, bf16[256,256]{1,0:T(8,128)(2,1)S(1)}, u32[]{:S(2)}, u32[]{:S(2)}) collective-permute-start(bf16[256,256]{1,0:T(8,128)(2,1)S(1)} %pad_maximum_fusion.1), channel_id=1, source_target_pairs={{0,4},{4,0},{8,12},{12,8},{16,20},{20,16},{24,28},{28,24},{1,5},{5... | collective-permute-start | bytes 393224 | tf_op jit(solution)/shard_map/ppermute | solution.py:248
  73.1 2.7 %collective-permute-start.16 = (bf16[256,256]{1,0:T(8,128)(2,1)S(1)}, bf16[256,256]{1,0:T(8,128)(2,1)S(1)}, u32[]{:S(2)}, u32[]{:S(2)}) collective-permute-start(bf16[256,256]{1,0:T(8,128)(2,1)S(1)} %pad_maximum_fusion.2), channel_id=1, source_target_pairs={{0,8},{4,12},{8,0},{12,4},{16,24},{20,28},{24,16},{28,20},{1,9},{5... | collective-permute-start | bytes 393224 | tf_op jit(solution)/shard_map/ppermute | solution.py:248
  76.6 2.2 %collective-permute-done.16 = bf16[256,256]{1,0:T(8,128)(2,1)S(1)} collective-permute-done((bf16[256,256]{1,0:T(8,128)(2,1)S(1)}, bf16[256,256]{1,0:T(8,128)(2,1)S(1)}, u32[]{:S(2)}, u32[]{:S(2)}) %collective-permute-start.16) | collective-permute-done | bytes 131104 | tf_op jit(solution)/shard_map/ppermute | solution.py:248
  78.8 0.8 %pad_maximum_fusion = bf16[1024,256]{1,0:T(8,128)(2,1)} fusion(bf16[256,256]{1,0:T(8,128)(2,1)S(1)} %get-tuple-element.47, bf16[256,256]{1,0:T(8,128)(2,1)S(1)} %get-tuple-element.46, bf16[256,256]{1,0:T(8,128)(2,1)S(1)} %get-tuple-element.45, bf16[256,256]{1,0:T(8,128)(2,1)S(1)} %get-tuple-element.44), kind=kLoop, calls=%fused_computation | loop fusion | flops 2097152 | bytes 1048576 | tf_op jit(solution)/shard_map/concatenate | solution.py:364
  (40 shorter events, 5.8 us)
Async XLA Ops:
  0.6 1.0 %copy-start = (bf16[1024,256]{1,0:T(8,128)(2,1)S(1)}, bf16[1024,256]{1,0:T(8,128)(2,1)}, u32[]{:S(2)}) copy-start(bf16[1024,256]{1,0:T(8,128)(2,1)} %w.1) | copy-start | bytes 1572868
  1.7 2.3 %copy-start.2 = (s32[8,8]{1,0:T(8,128)S(1)}, s32[8,8]{1,0:T(8,128)}, u32[]{:S(2)}) copy-start(s32[8,8]{1,0:T(8,128)} %pattern.3) | copy-start | bytes 772
  4.5 20.3 %copy-start.1 = (bf16[256,1024]{1,0:T(8,128)(2,1)S(1)}, bf16[256,1024]{1,0:T(8,128)(2,1)}, u32[]{:S(2)}) copy-start(bf16[256,1024]{1,0:T(8,128)(2,1)} %h.1) | copy-start | bytes 1572868
  4.6 2.9 %collective-permute-start.1 = (f32[256,512]{1,0:T(8,128)S(1)}, f32[256,512]{1,0:T(8,128)S(1)}, u32[]{:S(2)}, u32[]{:S(2)}) collective-permute-start(f32[256,512]{1,0:T(8,128)S(1)} %get-tuple-element.30), channel_id=1, source_target_pairs={{0,1},{1,0},{2,3},{3,2},{4,5},{5,4},{6,7},{7,6},{8,9},{9,8},{10,11... | collective-permute-start | bytes 1572872 | tf_op jit(solution)/shard_map/ppermute | solution.py:248
  5.1 1.7 %collective-permute-start = (f32[96,256]{1,0:T(8,128)S(1)}, f32[96,256]{1,0:T(8,128)S(1)}, u32[]{:S(2)}, u32[]{:S(2)}) collective-permute-start(f32[96,256]{1,0:T(8,128)S(1)} %get-tuple-element.27), channel_id=1, source_target_pairs={{0,1},{1,0},{2,3},{3,2},{4,5},{5,4},{6,7},{7,6},{8,9},{9,8},{10,11... | collective-permute-start | bytes 294920 | tf_op jit(solution)/shard_map/ppermute | solution.py:248
  7.5 18.6 %collective-permute-start.2 = (f32[256,512]{1,0:T(8,128)S(1)}, f32[256,512]{1,0:T(8,128)S(1)}, u32[]{:S(2)}, u32[]{:S(2)}) collective-permute-start(f32[256,512]{1,0:T(8,128)S(1)} %shard_map.63.mine), channel_id=1, source_target_pairs={{0,2},{1,3},{2,0},{3,1},{4,6},{5,7},{6,4},{7,5},{8,10},{9,11},{10,... | collective-permute-start | bytes 1572872 | tf_op jit(solution)/shard_map/ppermute | solution.py:248
  10.4 14.3 %collective-permute-start.3 = (f32[96,256]{1,0:T(8,128)S(1)}, f32[96,256]{1,0:T(8,128)S(1)}, u32[]{:S(2)}, u32[]{:S(2)}) collective-permute-start(f32[96,256]{1,0:T(8,128)S(1)} %shard_map.61.refs_0_.a), channel_id=1, source_target_pairs={{0,2},{1,3},{2,0},{3,1},{4,6},{5,7},{6,4},{7,5},{8,10},{9,11},{10,... | collective-permute-start | bytes 294920 | tf_op jit(solution)/shard_map/ppermute | solution.py:248
  24.8 1.3 %collective-permute-start.4 = (bf16[96,256]{1,0:T(8,128)(2,1)S(1)}, bf16[96,256]{1,0:T(8,128)(2,1)S(1)}, u32[]{:S(2)}, u32[]{:S(2)}) collective-permute-start(bf16[96,256]{1,0:T(8,128)(2,1)S(1)} %shard_map.64.gram_mine), channel_id=1, source_target_pairs={{0,1},{1,0},{2,3},{3,2},{4,5},{5,4},{6,7},{7,6},{8,9},{9,8},{10,11... | collective-permute-start | bytes 147464 | tf_op jit(solution)/shard_map/ppermute | solution.py:248
  26.3 1.6 %collective-permute-start.5 = (bf16[256,512]{1,0:T(8,128)(2,1)S(1)}, bf16[256,512]{1,0:T(8,128)(2,1)S(1)}, u32[]{:S(2)}, u32[]{:S(2)}) collective-permute-start(bf16[256,512]{1,0:T(8,128)(2,1)S(1)} %shard_map.66.h.h_own), channel_id=1, source_target_pairs={{0,1},{1,0},{2,3},{3,2},{4,5},{5,4},{6,7},{7,6},{8,9},{9,8},{10,11... | collective-permute-start | bytes 786440 | tf_op jit(solution)/shard_map/ppermute | solution.py:248
  29.3 10.5 %collective-permute-start.6 = (f32[352,256]{1,0:T(8,128)S(1)}, f32[352,256]{1,0:T(8,128)S(1)}, u32[]{:S(2)}, u32[]{:S(2)}) collective-permute-start(f32[352,256]{1,0:T(8,128)S(1)} %get-tuple-element.32), channel_id=1, source_target_pairs={{0,4},{4,0},{8,12},{12,8},{16,20},{20,16},{24,28},{28,24},{1,5},{5... | collective-permute-start | bytes 1081352 | tf_op jit(solution)/shard_map/ppermute | solution.py:248
  31.0 8.1 %collective-permute-start.7 = (f32[256,256]{1,0:T(8,128)S(1)}, f32[256,256]{1,0:T(8,128)S(1)}, u32[]{:S(2)}, u32[]{:S(2)}) collective-permute-start(f32[256,256]{1,0:T(8,128)S(1)} %get-tuple-element.34), channel_id=1, source_target_pairs={{0,8},{4,12},{8,0},{12,4},{16,24},{20,28},{24,16},{28,20},{1,9},{5... | collective-permute-start | bytes 786440 | tf_op jit(solution)/shard_map/ppermute | solution.py:248
  39.9 6.9 %collective-permute-start.8 = (f32[224,256]{1,0:T(8,128)S(1)}, f32[224,256]{1,0:T(8,128)S(1)}, u32[]{:S(2)}, u32[]{:S(2)}) collective-permute-start(f32[224,256]{1,0:T(8,128)S(1)} %get-tuple-element.36), channel_id=1, source_target_pairs={{0,8},{4,12},{8,0},{12,4},{16,24},{20,28},{24,16},{28,20},{1,9},{5... | collective-permute-start | bytes 688136 | tf_op jit(solution)/shard_map/ppermute | solution.py:248
  41.7 5.0 %collective-permute-start.9 = (f32[128,256]{1,0:T(8,128)S(1)}, f32[128,256]{1,0:T(8,128)S(1)}, u32[]{:S(2)}, u32[]{:S(2)}) collective-permute-start(f32[128,256]{1,0:T(8,128)S(1)} %get-tuple-element.38), channel_id=1, source_target_pairs={{0,4},{4,0},{8,12},{12,8},{16,20},{20,16},{24,28},{28,24},{1,5},{5... | collective-permute-start | bytes 393224 | tf_op jit(solution)/shard_map/ppermute | solution.py:248
  46.8 11.9 %collective-permute-start.10 = (f32[224,256]{1,0:T(8,128)S(1)}, f32[224,256]{1,0:T(8,128)S(1)}, u32[]{:S(2)}, u32[]{:S(2)}) collective-permute-start(f32[224,256]{1,0:T(8,128)S(1)} %get-tuple-element.40), channel_id=1, source_target_pairs={{0,16},{4,20},{8,24},{12,28},{16,0},{20,4},{24,8},{28,12},{1,17},{... | collective-permute-start | bytes 688136 | tf_op jit(solution)/shard_map/ppermute | solution.py:248
  58.8 1.3 %collective-permute-start.11 = (bf16[96,256]{1,0:T(8,128)(2,1)S(1)}, bf16[96,256]{1,0:T(8,128)(2,1)S(1)}, u32[]{:S(2)}, u32[]{:S(2)}) collective-permute-start(bf16[96,256]{1,0:T(8,128)(2,1)S(1)} %shard_map.71.gram_mine), channel_id=1, source_target_pairs={{0,1},{1,0},{2,3},{3,2},{4,5},{5,4},{6,7},{7,6},{8,9},{9,8},{10,11... | collective-permute-start | bytes 147464 | tf_op jit(solution)/shard_map/ppermute | solution.py:248
  60.3 6.6 %collective-permute-start.12 = (bf16[128,256]{1,0:T(8,128)(2,1)S(1)}, bf16[128,256]{1,0:T(8,128)(2,1)S(1)}, u32[]{:S(2)}, u32[]{:S(2)}) collective-permute-start(bf16[128,256]{1,0:T(8,128)(2,1)S(1)} %shard_map.72), channel_id=1, source_target_pairs={{0,16},{4,20},{8,24},{12,28},{16,0},{20,4},{24,8},{28,12},{1,17},{... | collective-permute-start | bytes 196616 | tf_op jit(solution)/shard_map/ppermute | solution.py:248
  67.0 4.3 %collective-permute-start.13 = (bf16[128,256]{1,0:T(8,128)(2,1)S(1)}, bf16[128,256]{1,0:T(8,128)(2,1)S(1)}, u32[]{:S(2)}, u32[]{:S(2)}) collective-permute-start(bf16[128,256]{1,0:T(8,128)(2,1)S(1)} %pad_maximum_fusion.3), channel_id=1, source_target_pairs={{0,8},{4,12},{8,0},{12,4},{16,24},{20,28},{24,16},{28,20},{1,9},{5... | collective-permute-start | bytes 196616 | tf_op jit(solution)/shard_map/ppermute | solution.py:248
  67.1 4.3 %collective-permute-start.15 = (bf16[128,256]{1,0:T(8,128)(2,1)S(1)}, bf16[128,256]{1,0:T(8,128)(2,1)S(1)}, u32[]{:S(2)}, u32[]{:S(2)}) collective-permute-start(bf16[128,256]{1,0:T(8,128)(2,1)S(1)} %pad_maximum_fusion.4), channel_id=1, source_target_pairs={{0,4},{4,0},{8,12},{12,8},{16,20},{20,16},{24,28},{28,24},{1,5},{5... | collective-permute-start | bytes 196616 | tf_op jit(solution)/shard_map/ppermute | solution.py:248
  71.5 5.0 %collective-permute-start.14 = (bf16[256,256]{1,0:T(8,128)(2,1)S(1)}, bf16[256,256]{1,0:T(8,128)(2,1)S(1)}, u32[]{:S(2)}, u32[]{:S(2)}) collective-permute-start(bf16[256,256]{1,0:T(8,128)(2,1)S(1)} %pad_maximum_fusion.1), channel_id=1, source_target_pairs={{0,4},{4,0},{8,12},{12,8},{16,20},{20,16},{24,28},{28,24},{1,5},{5... | collective-permute-start | bytes 393224 | tf_op jit(solution)/shard_map/ppermute | solution.py:248
  73.1 5.7 %collective-permute-start.16 = (bf16[256,256]{1,0:T(8,128)(2,1)S(1)}, bf16[256,256]{1,0:T(8,128)(2,1)S(1)}, u32[]{:S(2)}, u32[]{:S(2)}) collective-permute-start(bf16[256,256]{1,0:T(8,128)(2,1)S(1)} %pad_maximum_fusion.2), channel_id=1, source_target_pairs={{0,8},{4,12},{8,0},{12,4},{16,24},{20,28},{24,16},{28,20},{1,9},{5... | collective-permute-start | bytes 393224 | tf_op jit(solution)/shard_map/ppermute | solution.py:248

commit v2 on v1

--- a/solution.py
+++ b/solution.py
@@ -15,6 +15,7 @@
 HBM = pl.BlockSpec(memory_space=pltpu.HBM)
 PIECES = 4
 LIMIT = 50 << 20
+TABLE = 16
 
 
 def nt(a, b):
@@ -39,6 +40,82 @@
 
 def like(*shape, dtype=F32):
     return jax.ShapeDtypeStruct(shape, dtype)
+
+
+LEVELS = 65534
+PER_OCTAVE = 512
+EMPTY = -32768
+
+
+def limits(low, high):
+    empty = high == EMPTY
+    least = jnp.where(empty, 0.0, jnp.exp2(low * (1.0 / PER_OCTAVE)))
+    step = jnp.where(empty, 0.0, (jnp.exp2(high * (1.0 / PER_OCTAVE)) - least) * (1.0 / LEVELS))
+    return least, step
+
+
+def encode(x):
+    least = jnp.min(x, axis=0, keepdims=True)
+    most = jnp.max(x, axis=0, keepdims=True)
+    octave = lambda v: jnp.log2(jnp.maximum(v, 1e-18)) * PER_OCTAVE
+    empty = most <= 0.0
+    low = jnp.where(empty, EMPTY, jnp.floor(octave(least) - 0.5)).astype(F32)
+    high = jnp.where(empty, EMPTY, jnp.ceil(octave(most) + 0.5)).astype(F32)
+    base, step = limits(low, high)
+    scale = jnp.where(empty, 0.0, 1.0 / jnp.where(empty, 1.0, step))
+    code = jnp.clip((x - base) * scale + 0.5, 0.0, LEVELS).astype(jnp.int32) - LEVELS // 2
+    return code, low, high
+
+
+def decode(code, low, high):
+    base, step = limits(low, high)
+    return base + (code.astype(jnp.int32) + LEVELS // 2).astype(F32) * step
+
+
+def put_codes(ref, first, groups):
+    table = []
+    for x in groups:
+        code, low, high = encode(x)
+        ref[first : first + x.shape[0], :] = code.astype(jnp.int16)
+        table += [low, high]
+        first += x.shape[0]
+    return table
+
+
+def put_table(ref, at, table):
+    row = lax.broadcasted_iota(jnp.int32, (TABLE, table[0].shape[1]), 0)
+    out = jnp.zeros(row.shape, F32)
+    for i, line in enumerate(table):
+        out = jnp.where(row == i, line, out)
+    ref[at : at + TABLE, :] = out.astype(jnp.int32).astype(jnp.int16)
+
+
+def get_table(ref, at):
+    return ref[at : at + TABLE, :].astype(jnp.int32).astype(F32)
+
+
+def get_codes(ref, first, rows, group, table, entry):
+    out = []
+    for i in range(rows // group):
+        low, high = table[entry : entry + 1, :], table[entry + 1 : entry + 2, :]
+        out.append(decode(ref[first + i * group : first + (i + 1) * group, :], low, high))
+        entry += 2
+    return jnp.concatenate(out, axis=0)
+
+
+def put_gram(ref, first, gram):
+    high = jnp.ceil(jnp.log2(jnp.max(gram, axis=0, keepdims=True) + 1e-18) * PER_OCTAVE + 0.5)
+    unit = float(1 << 30) / jnp.exp2(high * (1.0 / PER_OCTAVE))
+    code = (gram * unit).astype(jnp.int32)
+    rows = gram.shape[0]
+    ref[first : first + rows, :] = (code >> 15).astype(jnp.int16)
+    ref[first + rows : first + 2 * rows, :] = (code & 32767).astype(jnp.int16)
+    return high
+
+
+def get_gram(ref, first, rows, high):
+    code = (ref[first : first + rows, :].astype(jnp.int32) << 15) + ref[first + rows : first + 2 * rows, :].astype(jnp.int32)
+    return code.astype(F32) * (jnp.exp2(high * (1.0 / PER_OCTAVE)) * (1.0 / (1 << 30)))
 
 
 def core_index():
@@ -162,12 +239,22 @@
     out[...] = (a[...] + b[...]).astype(BF16)
 
 
+def code_sum_body(a, b, out):
+    rows = a.shape[0]
+    table = put_codes(out, 0, [a[...] + b[...]])
+    put_table(out, rows, table)
+
+
 def new_h_body(mine, other, gram_mine, gram_other, h, out):
     core = core_index()
     a, b = gram_mine[...], gram_other[...]
     gram = unpack(pick(core, a, b), pick(core, b, a))
     old = h[...]
-    total = mine[...] + other[...]
+    rows = h.shape[0]
+    total = None
+    for ref in (mine, other):
+        part = get_codes(ref, 0, rows, rows, get_table(ref, rows), 0)
+        total = part if total is None else total + part
     out[...] = (old.astype(F32) * total / nn(gram, old)).astype(BF16)
 
 
@@ -178,24 +265,47 @@
         out[part, :] = nt(masked[part, :], h[...])
 
 
-def split_rows(parts, outs, gram, merged):
-    size = parts[0][0].shape[0]
-    for side in range(2):
-        if merged:
-            outs[side][:size, :] = parts[0][side]
-            outs[side][size : 2 * size, :] = parts[1][side]
-            outs[side][2 * size :, :] = gram
-        else:
-            outs[side][:size, :] = parts[0][side]
-            outs[side][size:, :] = gram
-            outs[2 + side][...] = parts[1][side]
-
-
-def second_w_body(masked, part, h, h_own, *outs, bits, merged):
+def blocks_of(x):
+    group = min(BLOCK, x.shape[0])
+    return [x[i : i + group] for i in range(0, x.shape[0], group)]
+
+
+def store_step(sent, gram, outs, merged):
+    if merged:
+        groups = blocks_of(sent[0]) + blocks_of(sent[1])
+        at = 2 * sent[0].shape[0]
+    else:
+        groups = blocks_of(sent[0])
+        at = sent[0].shape[0]
+        table = put_codes(outs[1], 0, blocks_of(sent[1]))
+        put_table(outs[1], at, table)
+    table = put_codes(outs[0], 0, groups)
+    table.append(put_gram(outs[0], at + TABLE, gram))
+    put_table(outs[0], at, table)
+
+
+def arrived(sent, got, size, pk, merged):
+    at = 2 * size if merged else size
+    group = min(BLOCK, size)
+    entry = 2 * (at // group)
+    table = get_table(got[0], at)
+    own_table = get_table(sent[0], at)
+    gram = get_gram(sent[0], at + TABLE, pk, own_table[entry : entry + 1, :]) + get_gram(
+        got[0], at + TABLE, pk, table[entry : entry + 1, :]
+    )
+    if merged:
+        both = get_codes(got[0], 0, at, group, table, 0)
+        return both[:size], both[size:], gram
+    a = get_codes(got[0], 0, size, group, table, 0)
+    b = get_codes(got[1], 0, size, group, get_table(got[1], size), 0)
+    return a, b, gram
+
+
+def second_w_body(masked, part, h, h_own, *outs, bits):
     rows, cols = masked.shape
     core = core_index()
     size = rows // 4
-    new_h = outs[-1]
+    keep_a, keep_b, new_h = outs[-3:]
 
     def piece(start_block):
         start = pl.multiple_of(start_block * size, size)
@@ -204,44 +314,47 @@
     bit_a, bit_b = doc_bit(bits[0]), doc_bit(bits[1])
     gram = nt(h[...], h[...]) + nt(h_own[...], h_own[...])
     mine = pick(core, pack(gram, 0), pack(gram, 1))
-    parts = ((piece(1 - bit_a), piece(bit_a)), (piece(3 - bit_b), piece(2 + bit_b)))
-    split_rows(parts, outs, mine, merged)
+    store_step((piece(1 - bit_a), piece(3 - bit_b)), mine, outs, False)
+    keep_a[...] = piece(bit_a)
+    keep_b[...] = piece(2 + bit_b)
     new_h[:, pl.ds(pl.multiple_of((1 - core) * cols, cols), cols)] = h[...]
     new_h[:, pl.ds(pl.multiple_of(core * cols, cols), cols)] = h_own[...]
 
 
-def arrived(refs, merged, size):
-    if merged:
-        total = refs[0][...] + refs[1][...]
-        return total[:size], total[size : 2 * size], total[2 * size :]
-    a = refs[0][...] + refs[1][...]
-    return a[:size], refs[2][...] + refs[3][...], a[size:]
-
-
-def halve_body(*refs, size, bits, was_merged, merged):
-    given = 2 if was_merged else 4
-    a, b, gram = arrived(refs[:given], was_merged, size)
+def next_step_body(keep_a, keep_b, *refs, size, pk, bits, was_merged, merged, last):
+    streams = 1 if was_merged else 2
+    sent, got, outs = refs[:streams], refs[streams : 2 * streams], refs[2 * streams :]
+    a, b, gram = arrived(sent, got, size, pk, was_merged)
+    a, b = keep_a[...] + a, keep_b[...] + b
+    if last:
+        store_step((a, b), gram, outs, True)
+        return
     half = size // 2
-    parts = []
-    for bit, x in ((doc_bit(bits[0]), a), (doc_bit(bits[1]), b)):
+    sends = []
+    for bit, x, keep in ((doc_bit(bits[0]), a, outs[-2]), (doc_bit(bits[1]), b, outs[-1])):
         low, high = x[:half], x[half:]
-        parts.append((pick(bit, high, low), pick(bit, low, high)))
-    split_rows(parts, refs[given:], gram, merged)
-
-
-def gram_h_body(*refs, size, merged):
-    refs[-1][...] = arrived(refs[:-1], merged, size)[2].astype(BF16)
-
-
-def new_w_body(gram_mine, gram_other, wa, wb, *refs, size, merged):
+        sends.append(pick(bit, high, low))
+        keep[...] = pick(bit, low, high)
+    store_step(sends, gram, outs, merged)
+
+
+def gram_h_body(sent, got, out, *, size, pk):
+    at, entry = 2 * size, 4 * size // min(BLOCK, size)
+    parts = [get_gram(ref, at + TABLE, pk, get_table(ref, at)[entry : entry + 1, :]) for ref in (sent, got)]
+    out[...] = (parts[0] + parts[1]).astype(BF16)
+
+
+def new_w_body(gram_mine, gram_other, wa, wb, sent, got, out, *, size):
     core = core_index()
     one, two = gram_mine[...], gram_other[...]
     gram = unpack(pick(core, one, two), pick(core, two, one))
-    a, b, _ = arrived(refs[:-1], merged, size)
-    out = refs[-1]
-    for first, old_ref, total in ((0, wa, a), (size, wb, b)):
+    group = min(BLOCK, size)
+    parts = [get_codes(ref, 0, 2 * size, group, get_table(ref, 2 * size), 0) for ref in (sent, got)]
+    total = parts[0] + parts[1]
+    for first, old_ref in ((0, wa), (size, wb)):
         old = old_ref[...]
-        out[first : first + size, :] = (old.astype(F32) * total / nn(old, gram)).astype(BF16)
+        part = slice(first, first + size)
+        out[part, :] = (old.astype(F32) * total[part] / nn(old, gram)).astype(BF16)
 
 
 def swap(x, axis, size, bit):
@@ -298,9 +411,10 @@
     g_far = over_term(g_sum, term_bits - 1)
     n_keep, masked_own = numer(own, False, g_sum)
     h_old = call(half_h_body, like(k, half, dtype=BF16), (h,))
-    n_sum = call(add_body, like(k, half), (n_keep, n_got))
     for bit in range(1, term_bits - 1):
-        n_sum = n_sum + over_term(n_sum, bit)
+        n_keep = call(add_body, like(k, half), (n_keep, n_got))
+        n_got = over_term(n_keep, bit)
+    n_sum = call(code_sum_body, like(k + TABLE, half, dtype=jnp.int16), (n_keep, n_got))
     n_far = over_term(n_sum, term_bits - 1)
     g_mine = call(round_add_body, like(pk, k, dtype=BF16), (g_sum, g_far))
     g_other = over_term(g_mine, 0)
@@ -310,45 +424,53 @@
     part = call(first_w_body, like(terms, k), (masked_own, h_own), flops=flops, moved=moved)
     size = terms // 4
 
-    def pieces(rows, merged):
+    def payloads(rows, merged):
         if merged:
-            return (like(2 * rows + pk, k),) * 2
-        return (like(rows + pk, k),) * 2 + (like(rows, k),) * 2
-
-    *state, new_h = call(
-        functools.partial(second_w_body, bits=order[0], merged=same[0]),
-        pieces(size, same[0]) + (like(k, docs, dtype=BF16),),
+            return (like(2 * rows + TABLE + 2 * pk, k, dtype=jnp.int16),)
+        return (like(rows + TABLE + 2 * pk, k, dtype=jnp.int16), like(rows + TABLE, k, dtype=jnp.int16))
+
+    *sent, keep_a, keep_b, new_h = call(
+        functools.partial(second_w_body, bits=order[0]),
+        payloads(size, False) + (like(size, k),) * 2 + (like(k, docs, dtype=BF16),),
         (masked_other, part, h_other, h_own),
         flops=flops,
         moved=moved,
     )
     for step in range(bits):
-        got = [over_doc(state[2 * i], order[step][i]) for i in range(len(state) // 2)]
-        refs = []
-        for i, x in enumerate(got):
-            refs += [state[2 * i + 1], x]
+        got = [over_doc(x, order[step][i]) for i, x in enumerate(sent)]
         if step == bits - 1:
             break
+        last = step == bits - 2
         body = functools.partial(
-            halve_body, size=size, bits=order[step + 1], was_merged=same[step], merged=same[step + 1]
+            next_step_body,
+            size=size,
+            pk=pk,
+            bits=order[step + 1],
+            was_merged=same[step],
+            merged=same[step + 1],
+            last=last,
         )
-        size //= 2
-        state = call(body, pieces(size, same[step + 1]), refs)
-    merged = same[bits - 1]
-    g_mine = call(functools.partial(gram_h_body, size=size, merged=merged), like(pk, k, dtype=BF16), refs)
+        args = (keep_a, keep_b, *sent, *got)
+        if last:
+            sent = call(body, payloads(size, True), args)
+        else:
+            size //= 2
+            *sent, keep_a, keep_b = call(body, payloads(size, same[step + 1]) + (like(size, k),) * 2, args)
+    ends = (sent[0], got[0])
+    g_mine = call(functools.partial(gram_h_body, size=size, pk=pk), like(pk, k, dtype=BF16), ends)
     g_other = over_term(g_mine, 0)
     old = []
     for stream in range(2):
         start = jnp.int32(stream * (terms // 2))
-        for step in range(bits):
+        for step in range(bits - 1):
             start += doc_bit(order[step][stream]) * (terms // 2 >> (step + 1))
         old.append(lax.dynamic_slice_in_dim(w, start, size, 0))
     both = call(
-        functools.partial(new_w_body, size=size, merged=merged),
+        functools.partial(new_w_body, size=size),
         like(2 * size, k, dtype=BF16),
-        (g_mine, g_other, *old, *refs),
+        (g_mine, g_other, *old, *ends),
     )
-    for step in reversed(range(bits)):
+    for step in reversed(range(bits - 1)):
         if same[step]:
             got = over_doc(both, order[step][0])
             w_a, w_b = [

time: 79.9 us -> 65.5 us (0.82)
  waiting for transfers between devices: 50.4 us -> 35.9 us
  starting transfers between devices: 19.6 us -> 18.6 us
  Pallas kernels: 5.97 us -> 6.95 us
    ppermute x17 -> x16, waiting for transfers between devices: 50.4 us -> 35.9 us  [swap(): return lax.ppermute(x, axis, [(i, i ^ 1 << bit) for i in range(size)])]
    ppermute x17 -> x16, starting transfers between devices: 19.6 us -> 18.6 us  [swap(): return lax.ppermute(x, axis, [(i, i ^ 1 << bit) for i in range(size)])]
    pallas_call x14, Pallas kernels: 5.97 us -> 6.95 us  [call(): pl.pallas_call(body, out_shape=out, in_specs=[HBM if i in hbm else VMEM f...]
  transfers between devices with their start and end apart: 17 -> 16, of which waited for: 15 -> 13; matrix products, arithmetic and copies ran while one was open for 1% -> 1% of each run, Pallas kernels for 1% -> 2%
where the time goes in v2:
time: 65.5 us; the launch traced here: 65.2 us
  waiting for transfers between devices  35.9 us (55%)
  starting transfers between devices  18.6 us (28%)
  Pallas kernels  6.95 us (11%)
  local copies, waits for them, and re-layouts  1.95 us (3%)
  other arithmetic  0.97 us (1%)
  between operations  0.81 us (1%)
    ppermute x16, waiting for transfers between devices, swap(): return lax.ppermute(x, axis, [(i, i ^ 1 << bit) for i in range(size)])  35.9 us
    ppermute x16, starting transfers between devices, swap(): return lax.ppermute(x, axis, [(i, i ^ 1 << bit) for i in range(size)])  18.6 us
    pallas_call x14, Pallas kernels, call(): pl.pallas_call(body, out_shape=out, in_specs=[HBM if i in hbm else VMEM f...  6.95 us
  transfers between devices with their start and end apart: 16, of which 13 were waited for; matrix products, arithmetic and copies ran while one was open for 1% of the time, Pallas kernels for 2%

profile of v2, /device:TPU:0, one launch (start us, length us, event | category | flops | bytes accessed | tf_op | source)
XLA Modules:
  0.0 65.2 jit_solution(11904546623411465848)
XLA Ops:
  0.6 1.0 %copy-done = bf16[1024,256]{1,0:T(8,128)(2,1)S(1)} copy-done((bf16[1024,256]{1,0:T(8,128)(2,1)S(1)}, bf16[1024,256]{1,0:T(8,128)(2,1)}, u32[]{:S(2)}) %copy-start) | copy-done | bytes 524312
  1.7 2.2 %shard_map.59 = (bf16[256,1024]{1,0:T(8,128)(2,1)S(1)}, f32[96,256]{1,0:T(8,128)S(1)}, f32[96,256]{1,0:T(8,128)S(1)}, bf16[1024,512]{1,0:T(8,128)(2,1)S(1)}, bf16[1024,512]{1,0:T(8,128)(2,1)S(1)}) custom-call(bf16[1024,1024]{1,0:T(8,128)(2,1)} %m.1, bf16[1024,256]{1,0:T(8,128)(2,1)S(1)} %copy-done), custom_call_target="tpu_custom_call" | custom-call | flops 1048576 | bytes 1048576 | tf_op jit(solution)/shard_map/pallas_call | solution.py:30
  5.2 1.6 %collective-permute-done.b = f32[96,256]{1,0:T(8,128)S(1)} collective-permute-done((f32[96,256]{1,0:T(8,128)S(1)}, f32[96,256]{1,0:T(8,128)S(1)}, u32[]{:S(2)}, u32[]{:S(2)}) %collective-permute-start) | collective-permute-done | bytes 98336 | tf_op jit(solution)/shard_map/ppermute | solution.py:361
  7.7 2.9 %collective-permute-start.2 = (s16[272,512]{1,0:T(8,128)(2,1)S(1)}, s16[272,512]{1,0:T(8,128)(2,1)S(1)}, u32[]{:S(2)}, u32[]{:S(2)}) collective-permute-start(s16[272,512]{1,0:T(8,128)(2,1)S(1)} %shard_map.63.mine), channel_id=1, source_target_pairs={{0,2},{1,3},{2,0},{3,1},{4,6},{5,7},{6,4},{7,5},{8,10},{9,11},{10,... | collective-permute-start | bytes 835592 | tf_op jit(solution)/shard_map/ppermute | solution.py:361
  10.7 9.0 %collective-permute-done.3.b = f32[96,256]{1,0:T(8,128)S(1)} collective-permute-done((f32[96,256]{1,0:T(8,128)S(1)}, f32[96,256]{1,0:T(8,128)S(1)}, u32[]{:S(2)}, u32[]{:S(2)}) %collective-permute-start.3) | collective-permute-done | bytes 98336 | tf_op jit(solution)/shard_map/ppermute | solution.py:361
  19.8 1.2 %collective-permute-done.4.gram_other = bf16[96,256]{1,0:T(8,128)(2,1)S(1)} collective-permute-done((bf16[96,256]{1,0:T(8,128)(2,1)S(1)}, bf16[96,256]{1,0:T(8,128)(2,1)S(1)}, u32[]{:S(2)}, u32[]{:S(2)}) %collective-permute-start.4) | collective-permute-done | bytes 49184 | tf_op jit(solution)/shard_map/ppermute | solution.py:361
  22.0 0.9 %collective-permute-done.5.h = bf16[256,512]{1,0:T(8,128)(2,1)S(1)} collective-permute-done((bf16[256,512]{1,0:T(8,128)(2,1)S(1)}, bf16[256,512]{1,0:T(8,128)(2,1)S(1)}, u32[]{:S(2)}, u32[]{:S(2)}) %collective-permute-start.5) | collective-permute-done | bytes 262176 | tf_op jit(solution)/shard_map/ppermute | solution.py:361
  23.0 1.4 %shard_map.68 = (s16[464,256]{1,0:T(8,128)(2,1)S(1)}, s16[272,256]{1,0:T(8,128)(2,1)S(1)}, f32[256,256]{1,0:T(8,128)S(1)}, f32[256,256]{1,0:T(8,128)S(1)}, bf16[256,1024]{1,0:T(8,128)(2,1)}) custom-call(bf16[1024,512]{1,0:T(8,128)(2,1)S(1)} %get-tuple-element.22.masked, f32[1024,256]{1,0:T(8,128)S(1)} %shard_map.67.part, ...), custom_call_target="tpu_custom_call" | custom-call | flops 268435456 | bytes 2097152 | tf_op jit(solution)/shard_map/pallas_call | solution.py:30
  24.4 1.8 %collective-permute-start.6 = (s16[464,256]{1,0:T(8,128)(2,1)S(1)}, s16[464,256]{1,0:T(8,128)(2,1)S(1)}, u32[]{:S(2)}, u32[]{:S(2)}) collective-permute-start(s16[464,256]{1,0:T(8,128)(2,1)S(1)} %get-tuple-element.31.refs_0_), channel_id=1, source_target_pairs={{0,4},{4,0},{8,12},{12,8},{16,20},{20,16},{24,28},{28,24},{1,5},{5... | collective-permute-start | bytes 712712 | tf_op jit(solution)/shard_map/ppermute | solution.py:361
  26.2 1.6 %collective-permute-start.7 = (s16[272,256]{1,0:T(8,128)(2,1)S(1)}, s16[272,256]{1,0:T(8,128)(2,1)S(1)}, u32[]{:S(2)}, u32[]{:S(2)}) collective-permute-start(s16[272,256]{1,0:T(8,128)(2,1)S(1)} %get-tuple-element.32.refs_1_), channel_id=1, source_target_pairs={{0,8},{4,12},{8,0},{12,4},{16,24},{20,28},{24,16},{28,20},{1,9},{5... | collective-permute-start | bytes 417800 | tf_op jit(solution)/shard_map/ppermute | solution.py:361
  27.7 3.9 %collective-permute-done.7.refs_3_ = s16[272,256]{1,0:T(8,128)(2,1)S(1)} collective-permute-done((s16[272,256]{1,0:T(8,128)(2,1)S(1)}, s16[272,256]{1,0:T(8,128)(2,1)S(1)}, u32[]{:S(2)}, u32[]{:S(2)}) %collective-permute-start.7) | collective-permute-done | bytes 139296 | tf_op jit(solution)/shard_map/ppermute | solution.py:361
  32.6 1.9 %collective-permute-start.8 = (s16[336,256]{1,0:T(8,128)(2,1)S(1)}, s16[336,256]{1,0:T(8,128)(2,1)S(1)}, u32[]{:S(2)}, u32[]{:S(2)}) collective-permute-start(s16[336,256]{1,0:T(8,128)(2,1)S(1)} %get-tuple-element.35.refs_0_), channel_id=1, source_target_pairs={{0,8},{4,12},{8,0},{12,4},{16,24},{20,28},{24,16},{28,20},{1,9},{5... | collective-permute-start | bytes 516104 | tf_op jit(solution)/shard_map/ppermute | solution.py:361
  34.5 1.5 %collective-permute-start.9 = (s16[144,256]{1,0:T(8,128)(2,1)S(1)}, s16[144,256]{1,0:T(8,128)(2,1)S(1)}, u32[]{:S(2)}, u32[]{:S(2)}) collective-permute-start(s16[144,256]{1,0:T(8,128)(2,1)S(1)} %get-tuple-element.36.refs_1_), channel_id=1, source_target_pairs={{0,4},{4,0},{8,12},{12,8},{16,20},{20,16},{24,28},{28,24},{1,5},{5... | collective-permute-start | bytes 221192 | tf_op jit(solution)/shard_map/ppermute | solution.py:361
  36.0 2.8 %collective-permute-done.9.refs_3_ = s16[144,256]{1,0:T(8,128)(2,1)S(1)} collective-permute-done((s16[144,256]{1,0:T(8,128)(2,1)S(1)}, s16[144,256]{1,0:T(8,128)(2,1)S(1)}, u32[]{:S(2)}, u32[]{:S(2)}) %collective-permute-start.9) | collective-permute-done | bytes 73760 | tf_op jit(solution)/shard_map/ppermute | solution.py:361
  39.1 2.7 %collective-permute-start.10 = (s16[464,256]{1,0:T(8,128)(2,1)S(1)}, s16[464,256]{1,0:T(8,128)(2,1)S(1)}, u32[]{:S(2)}, u32[]{:S(2)}) collective-permute-start(s16[464,256]{1,0:T(8,128)(2,1)S(1)} %shard_map.70.sent), channel_id=1, source_target_pairs={{0,16},{4,20},{8,24},{12,28},{16,0},{20,4},{24,8},{28,12},{1,17},{... | collective-permute-start | bytes 712712 | tf_op jit(solution)/shard_map/ppermute | solution.py:361
  41.8 9.2 %collective-permute-done.10.got = s16[464,256]{1,0:T(8,128)(2,1)S(1)} collective-permute-done((s16[464,256]{1,0:T(8,128)(2,1)S(1)}, s16[464,256]{1,0:T(8,128)(2,1)S(1)}, u32[]{:S(2)}, u32[]{:S(2)}) %collective-permute-start.10) | collective-permute-done | bytes 237600 | tf_op jit(solution)/shard_map/ppermute | solution.py:361
  51.2 0.9 %constant_dynamic-slice_fusion = (bf16[128,256]{1,0:T(8,128)(2,1)S(1)}, bf16[128,256]{1,0:T(8,128)(2,1)S(1)}) fusion(bf16[1024,256]{1,0:T(8,128)(2,1)} %w.1, s32[]{:T(128)S(6)} %select_n.53, s32[]{:T(128)S(6)} %select_n.52), kind=kLoop, calls=%fused_computation.11 | loop fusion | bytes 262152 | tf_op jit(solution)/shard_map/dynamic_slice | solution.py:467
  53.4 1.5 %collective-permute-start.14 = (bf16[128,256]{1,0:T(8,128)(2,1)S(1)}, bf16[128,256]{1,0:T(8,128)(2,1)S(1)}, u32[]{:S(2)}, u32[]{:S(2)}) collective-permute-start(bf16[128,256]{1,0:T(8,128)(2,1)S(1)} %get-tuple-element.51), channel_id=1, source_target_pairs={{0,4},{4,0},{8,12},{12,8},{16,20},{20,16},{24,28},{28,24},{1,5},{5... | collective-permute-start | bytes 196616 | tf_op jit(solution)/shard_map/ppermute | solution.py:361
  54.9 2.1 %collective-permute-done.12 = bf16[128,256]{1,0:T(8,128)(2,1)S(1)} collective-permute-done((bf16[128,256]{1,0:T(8,128)(2,1)S(1)}, bf16[128,256]{1,0:T(8,128)(2,1)S(1)}, u32[]{:S(2)}, u32[]{:S(2)}) %collective-permute-start.12) | collective-permute-done | bytes 65568 | tf_op jit(solution)/shard_map/ppermute | solution.py:361
  57.7 1.6 %collective-permute-start.13 = (bf16[256,256]{1,0:T(8,128)(2,1)S(1)}, bf16[256,256]{1,0:T(8,128)(2,1)S(1)}, u32[]{:S(2)}, u32[]{:S(2)}) collective-permute-start(bf16[256,256]{1,0:T(8,128)(2,1)S(1)} %pad_maximum_fusion.1), channel_id=1, source_target_pairs={{0,4},{4,0},{8,12},{12,8},{16,20},{20,16},{24,28},{28,24},{1,5},{5... | collective-permute-start | bytes 393224 | tf_op jit(solution)/shard_map/ppermute | solution.py:361
  59.3 1.4 %collective-permute-start.15 = (bf16[256,256]{1,0:T(8,128)(2,1)S(1)}, bf16[256,256]{1,0:T(8,128)(2,1)S(1)}, u32[]{:S(2)}, u32[]{:S(2)}) collective-permute-start(bf16[256,256]{1,0:T(8,128)(2,1)S(1)} %pad_maximum_fusion.2), channel_id=1, source_target_pairs={{0,8},{4,12},{8,0},{12,4},{16,24},{20,28},{24,16},{28,20},{1,9},{5... | collective-permute-start | bytes 393224 | tf_op jit(solution)/shard_map/ppermute | solution.py:361
  60.7 2.0 %collective-permute-done.13 = bf16[256,256]{1,0:T(8,128)(2,1)S(1)} collective-permute-done((bf16[256,256]{1,0:T(8,128)(2,1)S(1)}, bf16[256,256]{1,0:T(8,128)(2,1)S(1)}, u32[]{:S(2)}, u32[]{:S(2)}) %collective-permute-start.13) | collective-permute-done | bytes 131104 | tf_op jit(solution)/shard_map/ppermute | solution.py:361
  62.8 1.5 %collective-permute-done.15 = bf16[256,256]{1,0:T(8,128)(2,1)S(1)} collective-permute-done((bf16[256,256]{1,0:T(8,128)(2,1)S(1)}, bf16[256,256]{1,0:T(8,128)(2,1)S(1)}, u32[]{:S(2)}, u32[]{:S(2)}) %collective-permute-start.15) | collective-permute-done | bytes 131104 | tf_op jit(solution)/shard_map/ppermute | solution.py:361
  64.4 0.8 %pad_maximum_fusion = bf16[1024,256]{1,0:T(8,128)(2,1)} fusion(bf16[256,256]{1,0:T(8,128)(2,1)S(1)} %get-tuple-element.43, bf16[256,256]{1,0:T(8,128)(2,1)S(1)} %get-tuple-element.42, bf16[256,256]{1,0:T(8,128)(2,1)S(1)} %get-tuple-element.41, bf16[256,256]{1,0:T(8,128)(2,1)S(1)} %get-tuple-element.40), kind=kLoop, calls=%fused_computation | loop fusion | flops 2097152 | bytes 1048576 | tf_op jit(solution)/shard_map/concatenate | solution.py:486
  (36 shorter events, 6.9 us)
Async XLA Ops:
  0.6 1.0 %copy-start = (bf16[1024,256]{1,0:T(8,128)(2,1)S(1)}, bf16[1024,256]{1,0:T(8,128)(2,1)}, u32[]{:S(2)}) copy-start(bf16[1024,256]{1,0:T(8,128)(2,1)} %w.1) | copy-start | bytes 1572868
  1.7 2.3 %copy-start.2 = (s32[8,8]{1,0:T(8,128)S(1)}, s32[8,8]{1,0:T(8,128)}, u32[]{:S(2)}) copy-start(s32[8,8]{1,0:T(8,128)} %pattern.3) | copy-start | bytes 772
  4.5 15.2 %copy-start.1 = (bf16[256,1024]{1,0:T(8,128)(2,1)S(1)}, bf16[256,1024]{1,0:T(8,128)(2,1)}, u32[]{:S(2)}) copy-start(bf16[256,1024]{1,0:T(8,128)(2,1)} %h.1) | copy-start | bytes 1572868
  4.6 2.9 %collective-permute-start.1 = (f32[256,512]{1,0:T(8,128)S(1)}, f32[256,512]{1,0:T(8,128)S(1)}, u32[]{:S(2)}, u32[]{:S(2)}) collective-permute-start(f32[256,512]{1,0:T(8,128)S(1)} %get-tuple-element.28), channel_id=1, source_target_pairs={{0,1},{1,0},{2,3},{3,2},{4,5},{5,4},{6,7},{7,6},{8,9},{9,8},{10,11... | collective-permute-start | bytes 1572872 | tf_op jit(solution)/shard_map/ppermute | solution.py:361
  5.1 1.7 %collective-permute-start = (f32[96,256]{1,0:T(8,128)S(1)}, f32[96,256]{1,0:T(8,128)S(1)}, u32[]{:S(2)}, u32[]{:S(2)}) collective-permute-start(f32[96,256]{1,0:T(8,128)S(1)} %get-tuple-element.25), channel_id=1, source_target_pairs={{0,1},{1,0},{2,3},{3,2},{4,5},{5,4},{6,7},{7,6},{8,9},{9,8},{10,11... | collective-permute-start | bytes 294920 | tf_op jit(solution)/shard_map/ppermute | solution.py:361
  7.7 13.3 %collective-permute-start.2 = (s16[272,512]{1,0:T(8,128)(2,1)S(1)}, s16[272,512]{1,0:T(8,128)(2,1)S(1)}, u32[]{:S(2)}, u32[]{:S(2)}) collective-permute-start(s16[272,512]{1,0:T(8,128)(2,1)S(1)} %shard_map.63.mine), channel_id=1, source_target_pairs={{0,2},{1,3},{2,0},{3,1},{4,6},{5,7},{6,4},{7,5},{8,10},{9,11},{10,... | collective-permute-start | bytes 835592 | tf_op jit(solution)/shard_map/ppermute | solution.py:361
  10.6 9.1 %collective-permute-start.3 = (f32[96,256]{1,0:T(8,128)S(1)}, f32[96,256]{1,0:T(8,128)S(1)}, u32[]{:S(2)}, u32[]{:S(2)}) collective-permute-start(f32[96,256]{1,0:T(8,128)S(1)} %shard_map.61.refs_0_.a), channel_id=1, source_target_pairs={{0,2},{1,3},{2,0},{3,1},{4,6},{5,7},{6,4},{7,5},{8,10},{9,11},{10,... | collective-permute-start | bytes 294920 | tf_op jit(solution)/shard_map/ppermute | solution.py:361
  19.7 1.3 %collective-permute-start.4 = (bf16[96,256]{1,0:T(8,128)(2,1)S(1)}, bf16[96,256]{1,0:T(8,128)(2,1)S(1)}, u32[]{:S(2)}, u32[]{:S(2)}) collective-permute-start(bf16[96,256]{1,0:T(8,128)(2,1)S(1)} %shard_map.64.gram_mine), channel_id=1, source_target_pairs={{0,1},{1,0},{2,3},{3,2},{4,5},{5,4},{6,7},{7,6},{8,9},{9,8},{10,11... | collective-permute-start | bytes 147464 | tf_op jit(solution)/shard_map/ppermute | solution.py:361
  21.4 1.6 %collective-permute-start.5 = (bf16[256,512]{1,0:T(8,128)(2,1)S(1)}, bf16[256,512]{1,0:T(8,128)(2,1)S(1)}, u32[]{:S(2)}, u32[]{:S(2)}) collective-permute-start(bf16[256,512]{1,0:T(8,128)(2,1)S(1)} %shard_map.66.h.h_own), channel_id=1, source_target_pairs={{0,1},{1,0},{2,3},{3,2},{4,5},{5,4},{6,7},{7,6},{8,9},{9,8},{10,11... | collective-permute-start | bytes 786440 | tf_op jit(solution)/shard_map/ppermute | solution.py:361
  24.4 7.9 %collective-permute-start.6 = (s16[464,256]{1,0:T(8,128)(2,1)S(1)}, s16[464,256]{1,0:T(8,128)(2,1)S(1)}, u32[]{:S(2)}, u32[]{:S(2)}) collective-permute-start(s16[464,256]{1,0:T(8,128)(2,1)S(1)} %get-tuple-element.31.refs_0_), channel_id=1, source_target_pairs={{0,4},{4,0},{8,12},{12,8},{16,20},{20,16},{24,28},{28,24},{1,5},{5... | collective-permute-start | bytes 712712 | tf_op jit(solution)/shard_map/ppermute | solution.py:361
  26.2 5.5 %collective-permute-start.7 = (s16[272,256]{1,0:T(8,128)(2,1)S(1)}, s16[272,256]{1,0:T(8,128)(2,1)S(1)}, u32[]{:S(2)}, u32[]{:S(2)}) collective-permute-start(s16[272,256]{1,0:T(8,128)(2,1)S(1)} %get-tuple-element.32.refs_1_), channel_id=1, source_target_pairs={{0,8},{4,12},{8,0},{12,4},{16,24},{20,28},{24,16},{28,20},{1,9},{5... | collective-permute-start | bytes 417800 | tf_op jit(solution)/shard_map/ppermute | solution.py:361
  32.6 6.2 %collective-permute-start.8 = (s16[336,256]{1,0:T(8,128)(2,1)S(1)}, s16[336,256]{1,0:T(8,128)(2,1)S(1)}, u32[]{:S(2)}, u32[]{:S(2)}) collective-permute-start(s16[336,256]{1,0:T(8,128)(2,1)S(1)} %get-tuple-element.35.refs_0_), channel_id=1, source_target_pairs={{0,8},{4,12},{8,0},{12,4},{16,24},{20,28},{24,16},{28,20},{1,9},{5... | collective-permute-start | bytes 516104 | tf_op jit(solution)/shard_map/ppermute | solution.py:361
  34.5 4.4 %collective-permute-start.9 = (s16[144,256]{1,0:T(8,128)(2,1)S(1)}, s16[144,256]{1,0:T(8,128)(2,1)S(1)}, u32[]{:S(2)}, u32[]{:S(2)}) collective-permute-start(s16[144,256]{1,0:T(8,128)(2,1)S(1)} %get-tuple-element.36.refs_1_), channel_id=1, source_target_pairs={{0,4},{4,0},{8,12},{12,8},{16,20},{20,16},{24,28},{28,24},{1,5},{5... | collective-permute-start | bytes 221192 | tf_op jit(solution)/shard_map/ppermute | solution.py:361
  39.1 11.9 %collective-permute-start.10 = (s16[464,256]{1,0:T(8,128)(2,1)S(1)}, s16[464,256]{1,0:T(8,128)(2,1)S(1)}, u32[]{:S(2)}, u32[]{:S(2)}) collective-permute-start(s16[464,256]{1,0:T(8,128)(2,1)S(1)} %shard_map.70.sent), channel_id=1, source_target_pairs={{0,16},{4,20},{8,24},{12,28},{16,0},{20,4},{24,8},{28,12},{1,17},{... | collective-permute-start | bytes 712712 | tf_op jit(solution)/shard_map/ppermute | solution.py:361
  51.1 1.3 %collective-permute-start.11 = (bf16[96,256]{1,0:T(8,128)(2,1)S(1)}, bf16[96,256]{1,0:T(8,128)(2,1)S(1)}, u32[]{:S(2)}, u32[]{:S(2)}) collective-permute-start(bf16[96,256]{1,0:T(8,128)(2,1)S(1)} %shard_map.71.gram_mine), channel_id=1, source_target_pairs={{0,1},{1,0},{2,3},{3,2},{4,5},{5,4},{6,7},{7,6},{8,9},{9,8},{10,11... | collective-permute-start | bytes 147464 | tf_op jit(solution)/shard_map/ppermute | solution.py:361
  52.7 4.3 %collective-permute-start.12 = (bf16[128,256]{1,0:T(8,128)(2,1)S(1)}, bf16[128,256]{1,0:T(8,128)(2,1)S(1)}, u32[]{:S(2)}, u32[]{:S(2)}) collective-permute-start(bf16[128,256]{1,0:T(8,128)(2,1)S(1)} %get-tuple-element.50), channel_id=1, source_target_pairs={{0,8},{4,12},{8,0},{12,4},{16,24},{20,28},{24,16},{28,20},{1,9},{5... | collective-permute-start | bytes 196616 | tf_op jit(solution)/shard_map/ppermute | solution.py:361
  53.4 4.3 %collective-permute-start.14 = (bf16[128,256]{1,0:T(8,128)(2,1)S(1)}, bf16[128,256]{1,0:T(8,128)(2,1)S(1)}, u32[]{:S(2)}, u32[]{:S(2)}) collective-permute-start(bf16[128,256]{1,0:T(8,128)(2,1)S(1)} %get-tuple-element.51), channel_id=1, source_target_pairs={{0,4},{4,0},{8,12},{12,8},{16,20},{20,16},{24,28},{28,24},{1,5},{5... | collective-permute-start | bytes 196616 | tf_op jit(solution)/shard_map/ppermute | solution.py:361
  57.7 5.0 %collective-permute-start.13 = (bf16[256,256]{1,0:T(8,128)(2,1)S(1)}, bf16[256,256]{1,0:T(8,128)(2,1)S(1)}, u32[]{:S(2)}, u32[]{:S(2)}) collective-permute-start(bf16[256,256]{1,0:T(8,128)(2,1)S(1)} %pad_maximum_fusion.1), channel_id=1, source_target_pairs={{0,4},{4,0},{8,12},{12,8},{16,20},{20,16},{24,28},{28,24},{1,5},{5... | collective-permute-start | bytes 393224 | tf_op jit(solution)/shard_map/ppermute | solution.py:361
  59.3 5.0 %collective-permute-start.15 = (bf16[256,256]{1,0:T(8,128)(2,1)S(1)}, bf16[256,256]{1,0:T(8,128)(2,1)S(1)}, u32[]{:S(2)}, u32[]{:S(2)}) collective-permute-start(bf16[256,256]{1,0:T(8,128)(2,1)S(1)} %pad_maximum_fusion.2), channel_id=1, source_target_pairs={{0,8},{4,12},{8,0},{12,4},{16,24},{20,28},{24,16},{28,20},{1,9},{5... | collective-permute-start | bytes 393224 | tf_op jit(solution)/shard_map/ppermute | solution.py:361

commit v3 on v2

--- a/solution.py
+++ b/solution.py
@@ -103,23 +103,32 @@
     return jnp.concatenate(out, axis=0)
 
 
-def put_gram(ref, first, gram):
-    high = jnp.ceil(jnp.log2(jnp.max(gram, axis=0, keepdims=True) + 1e-18) * PER_OCTAVE + 0.5)
-    unit = float(1 << 30) / jnp.exp2(high * (1.0 / PER_OCTAVE))
-    code = (gram * unit).astype(jnp.int32)
-    rows = gram.shape[0]
-    ref[first : first + rows, :] = (code >> 15).astype(jnp.int16)
-    ref[first + rows : first + 2 * rows, :] = (code & 32767).astype(jnp.int16)
-    return high
-
-
-def get_gram(ref, first, rows, high):
-    code = (ref[first : first + rows, :].astype(jnp.int32) << 15) + ref[first + rows : first + 2 * rows, :].astype(jnp.int32)
-    return code.astype(F32) * (jnp.exp2(high * (1.0 / PER_OCTAVE)) * (1.0 / (1 << 30)))
+def put_parts(ref, parts):
+    groups = []
+    for x in parts:
+        group = min(BLOCK, x.shape[0])
+        groups += [x[i : i + group] for i in range(0, x.shape[0], group)]
+    table = put_codes(ref, 0, groups)
+    put_table(ref, sum(x.shape[0] for x in parts), table)
+
+
+def get_parts(ref, sizes):
+    table = get_table(ref, sum(sizes))
+    out, first, entry = [], 0, 0
+    for rows in sizes:
+        group = min(BLOCK, rows)
+        out.append(get_codes(ref, first, rows, group, table, entry))
+        first += rows
+        entry += 2 * (rows // group)
+    return out
 
 
 def core_index():
     return lax.axis_index("term") & 1
+
+
+def quad_index():
+    return lax.axis_index("doc") & 3
 
 
 def doc_bit(bit):
@@ -265,100 +274,82 @@
         out[part, :] = nt(masked[part, :], h[...])
 
 
-def blocks_of(x):
-    group = min(BLOCK, x.shape[0])
-    return [x[i : i + group] for i in range(0, x.shape[0], group)]
-
-
-def store_step(sent, gram, outs, merged):
-    if merged:
-        groups = blocks_of(sent[0]) + blocks_of(sent[1])
-        at = 2 * sent[0].shape[0]
-    else:
-        groups = blocks_of(sent[0])
-        at = sent[0].shape[0]
-        table = put_codes(outs[1], 0, blocks_of(sent[1]))
-        put_table(outs[1], at, table)
-    table = put_codes(outs[0], 0, groups)
-    table.append(put_gram(outs[0], at + TABLE, gram))
-    put_table(outs[0], at, table)
-
-
-def arrived(sent, got, size, pk, merged):
-    at = 2 * size if merged else size
-    group = min(BLOCK, size)
-    entry = 2 * (at // group)
-    table = get_table(got[0], at)
-    own_table = get_table(sent[0], at)
-    gram = get_gram(sent[0], at + TABLE, pk, own_table[entry : entry + 1, :]) + get_gram(
-        got[0], at + TABLE, pk, table[entry : entry + 1, :]
-    )
-    if merged:
-        both = get_codes(got[0], 0, at, group, table, 0)
-        return both[:size], both[size:], gram
-    a = get_codes(got[0], 0, size, group, table, 0)
-    b = get_codes(got[1], 0, size, group, get_table(got[1], size), 0)
-    return a, b, gram
-
-
-def second_w_body(masked, part, h, h_own, *outs, bits):
-    rows, cols = masked.shape
-    core = core_index()
-    size = rows // 4
-    keep_a, keep_b, new_h = outs[-3:]
-
-    def piece(start_block):
-        start = pl.multiple_of(start_block * size, size)
-        return part[pl.ds(start, size), :] + nt(masked[pl.ds(start, size), :], h[...])
-
-    bit_a, bit_b = doc_bit(bits[0]), doc_bit(bits[1])
+def piece_of(masked, part, h, index, size):
+    start = pl.multiple_of(index * size, size)
+    return part[pl.ds(start, size), :] + nt(masked[pl.ds(start, size), :], h[...])
+
+
+def first_send_body(masked, part, h, h_own, out, gram_out, *, away):
+    size = masked.shape[0] // 4
     gram = nt(h[...], h[...]) + nt(h_own[...], h_own[...])
-    mine = pick(core, pack(gram, 0), pack(gram, 1))
-    store_step((piece(1 - bit_a), piece(3 - bit_b)), mine, outs, False)
-    keep_a[...] = piece(bit_a)
-    keep_b[...] = piece(2 + bit_b)
-    new_h[:, pl.ds(pl.multiple_of((1 - core) * cols, cols), cols)] = h[...]
-    new_h[:, pl.ds(pl.multiple_of(core * cols, cols), cols)] = h_own[...]
-
-
-def next_step_body(keep_a, keep_b, *refs, size, pk, bits, was_merged, merged, last):
-    streams = 1 if was_merged else 2
-    sent, got, outs = refs[:streams], refs[streams : 2 * streams], refs[2 * streams :]
-    a, b, gram = arrived(sent, got, size, pk, was_merged)
-    a, b = keep_a[...] + a, keep_b[...] + b
+    gram = pick(core_index(), pack(gram, 0), pack(gram, 1))
+    gram_out[...] = gram
+    put_parts(out, [piece_of(masked, part, h, quad_index() ^ away, size), gram])
+
+
+def send_body(masked, part, h, gram, out, *, away):
+    size = masked.shape[0] // 4
+    put_parts(out, [piece_of(masked, part, h, quad_index() ^ away, size), gram[...]])
+
+
+def keep_rows_body(masked, part, h, out):
+    out[...] = piece_of(masked, part, h, quad_index(), out.shape[0])
+
+
+def new_h_out_body(h, h_own, out):
+    core, cols = core_index(), h.shape[1]
+    out[:, pl.ds(pl.multiple_of((1 - core) * cols, cols), cols)] = h[...]
+    out[:, pl.ds(pl.multiple_of(core * cols, cols), cols)] = h_own[...]
+
+
+def quad_sum_body(keep, own, one, two, three, *outs, pk, bit, last):
+    size = keep.shape[0]
+    rows, gram = zip(*[get_parts(ref, (size, pk)) for ref in (one, two, three)])
+    gram_own = get_parts(own, (size, pk))[1]
+    total = (keep[...] + rows[0]) + (rows[1] + rows[2])
+    store_step(total, (gram_own + gram[0]) + (gram[1] + gram[2]), outs, bit, last)
+
+
+def step_sum_body(keep, sent, got, *outs, pk, bit, last):
+    size = keep.shape[0]
+    rows, gram = get_parts(got, (size, pk))
+    store_step(keep[...] + rows, get_parts(sent, (size, pk))[1] + gram, outs, bit, last)
+
+
+def store_step(rows, gram, outs, bit, last):
     if last:
-        store_step((a, b), gram, outs, True)
+        put_parts(outs[0], [rows, gram])
         return
-    half = size // 2
-    sends = []
-    for bit, x, keep in ((doc_bit(bits[0]), a, outs[-2]), (doc_bit(bits[1]), b, outs[-1])):
-        low, high = x[:half], x[half:]
-        sends.append(pick(bit, high, low))
-        keep[...] = pick(bit, low, high)
-    store_step(sends, gram, outs, merged)
-
-
-def gram_h_body(sent, got, out, *, size, pk):
-    at, entry = 2 * size, 4 * size // min(BLOCK, size)
-    parts = [get_gram(ref, at + TABLE, pk, get_table(ref, at)[entry : entry + 1, :]) for ref in (sent, got)]
-    out[...] = (parts[0] + parts[1]).astype(BF16)
-
-
-def new_w_body(gram_mine, gram_other, wa, wb, sent, got, out, *, size):
+    half = rows.shape[0] // 2
+    low, high = rows[:half], rows[half:]
+    side = doc_bit(bit)
+    put_parts(outs[0], [pick(side, high, low), gram])
+    outs[1][...] = pick(side, low, high)
+
+
+def gram_h_body(sent, got, out, *, size):
+    pk = out.shape[0]
+    out[...] = (get_parts(sent, (size, pk))[1] + get_parts(got, (size, pk))[1]).astype(BF16)
+
+
+def new_w_body(gram_mine, gram_other, w, sent, got, out):
     core = core_index()
     one, two = gram_mine[...], gram_other[...]
     gram = unpack(pick(core, one, two), pick(core, two, one))
-    group = min(BLOCK, size)
-    parts = [get_codes(ref, 0, 2 * size, group, get_table(ref, 2 * size), 0) for ref in (sent, got)]
-    total = parts[0] + parts[1]
-    for first, old_ref in ((0, wa), (size, wb)):
-        old = old_ref[...]
-        part = slice(first, first + size)
-        out[part, :] = (old.astype(F32) * total[part] / nn(old, gram)).astype(BF16)
-
-
-def swap(x, axis, size, bit):
-    return lax.ppermute(x, axis, [(i, i ^ (1 << bit)) for i in range(size)])
+    size, pk = w.shape[0], one.shape[0]
+    total = get_parts(sent, (size, pk))[0] + get_parts(got, (size, pk))[0]
+    old = w[...]
+    out[...] = (old.astype(F32) * total / nn(old, gram)).astype(BF16)
+
+
+def new_w_out_body(own, one, two, three, out):
+    size = own.shape[0]
+    for away, ref in enumerate((own, one, two, three)):
+        out[pl.ds(pl.multiple_of((quad_index() ^ away) * size, size), size), :] = ref[...]
+
+
+def swap(x, axis, size, away):
+    return lax.ppermute(x, axis, [(i, i ^ away) for i in range(size)])
 
 
 def join(bit, mine, other):
@@ -376,14 +367,12 @@
     pk = 3 * k // 8
     bits = n_doc.bit_length() - 1
     term_bits = n_term.bit_length() - 1
-    order = [tuple(pair) for pair in zip(range(bits), [1, 0] + list(range(2, bits)))]
-    same = [one == two for one, two in order]
 
     def over_term(x, bit):
-        return swap(x, "term", n_term, bit)
-
-    def over_doc(x, bit):
-        return swap(x, "doc", n_doc, bit)
+        return swap(x, "term", n_term, 1 << bit)
+
+    def over_doc(x, away):
+        return swap(x, "doc", n_doc, away)
 
     flops = terms * docs * k
     moved = 2 * terms * docs
@@ -423,68 +412,39 @@
 
     part = call(first_w_body, like(terms, k), (masked_own, h_own), flops=flops, moved=moved)
     size = terms // 4
-
-    def payloads(rows, merged):
-        if merged:
-            return (like(2 * rows + TABLE + 2 * pk, k, dtype=jnp.int16),)
-        return (like(rows + TABLE + 2 * pk, k, dtype=jnp.int16), like(rows + TABLE, k, dtype=jnp.int16))
-
-    *sent, keep_a, keep_b, new_h = call(
-        functools.partial(second_w_body, bits=order[0]),
-        payloads(size, False) + (like(size, k),) * 2 + (like(k, docs, dtype=BF16),),
-        (masked_other, part, h_other, h_own),
-        flops=flops,
-        moved=moved,
-    )
-    for step in range(bits):
-        got = [over_doc(x, order[step][i]) for i, x in enumerate(sent)]
-        if step == bits - 1:
-            break
-        last = step == bits - 2
-        body = functools.partial(
-            next_step_body,
-            size=size,
-            pk=pk,
-            bits=order[step + 1],
-            was_merged=same[step],
-            merged=same[step + 1],
-            last=last,
-        )
-        args = (keep_a, keep_b, *sent, *got)
-        if last:
-            sent = call(body, payloads(size, True), args)
-        else:
-            size //= 2
-            *sent, keep_a, keep_b = call(body, payloads(size, same[step + 1]) + (like(size, k),) * 2, args)
-    ends = (sent[0], got[0])
-    g_mine = call(functools.partial(gram_h_body, size=size, pk=pk), like(pk, k, dtype=BF16), ends)
+    payload = lambda rows: like(rows + pk + TABLE, k, dtype=jnp.int16)
+    costs = dict(flops=flops // 4, moved=moved // 4)
+    sent, got = {}, {}
+    body = functools.partial(first_send_body, away=3)
+    sent[3], gram = call(body, (payload(size), like(pk, k)), (masked_other, part, h_other, h_own), **costs)
+    for away in (1, 2):
+        body = functools.partial(send_body, away=away)
+        sent[away] = call(body, payload(size), (masked_other, part, h_other, gram), **costs)
+    for away in (3, 1, 2):
+        got[away] = over_doc(sent[away], away)
+    keep = call(keep_rows_body, like(size, k), (masked_other, part, h_other), **costs)
+    new_h = call(new_h_out_body, like(k, docs, dtype=BF16), (h_other, h_own))
+    ends = (sent[1], got[1], got[2], got[3])
+    for bit in range(2, bits):
+        last = bit == bits - 1
+        body = quad_sum_body if bit == 2 else step_sum_body
+        rows = size if last else size // 2
+        outs = (payload(rows),) if last else (payload(rows), like(rows, k))
+        moving, *kept = call(functools.partial(body, pk=pk, bit=bit, last=last), outs, (keep, *ends))
+        keep, size = (kept[0] if kept else None), rows
+        ends = (moving, over_doc(moving, 1 << bit))
+    g_mine = call(functools.partial(gram_h_body, size=size), like(pk, k, dtype=BF16), ends)
     g_other = over_term(g_mine, 0)
-    old = []
-    for stream in range(2):
-        start = jnp.int32(stream * (terms // 2))
-        for step in range(bits - 1):
-            start += doc_bit(order[step][stream]) * (terms // 2 >> (step + 1))
-        old.append(lax.dynamic_slice_in_dim(w, start, size, 0))
-    both = call(
-        functools.partial(new_w_body, size=size),
-        like(2 * size, k, dtype=BF16),
-        (g_mine, g_other, *old, *ends),
-    )
-    for step in reversed(range(bits - 1)):
-        if same[step]:
-            got = over_doc(both, order[step][0])
-            w_a, w_b = [
-                join(doc_bit(order[step][0]), both[i * size : (i + 1) * size], got[i * size : (i + 1) * size])
-                for i in range(2)
-            ]
-        else:
-            w_a, w_b = both[:size], both[size:]
-            w_a, w_b = [
-                join(doc_bit(bit), x, over_doc(x, bit)) for x, bit in zip((w_a, w_b), order[step])
-            ]
-        size *= 2
-        both = jnp.concatenate([w_a, w_b], axis=0)
-    return both, new_h
+    start = quad_index() * (terms // 4)
+    for bit in range(2, bits - 1):
+        start += doc_bit(bit) * (terms // 4 >> (bit - 1))
+    old = lax.dynamic_slice_in_dim(w, start, size, 0)
+    share = call(new_w_body, like(size, k, dtype=BF16), (g_mine, g_other, old, *ends))
+    for bit in reversed(range(2, bits - 1)):
+        share = join(doc_bit(bit), share, over_doc(share, 1 << bit))
+    shares = {away: over_doc(share, away) for away in (3, 1, 2)}
+    new_w = call(new_w_out_body, like(terms, k, dtype=BF16), (share, shares[1], shares[2], shares[3]))
+    return new_w, new_h
 
 
 def solution(mesh):

time: 65.5 us -> 59.8 us (0.913)
  starting transfers between devices: 18.6 us -> 13.8 us
  Pallas kernels: 6.95 us -> 8.6 us
  waiting for transfers between devices: 35.9 us -> 34.3 us
  other arithmetic: 0.97 us -> 0 us
    ppermute x16 -> x14, starting transfers between devices: 18.6 us -> 13.8 us  [swap(): return lax.ppermute(x, axis, [(i, i ^ away) for i in range(size)])]
    pallas_call x14 -> x18, Pallas kernels: 6.95 us -> 8.6 us  [call(): pl.pallas_call(body, out_shape=out, in_specs=[HBM if i in hbm else VMEM f...]
    ppermute x16 -> x14, waiting for transfers between devices: 35.9 us -> 34.3 us  [swap(): return lax.ppermute(x, axis, [(i, i ^ away) for i in range(size)])]
    concatenate x3 -> x0, other arithmetic: 0.85 us -> none  [the longest x1 0.83 us: update(): both = jnp.concatenate([w_a, w_b], axis=0)]
  transfers between devices with their start and end apart: 16 -> 14, of which waited for: 13 -> 11; matrix products, arithmetic and copies ran while one was open for 1% -> 2% of each run, Pallas kernels for 2% -> 4%
where the time goes in v3:
time: 59.8 us; the launch traced here: 59.5 us
  waiting for transfers between devices  34.3 us (57%)
  starting transfers between devices  13.8 us (23%)
  Pallas kernels  8.6 us (14%)
  local copies, waits for them, and re-layouts  1.97 us (3%)
  between operations  0.8 us (1%)
    ppermute x14, waiting for transfers between devices, swap(): return lax.ppermute(x, axis, [(i, i ^ away) for i in range(size)])  34.3 us
    ppermute x14, starting transfers between devices, swap(): return lax.ppermute(x, axis, [(i, i ^ away) for i in range(size)])  13.8 us
    pallas_call x18, Pallas kernels, call(): pl.pallas_call(body, out_shape=out, in_specs=[HBM if i in hbm else VMEM f...  8.6 us
  transfers between devices with their start and end apart: 14, of which 11 were waited for; matrix products, arithmetic and copies ran while one was open for 2% of the time, Pallas kernels for 4%

profile of v3, /device:TPU:0, one launch (start us, length us, event | category | flops | bytes accessed | tf_op | source)
XLA Modules:
  0.0 59.5 jit_solution(15323016746245189117)
XLA Ops:
  0.6 1.0 %copy-done = bf16[1024,256]{1,0:T(8,128)(2,1)S(1)} copy-done((bf16[1024,256]{1,0:T(8,128)(2,1)S(1)}, bf16[1024,256]{1,0:T(8,128)(2,1)}, u32[]{:S(2)}) %copy-start) | copy-done | bytes 524312
  1.7 2.2 %shard_map.59 = (bf16[256,1024]{1,0:T(8,128)(2,1)S(1)}, f32[96,256]{1,0:T(8,128)S(1)}, f32[96,256]{1,0:T(8,128)S(1)}, bf16[1024,512]{1,0:T(8,128)(2,1)S(1)}, bf16[1024,512]{1,0:T(8,128)(2,1)S(1)}) custom-call(bf16[1024,1024]{1,0:T(8,128)(2,1)} %m.1, bf16[1024,256]{1,0:T(8,128)(2,1)S(1)} %copy-done), custom_call_target="tpu_custom_call" | custom-call | flops 1048576 | bytes 1048576 | tf_op jit(solution)/shard_map/pallas_call | solution.py:30
  3.9 0.6 %shard_map.60 = (f32[256,512]{1,0:T(8,128)S(1)}, bf16[1024,512]{1,0:T(8,128)(2,1)S(1)}) custom-call(bf16[1024,512]{1,0:T(8,128)(2,1)S(1)} %get-tuple-element.13.half, s32[8,8]{1,0:T(8,128)S(1)} %copy-done.2, bf16[256,1024]{1,0:T(8,128)(2,1)S(1)} %get-tuple-element.14.wt), custom_call_target="tpu_custom_call" | custom-call | flops 268435456 | bytes 2097152 | tf_op jit(solution)/shard_map/pallas_call | solution.py:30
  4.6 0.6 collective-permute-start.1
  5.2 1.6 %collective-permute-done.b = f32[96,256]{1,0:T(8,128)S(1)} collective-permute-done((f32[96,256]{1,0:T(8,128)S(1)}, f32[96,256]{1,0:T(8,128)S(1)}, u32[]{:S(2)}, u32[]{:S(2)}) %collective-permute-start) | collective-permute-done | bytes 98336 | tf_op jit(solution)/shard_map/ppermute | solution.py:352
  6.8 0.6 %shard_map.62 = (f32[256,512]{1,0:T(8,128)S(1)}, bf16[1024,512]{1,0:T(8,128)(2,1)S(1)}) custom-call(bf16[1024,512]{1,0:T(8,128)(2,1)S(1)} %get-tuple-element.16.half, s32[8,8]{1,0:T(8,128)S(1)} %copy-done.2, bf16[256,1024]{1,0:T(8,128)(2,1)S(1)} %get-tuple-element.14.wt, f32[96,256]{1,0:T(8,128)S(1)} %shard_map.61.refs_0_.a), custom_call_target="tpu_custom_call" | custom-call | flops 268435456 | bytes 2097152 | tf_op jit(solution)/shard_map/pallas_call | solution.py:30
  7.7 2.9 %collective-permute-start.2 = (s16[272,512]{1,0:T(8,128)(2,1)S(1)}, s16[272,512]{1,0:T(8,128)(2,1)S(1)}, u32[]{:S(2)}, u32[]{:S(2)}) collective-permute-start(s16[272,512]{1,0:T(8,128)(2,1)S(1)} %shard_map.63.mine), channel_id=1, source_target_pairs={{0,2},{1,3},{2,0},{3,1},{4,6},{5,7},{6,4},{7,5},{8,10},{9,11},{10,... | collective-permute-start | bytes 835592 | tf_op jit(solution)/shard_map/ppermute | solution.py:352
  10.7 9.0 %collective-permute-done.3.b = f32[96,256]{1,0:T(8,128)S(1)} collective-permute-done((f32[96,256]{1,0:T(8,128)S(1)}, f32[96,256]{1,0:T(8,128)S(1)}, u32[]{:S(2)}, u32[]{:S(2)}) %collective-permute-start.3) | collective-permute-done | bytes 98336 | tf_op jit(solution)/shard_map/ppermute | solution.py:352
  19.8 1.2 %collective-permute-done.4.gram_other = bf16[96,256]{1,0:T(8,128)(2,1)S(1)} collective-permute-done((bf16[96,256]{1,0:T(8,128)(2,1)S(1)}, bf16[96,256]{1,0:T(8,128)(2,1)S(1)}, u32[]{:S(2)}, u32[]{:S(2)}) %collective-permute-start.4) | collective-permute-done | bytes 49184 | tf_op jit(solution)/shard_map/ppermute | solution.py:352
  22.0 0.9 %collective-permute-done.5.h = bf16[256,512]{1,0:T(8,128)(2,1)S(1)} collective-permute-done((bf16[256,512]{1,0:T(8,128)(2,1)S(1)}, bf16[256,512]{1,0:T(8,128)(2,1)S(1)}, u32[]{:S(2)}, u32[]{:S(2)}) %collective-permute-start.5) | collective-permute-done | bytes 262176 | tf_op jit(solution)/shard_map/ppermute | solution.py:352
  23.9 1.9 %collective-permute-start.7 = (s16[368,256]{1,0:T(8,128)(2,1)S(1)}, s16[368,256]{1,0:T(8,128)(2,1)S(1)}, u32[]{:S(2)}, u32[]{:S(2)}) collective-permute-start(s16[368,256]{1,0:T(8,128)(2,1)S(1)} %shard_map.71), channel_id=1, source_target_pairs={{0,8},{4,12},{8,0},{12,4},{16,24},{20,28},{24,16},{28,20},{1,9},{5... | collective-permute-start | bytes 565256 | tf_op jit(solution)/shard_map/ppermute | solution.py:352
  26.2 1.6 %collective-permute-start.6 = (s16[368,256]{1,0:T(8,128)(2,1)S(1)}, s16[368,256]{1,0:T(8,128)(2,1)S(1)}, u32[]{:S(2)}, u32[]{:S(2)}) collective-permute-start(s16[368,256]{1,0:T(8,128)(2,1)S(1)} %shard_map.70.own), channel_id=1, source_target_pairs={{0,4},{4,0},{8,12},{12,8},{16,20},{20,16},{24,28},{28,24},{1,5},{5... | collective-permute-start | bytes 565256 | tf_op jit(solution)/shard_map/ppermute | solution.py:352
  28.2 3.4 %collective-permute-done.7.two = s16[368,256]{1,0:T(8,128)(2,1)S(1)} collective-permute-done((s16[368,256]{1,0:T(8,128)(2,1)S(1)}, s16[368,256]{1,0:T(8,128)(2,1)S(1)}, u32[]{:S(2)}, u32[]{:S(2)}) %collective-permute-start.7) | collective-permute-done | bytes 188448 | tf_op jit(solution)/shard_map/ppermute | solution.py:352
  31.6 5.2 %collective-permute-done.6.one = s16[368,256]{1,0:T(8,128)(2,1)S(1)} collective-permute-done((s16[368,256]{1,0:T(8,128)(2,1)S(1)}, s16[368,256]{1,0:T(8,128)(2,1)S(1)}, u32[]{:S(2)}, u32[]{:S(2)}) %collective-permute-start.6) | collective-permute-done | bytes 188448 | tf_op jit(solution)/shard_map/ppermute | solution.py:352
  37.3 2.7 %collective-permute-start.9 = (s16[368,256]{1,0:T(8,128)(2,1)S(1)}, s16[368,256]{1,0:T(8,128)(2,1)S(1)}, u32[]{:S(2)}, u32[]{:S(2)}) collective-permute-start(s16[368,256]{1,0:T(8,128)(2,1)S(1)} %shard_map.72.sent), channel_id=1, source_target_pairs={{0,16},{4,20},{8,24},{12,28},{16,0},{20,4},{24,8},{28,12},{1,17},{... | collective-permute-start | bytes 565256 | tf_op jit(solution)/shard_map/ppermute | solution.py:352
  39.9 7.5 %collective-permute-done.9.got = s16[368,256]{1,0:T(8,128)(2,1)S(1)} collective-permute-done((s16[368,256]{1,0:T(8,128)(2,1)S(1)}, s16[368,256]{1,0:T(8,128)(2,1)S(1)}, u32[]{:S(2)}, u32[]{:S(2)}) %collective-permute-start.9) | collective-permute-done | bytes 188448 | tf_op jit(solution)/shard_map/ppermute | solution.py:352
  47.5 0.9 %constant_dynamic-slice_fusion.w = bf16[256,256]{1,0:T(8,128)(2,1)S(1)} fusion(bf16[1024,256]{1,0:T(8,128)(2,1)} %w.1, s32[]{:T(128)S(6)} %select_n.3), kind=kLoop, calls=%fused_computation | loop fusion | bytes 262148 | tf_op jit(solution)/shard_map/dynamic_slice | solution.py:441
  49.0 1.6 %collective-permute-start.11 = (bf16[256,256]{1,0:T(8,128)(2,1)S(1)}, bf16[256,256]{1,0:T(8,128)(2,1)S(1)}, u32[]{:S(2)}, u32[]{:S(2)}) collective-permute-start(bf16[256,256]{1,0:T(8,128)(2,1)S(1)} %shard_map.74.own), channel_id=1, source_target_pairs={{0,4},{4,0},{8,12},{12,8},{16,20},{20,16},{24,28},{28,24},{1,5},{5... | collective-permute-start | bytes 393224 | tf_op jit(solution)/shard_map/ppermute | solution.py:352
  50.6 2.0 %collective-permute-start.13 = (bf16[256,256]{1,0:T(8,128)(2,1)S(1)}, bf16[256,256]{1,0:T(8,128)(2,1)S(1)}, u32[]{:S(2)}, u32[]{:S(2)}) collective-permute-start(bf16[256,256]{1,0:T(8,128)(2,1)S(1)} %shard_map.74.own), channel_id=1, source_target_pairs={{0,12},{4,8},{8,4},{12,0},{16,28},{20,24},{24,20},{28,16},{1,13},{... | collective-permute-start | bytes 393224 | tf_op jit(solution)/shard_map/ppermute | solution.py:352
  52.6 0.8 %shard_map.76 = bf16[256,1024]{1,0:T(8,128)(2,1)} custom-call(bf16[256,512]{1,0:T(8,128)(2,1)S(1)} %collective-permute-done.5.h, bf16[256,512]{1,0:T(8,128)(2,1)S(1)} %shard_map.66.h.h_own), custom_call_target="tpu_custom_call" | custom-call | flops 1048576 | bytes 1048576 | tf_op jit(solution)/shard_map/pallas_call | solution.py:30
  53.4 1.3 %collective-permute-done.11.one = bf16[256,256]{1,0:T(8,128)(2,1)S(1)} collective-permute-done((bf16[256,256]{1,0:T(8,128)(2,1)S(1)}, bf16[256,256]{1,0:T(8,128)(2,1)S(1)}, u32[]{:S(2)}, u32[]{:S(2)}) %collective-permute-start.11) | collective-permute-done | bytes 131104 | tf_op jit(solution)/shard_map/ppermute | solution.py:352
  54.7 2.3 %collective-permute-done.12.two = bf16[256,256]{1,0:T(8,128)(2,1)S(1)} collective-permute-done((bf16[256,256]{1,0:T(8,128)(2,1)S(1)}, bf16[256,256]{1,0:T(8,128)(2,1)S(1)}, u32[]{:S(2)}, u32[]{:S(2)}) %collective-permute-start.12) | collective-permute-done | bytes 131104 | tf_op jit(solution)/shard_map/ppermute | solution.py:352
  57.0 1.7 %collective-permute-done.13.three = bf16[256,256]{1,0:T(8,128)(2,1)S(1)} collective-permute-done((bf16[256,256]{1,0:T(8,128)(2,1)S(1)}, bf16[256,256]{1,0:T(8,128)(2,1)S(1)}, u32[]{:S(2)}, u32[]{:S(2)}) %collective-permute-start.13) | collective-permute-done | bytes 131104 | tf_op jit(solution)/shard_map/ppermute | solution.py:352
  58.7 0.8 %shard_map.75 = bf16[1024,256]{1,0:T(8,128)(2,1)} custom-call(bf16[256,256]{1,0:T(8,128)(2,1)S(1)} %shard_map.74.own, bf16[256,256]{1,0:T(8,128)(2,1)S(1)} %collective-permute-done.11.one, bf16[256,256]{1,0:T(8,128)(2,1)S(1)} %collective-permute-done.12.two, bf16[256,256]{1,0:T(8,128)(2,1)S(1)} %collective-permute-done.13.three), custom_call_target="tpu_custom_call" | custom-call | flops 1048576 | bytes 1048576 | tf_op jit(solution)/shard_map/pallas_call | solution.py:30
  (29 shorter events, 4.5 us)
Async XLA Ops:
  0.6 1.0 %copy-start = (bf16[1024,256]{1,0:T(8,128)(2,1)S(1)}, bf16[1024,256]{1,0:T(8,128)(2,1)}, u32[]{:S(2)}) copy-start(bf16[1024,256]{1,0:T(8,128)(2,1)} %w.1) | copy-start | bytes 1572868
  1.7 2.3 %copy-start.2 = (s32[8,8]{1,0:T(8,128)S(1)}, s32[8,8]{1,0:T(8,128)}, u32[]{:S(2)}) copy-start(s32[8,8]{1,0:T(8,128)} %pattern.3) | copy-start | bytes 772
  4.5 15.2 %copy-start.1 = (bf16[256,1024]{1,0:T(8,128)(2,1)S(1)}, bf16[256,1024]{1,0:T(8,128)(2,1)}, u32[]{:S(2)}) copy-start(bf16[256,1024]{1,0:T(8,128)(2,1)} %h.1) | copy-start | bytes 1572868
  4.6 2.9 %collective-permute-start.1 = (f32[256,512]{1,0:T(8,128)S(1)}, f32[256,512]{1,0:T(8,128)S(1)}, u32[]{:S(2)}, u32[]{:S(2)}) collective-permute-start(f32[256,512]{1,0:T(8,128)S(1)} %get-tuple-element.21), channel_id=1, source_target_pairs={{0,1},{1,0},{2,3},{3,2},{4,5},{5,4},{6,7},{7,6},{8,9},{9,8},{10,11... | collective-permute-start | bytes 1572872 | tf_op jit(solution)/shard_map/ppermute | solution.py:352
  5.1 1.7 %collective-permute-start = (f32[96,256]{1,0:T(8,128)S(1)}, f32[96,256]{1,0:T(8,128)S(1)}, u32[]{:S(2)}, u32[]{:S(2)}) collective-permute-start(f32[96,256]{1,0:T(8,128)S(1)} %get-tuple-element.18), channel_id=1, source_target_pairs={{0,1},{1,0},{2,3},{3,2},{4,5},{5,4},{6,7},{7,6},{8,9},{9,8},{10,11... | collective-permute-start | bytes 294920 | tf_op jit(solution)/shard_map/ppermute | solution.py:352
  7.7 13.3 %collective-permute-start.2 = (s16[272,512]{1,0:T(8,128)(2,1)S(1)}, s16[272,512]{1,0:T(8,128)(2,1)S(1)}, u32[]{:S(2)}, u32[]{:S(2)}) collective-permute-start(s16[272,512]{1,0:T(8,128)(2,1)S(1)} %shard_map.63.mine), channel_id=1, source_target_pairs={{0,2},{1,3},{2,0},{3,1},{4,6},{5,7},{6,4},{7,5},{8,10},{9,11},{10,... | collective-permute-start | bytes 835592 | tf_op jit(solution)/shard_map/ppermute | solution.py:352
  10.6 9.1 %collective-permute-start.3 = (f32[96,256]{1,0:T(8,128)S(1)}, f32[96,256]{1,0:T(8,128)S(1)}, u32[]{:S(2)}, u32[]{:S(2)}) collective-permute-start(f32[96,256]{1,0:T(8,128)S(1)} %shard_map.61.refs_0_.a), channel_id=1, source_target_pairs={{0,2},{1,3},{2,0},{3,1},{4,6},{5,7},{6,4},{7,5},{8,10},{9,11},{10,... | collective-permute-start | bytes 294920 | tf_op jit(solution)/shard_map/ppermute | solution.py:352
  19.7 1.3 %collective-permute-start.4 = (bf16[96,256]{1,0:T(8,128)(2,1)S(1)}, bf16[96,256]{1,0:T(8,128)(2,1)S(1)}, u32[]{:S(2)}, u32[]{:S(2)}) collective-permute-start(bf16[96,256]{1,0:T(8,128)(2,1)S(1)} %shard_map.64.gram_mine), channel_id=1, source_target_pairs={{0,1},{1,0},{2,3},{3,2},{4,5},{5,4},{6,7},{7,6},{8,9},{9,8},{10,11... | collective-permute-start | bytes 147464 | tf_op jit(solution)/shard_map/ppermute | solution.py:352
  21.3 1.6 %collective-permute-start.5 = (bf16[256,512]{1,0:T(8,128)(2,1)S(1)}, bf16[256,512]{1,0:T(8,128)(2,1)S(1)}, u32[]{:S(2)}, u32[]{:S(2)}) collective-permute-start(bf16[256,512]{1,0:T(8,128)(2,1)S(1)} %shard_map.66.h.h_own), channel_id=1, source_target_pairs={{0,1},{1,0},{2,3},{3,2},{4,5},{5,4},{6,7},{7,6},{8,9},{9,8},{10,11... | collective-permute-start | bytes 786440 | tf_op jit(solution)/shard_map/ppermute | solution.py:352
  23.9 7.7 %collective-permute-start.7 = (s16[368,256]{1,0:T(8,128)(2,1)S(1)}, s16[368,256]{1,0:T(8,128)(2,1)S(1)}, u32[]{:S(2)}, u32[]{:S(2)}) collective-permute-start(s16[368,256]{1,0:T(8,128)(2,1)S(1)} %shard_map.71), channel_id=1, source_target_pairs={{0,8},{4,12},{8,0},{12,4},{16,24},{20,28},{24,16},{28,20},{1,9},{5... | collective-permute-start | bytes 565256 | tf_op jit(solution)/shard_map/ppermute | solution.py:352
  26.2 10.6 %collective-permute-start.6 = (s16[368,256]{1,0:T(8,128)(2,1)S(1)}, s16[368,256]{1,0:T(8,128)(2,1)S(1)}, u32[]{:S(2)}, u32[]{:S(2)}) collective-permute-start(s16[368,256]{1,0:T(8,128)(2,1)S(1)} %shard_map.70.own), channel_id=1, source_target_pairs={{0,4},{4,0},{8,12},{12,8},{16,20},{20,16},{24,28},{28,24},{1,5},{5... | collective-permute-start | bytes 565256 | tf_op jit(solution)/shard_map/ppermute | solution.py:352
  27.8 9.0 %collective-permute-start.8 = (s16[368,256]{1,0:T(8,128)(2,1)S(1)}, s16[368,256]{1,0:T(8,128)(2,1)S(1)}, u32[]{:S(2)}, u32[]{:S(2)}) collective-permute-start(s16[368,256]{1,0:T(8,128)(2,1)S(1)} %get-tuple-element.23), channel_id=1, source_target_pairs={{0,12},{4,8},{8,4},{12,0},{16,28},{20,24},{24,20},{28,16},{1,13},{... | collective-permute-start | bytes 565256 | tf_op jit(solution)/shard_map/ppermute | solution.py:352
  37.3 10.1 %collective-permute-start.9 = (s16[368,256]{1,0:T(8,128)(2,1)S(1)}, s16[368,256]{1,0:T(8,128)(2,1)S(1)}, u32[]{:S(2)}, u32[]{:S(2)}) collective-permute-start(s16[368,256]{1,0:T(8,128)(2,1)S(1)} %shard_map.72.sent), channel_id=1, source_target_pairs={{0,16},{4,20},{8,24},{12,28},{16,0},{20,4},{24,8},{28,12},{1,17},{... | collective-permute-start | bytes 565256 | tf_op jit(solution)/shard_map/ppermute | solution.py:352
  47.5 1.3 %collective-permute-start.10 = (bf16[96,256]{1,0:T(8,128)(2,1)S(1)}, bf16[96,256]{1,0:T(8,128)(2,1)S(1)}, u32[]{:S(2)}, u32[]{:S(2)}) collective-permute-start(bf16[96,256]{1,0:T(8,128)(2,1)S(1)} %shard_map.73.gram_mine), channel_id=1, source_target_pairs={{0,1},{1,0},{2,3},{3,2},{4,5},{5,4},{6,7},{7,6},{8,9},{9,8},{10,11... | collective-permute-start | bytes 147464 | tf_op jit(solution)/shard_map/ppermute | solution.py:352
  49.0 5.7 %collective-permute-start.11 = (bf16[256,256]{1,0:T(8,128)(2,1)S(1)}, bf16[256,256]{1,0:T(8,128)(2,1)S(1)}, u32[]{:S(2)}, u32[]{:S(2)}) collective-permute-start(bf16[256,256]{1,0:T(8,128)(2,1)S(1)} %shard_map.74.own), channel_id=1, source_target_pairs={{0,4},{4,0},{8,12},{12,8},{16,20},{20,16},{24,28},{28,24},{1,5},{5... | collective-permute-start | bytes 393224 | tf_op jit(solution)/shard_map/ppermute | solution.py:352
  50.6 6.4 %collective-permute-start.12 = (bf16[256,256]{1,0:T(8,128)(2,1)S(1)}, bf16[256,256]{1,0:T(8,128)(2,1)S(1)}, u32[]{:S(2)}, u32[]{:S(2)}) collective-permute-start(bf16[256,256]{1,0:T(8,128)(2,1)S(1)} %shard_map.74.own), channel_id=1, source_target_pairs={{0,8},{4,12},{8,0},{12,4},{16,24},{20,28},{24,16},{28,20},{1,9},{5... | collective-permute-start | bytes 393224 | tf_op jit(solution)/shard_map/ppermute | solution.py:352
  50.6 8.1 %collective-permute-start.13 = (bf16[256,256]{1,0:T(8,128)(2,1)S(1)}, bf16[256,256]{1,0:T(8,128)(2,1)S(1)}, u32[]{:S(2)}, u32[]{:S(2)}) collective-permute-start(bf16[256,256]{1,0:T(8,128)(2,1)S(1)} %shard_map.74.own), channel_id=1, source_target_pairs={{0,12},{4,8},{8,4},{12,0},{16,28},{20,24},{24,20},{28,16},{1,13},{... | collective-permute-start | bytes 393224 | tf_op jit(solution)/shard_map/ppermute | solution.py:352

commit v4 on v3

--- a/solution.py
+++ b/solution.py
@@ -14,7 +14,6 @@
 VMEM = pl.BlockSpec(memory_space=pltpu.VMEM)
 HBM = pl.BlockSpec(memory_space=pltpu.HBM)
 PIECES = 4
-LIMIT = 50 << 20
 TABLE = 16
 
 
@@ -189,33 +188,14 @@
     return jnp.concatenate(out, axis=0)
 
 
-def load_body(m, w, wt, send, keep, own, other, w_all, sems):
+def gram_w_body(w, wt, send, keep):
     core = core_index()
-    terms, cols = own.shape
-    k = w.shape[1]
-    rows = terms // PIECES
-    columns = lambda side: pl.ds(pl.multiple_of(side * cols, cols), cols)
-    copies = []
-    for i in range(PIECES):
-        part = pl.ds(i * rows, rows)
-        copies.append(pltpu.make_async_copy(w.at[part, :], w_all.at[part, :], sems.at[i]))
-    copies.append(pltpu.make_async_copy(m.at[:, columns(1 - core)], other, sems.at[PIECES]))
-    copies.append(pltpu.make_async_copy(m.at[:, columns(core)], own, sems.at[PIECES + 1]))
-    for copy in copies:
-        copy.start()
-    gram = jnp.zeros((k, k), F32)
-    for i in range(PIECES):
-        part = slice(i * rows, (i + 1) * rows)
-        copies[i].wait()
-        piece = w_all[part, :]
-        flipped = piece.T
-        wt[:, part] = flipped
-        gram += nn(flipped, piece)
+    flipped = w[...].T
+    wt[...] = flipped
+    gram = nn(flipped, w[...])
     one, two = pack(gram, 0), pack(gram, 1)
     send[...] = pick(core, two, one)
     keep[...] = pick(core, one, two)
-    for copy in copies[PIECES:]:
-        copy.wait()
 
 
 def half_h_body(h, out):
@@ -223,11 +203,12 @@
     out[...] = h[:, pl.ds(pl.multiple_of(core_index() * cols, cols), cols)]
 
 
-def numer_body(half, pattern, wt, *refs, other):
+def numer_body(m, pattern, wt, *refs, other):
     out, masked = refs[-2:]
     side = 1 - core_index() if other else core_index()
-    terms, cols = half.shape
+    terms, cols = masked.shape
     rows = terms // PIECES
+    half = m.at[:, pl.ds(pl.multiple_of(side * cols, cols), cols)]
     mask = mask_rows(pattern[...], side, cols)
     for i in range(PIECES):
         part = slice(i * rows, (i + 1) * rows)
@@ -244,14 +225,14 @@
     out[...] = a[...] + b[...]
 
 
-def round_add_body(a, b, out):
-    out[...] = (a[...] + b[...]).astype(BF16)
+def round_sum_body(a, b, out):
+    rows = out.shape[0]
+    out[...] = (get_parts(a, (rows,))[0] + get_parts(b, (rows,))[0]).astype(BF16)
 
 
 def code_sum_body(a, b, out):
-    rows = a.shape[0]
-    table = put_codes(out, 0, [a[...] + b[...]])
-    put_table(out, rows, table)
+    total = a[...] + b[...]
+    put_table(out, total.shape[0], put_codes(out, 0, [total]))
 
 
 def new_h_body(mine, other, gram_mine, gram_other, h, out):
@@ -378,34 +359,30 @@
     moved = 2 * terms * docs
 
     side = like(terms, half, dtype=BF16)
-    wt, g_send, g_keep, own, other = call(
-        load_body,
-        (like(k, terms, dtype=BF16), like(pk, k), like(pk, k), side, side),
-        (m, w),
-        hbm=(0, 1),
-        scratch=(pltpu.VMEM((terms, k), BF16), pltpu.SemaphoreType.DMA((PIECES + 2,))),
-        limit=LIMIT,
+    wt, g_send, g_keep = call(
+        gram_w_body, (like(k, terms, dtype=BF16), like(pk, k), like(pk, k)), (w,), flops=32 * flops, moved=moved
     )
     g_got = over_term(g_send, 0)
 
-    def numer(half_m, is_other, *after):
+    def numer(is_other, *after):
         body = functools.partial(numer_body, other=is_other)
-        return call(body, (like(k, half), side), (half_m, pattern, wt, *after), flops=flops, moved=moved)
-
-    n_send, masked_other = numer(other, True)
+        return call(body, (like(k, half), side), (m, pattern, wt, *after), flops=flops, moved=moved)
+
+    n_send, masked_other = numer(True)
     n_got = over_term(n_send, 0)
-    g_sum = call(add_body, like(pk, k), (g_keep, g_got))
     for bit in range(1, term_bits - 1):
-        g_sum = g_sum + over_term(g_sum, bit)
+        g_keep = call(add_body, like(pk, k), (g_keep, g_got))
+        g_got = over_term(g_keep, bit)
+    g_sum = call(code_sum_body, like(pk + TABLE, k, dtype=jnp.int16), (g_keep, g_got))
     g_far = over_term(g_sum, term_bits - 1)
-    n_keep, masked_own = numer(own, False, g_sum)
+    n_keep, masked_own = numer(False, g_sum)
     h_old = call(half_h_body, like(k, half, dtype=BF16), (h,))
     for bit in range(1, term_bits - 1):
         n_keep = call(add_body, like(k, half), (n_keep, n_got))
         n_got = over_term(n_keep, bit)
     n_sum = call(code_sum_body, like(k + TABLE, half, dtype=jnp.int16), (n_keep, n_got))
     n_far = over_term(n_sum, term_bits - 1)
-    g_mine = call(round_add_body, like(pk, k, dtype=BF16), (g_sum, g_far))
+    g_mine = call(round_sum_body, like(pk, k, dtype=BF16), (g_sum, g_far))
     g_other = over_term(g_mine, 0)
     h_own = call(new_h_body, like(k, half, dtype=BF16), (n_sum, n_far, g_mine, g_other, h_old))
     h_other = over_term(h_own, 0)

time: 59.8 us -> 58.1 us (0.972)
  Pallas kernels: 8.6 us -> 6.83 us
  local copies, waits for them, and re-layouts: 1.97 us -> 2.58 us
  waiting for transfers between devices: 34.3 us -> 33.7 us
    pallas_call x18, Pallas kernels: 8.6 us -> 6.83 us  [call(): pl.pallas_call(body, out_shape=out, in_specs=[HBM if i in hbm else VMEM f...]
    ppermute x14, waiting for transfers between devices: 34.3 us -> 33.7 us  [swap(): return lax.ppermute(x, axis, [(i, i ^ away) for i in range(size)])]
    unnamed x6 -> x8, local copies, waits for them, and re-layouts: 1.05 us -> 1.66 us
  transfers between devices with their start and end apart: 14 -> 14, of which waited for: 11 -> 12; matrix products, arithmetic and copies ran while one was open for 2% -> 2% of each run, Pallas kernels for 4% -> 5%
where the time goes in v4:
time: 58.1 us; the launch traced here: 57.9 us
  waiting for transfers between devices  33.7 us (58%)
  starting transfers between devices  14 us (24%)
  Pallas kernels  6.83 us (12%)
  local copies, waits for them, and re-layouts  2.58 us (4%)
  between operations  0.8 us (1%)
    ppermute x14, waiting for transfers between devices, swap(): return lax.ppermute(x, axis, [(i, i ^ away) for i in range(size)])  33.7 us
    ppermute x14, starting transfers between devices, swap(): return lax.ppermute(x, axis, [(i, i ^ away) for i in range(size)])  14 us
    pallas_call x18, Pallas kernels, call(): pl.pallas_call(body, out_shape=out, in_specs=[HBM if i in hbm else VMEM f...  6.83 us
    unnamed x8, local copies, waits for them, and re-layouts  1.66 us
  transfers between devices with their start and end apart: 14, of which 12 were waited for; matrix products, arithmetic and copies ran while one was open for 2% of the time, Pallas kernels for 5%

profile of v4, /device:TPU:0, one launch (start us, length us, event | category | flops | bytes accessed | tf_op | source)
XLA Modules:
  0.0 57.9 jit_solution(15127623204154413049)
XLA Ops:
  0.7 1.2 %copy-done.2 = bf16[1024,256]{1,0:T(8,128)(2,1)S(1)} copy-done((bf16[1024,256]{1,0:T(8,128)(2,1)S(1)}, bf16[1024,256]{1,0:T(8,128)(2,1)}, u32[]{:S(2)}) %copy-start.2) | copy-done | bytes 524312
  2.7 0.6 %shard_map.60 = (f32[256,512]{1,0:T(8,128)S(1)}, bf16[1024,512]{1,0:T(8,128)(2,1)S(1)}) custom-call(bf16[1024,1024]{1,0:T(8,128)(2,1)S(1)} %copy-done, s32[8,8]{1,0:T(8,128)S(1)} %copy-done.3, bf16[256,1024]{1,0:T(8,128)(2,1)S(1)} %get-tuple-element.11.wt), custom_call_target="tpu_custom_call" | custom-call | flops 268435456 | bytes 2097152 | tf_op jit(solution)/shard_map/pallas_call | solution.py:29
  3.9 1.6 %collective-permute-done.b = f32[96,256]{1,0:T(8,128)S(1)} collective-permute-done((f32[96,256]{1,0:T(8,128)S(1)}, f32[96,256]{1,0:T(8,128)S(1)}, u32[]{:S(2)}, u32[]{:S(2)}) %collective-permute-start) | collective-permute-done | bytes 98336 | tf_op jit(solution)/shard_map/ppermute | solution.py:333
  5.6 0.6 %shard_map.62 = (f32[256,512]{1,0:T(8,128)S(1)}, bf16[1024,512]{1,0:T(8,128)(2,1)S(1)}) custom-call(bf16[1024,1024]{1,0:T(8,128)(2,1)S(1)} %copy-done, s32[8,8]{1,0:T(8,128)S(1)} %copy-done.3, bf16[256,1024]{1,0:T(8,128)(2,1)S(1)} %get-tuple-element.11.wt, s16[112,256]{1,0:T(8,128)(2,1)S(1)} %shard_map.61.refs_0_.a), custom_call_target="tpu_custom_call" | custom-call | flops 268435456 | bytes 2097152 | tf_op jit(solution)/shard_map/pallas_call | solution.py:29
  6.5 2.9 %collective-permute-start.2 = (s16[272,512]{1,0:T(8,128)(2,1)S(1)}, s16[272,512]{1,0:T(8,128)(2,1)S(1)}, u32[]{:S(2)}, u32[]{:S(2)}) collective-permute-start(s16[272,512]{1,0:T(8,128)(2,1)S(1)} %shard_map.63.mine), channel_id=1, source_target_pairs={{0,2},{1,3},{2,0},{3,1},{4,6},{5,7},{6,4},{7,5},{8,10},{9,11},{10,... | collective-permute-start | bytes 835592 | tf_op jit(solution)/shard_map/ppermute | solution.py:333
  9.5 8.1 %collective-permute-done.3.b = s16[112,256]{1,0:T(8,128)(2,1)S(1)} collective-permute-done((s16[112,256]{1,0:T(8,128)(2,1)S(1)}, s16[112,256]{1,0:T(8,128)(2,1)S(1)}, u32[]{:S(2)}, u32[]{:S(2)}) %collective-permute-start.3) | collective-permute-done | bytes 57376 | tf_op jit(solution)/shard_map/ppermute | solution.py:333
  17.8 1.2 %collective-permute-done.4.gram_other = bf16[96,256]{1,0:T(8,128)(2,1)S(1)} collective-permute-done((bf16[96,256]{1,0:T(8,128)(2,1)S(1)}, bf16[96,256]{1,0:T(8,128)(2,1)S(1)}, u32[]{:S(2)}, u32[]{:S(2)}) %collective-permute-start.4) | collective-permute-done | bytes 49184 | tf_op jit(solution)/shard_map/ppermute | solution.py:333
  20.0 0.9 %collective-permute-done.5.h = bf16[256,512]{1,0:T(8,128)(2,1)S(1)} collective-permute-done((bf16[256,512]{1,0:T(8,128)(2,1)S(1)}, bf16[256,512]{1,0:T(8,128)(2,1)S(1)}, u32[]{:S(2)}, u32[]{:S(2)}) %collective-permute-start.5) | collective-permute-done | bytes 262176 | tf_op jit(solution)/shard_map/ppermute | solution.py:333
  21.9 1.9 %collective-permute-start.6 = (s16[368,256]{1,0:T(8,128)(2,1)S(1)}, s16[368,256]{1,0:T(8,128)(2,1)S(1)}, u32[]{:S(2)}, u32[]{:S(2)}) collective-permute-start(s16[368,256]{1,0:T(8,128)(2,1)S(1)} %shard_map.70.own), channel_id=1, source_target_pairs={{0,4},{4,0},{8,12},{12,8},{16,20},{20,16},{24,28},{28,24},{1,5},{5... | collective-permute-start | bytes 565256 | tf_op jit(solution)/shard_map/ppermute | solution.py:333
  24.1 1.6 %collective-permute-start.7 = (s16[368,256]{1,0:T(8,128)(2,1)S(1)}, s16[368,256]{1,0:T(8,128)(2,1)S(1)}, u32[]{:S(2)}, u32[]{:S(2)}) collective-permute-start(s16[368,256]{1,0:T(8,128)(2,1)S(1)} %shard_map.71), channel_id=1, source_target_pairs={{0,8},{4,12},{8,0},{12,4},{16,24},{20,28},{24,16},{28,20},{1,9},{5... | collective-permute-start | bytes 565256 | tf_op jit(solution)/shard_map/ppermute | solution.py:333
  26.2 2.6 %collective-permute-done.6.one = s16[368,256]{1,0:T(8,128)(2,1)S(1)} collective-permute-done((s16[368,256]{1,0:T(8,128)(2,1)S(1)}, s16[368,256]{1,0:T(8,128)(2,1)S(1)}, u32[]{:S(2)}, u32[]{:S(2)}) %collective-permute-start.6) | collective-permute-done | bytes 188448 | tf_op jit(solution)/shard_map/ppermute | solution.py:333
  28.8 3.0 %collective-permute-done.7.two = s16[368,256]{1,0:T(8,128)(2,1)S(1)} collective-permute-done((s16[368,256]{1,0:T(8,128)(2,1)S(1)}, s16[368,256]{1,0:T(8,128)(2,1)S(1)}, u32[]{:S(2)}, u32[]{:S(2)}) %collective-permute-start.7) | collective-permute-done | bytes 188448 | tf_op jit(solution)/shard_map/ppermute | solution.py:333
  31.8 2.7 %collective-permute-done.8.three = s16[368,256]{1,0:T(8,128)(2,1)S(1)} collective-permute-done((s16[368,256]{1,0:T(8,128)(2,1)S(1)}, s16[368,256]{1,0:T(8,128)(2,1)S(1)}, u32[]{:S(2)}, u32[]{:S(2)}) %collective-permute-start.8) | collective-permute-done | bytes 188448 | tf_op jit(solution)/shard_map/ppermute | solution.py:333
  35.0 2.8 %collective-permute-start.9 = (s16[368,256]{1,0:T(8,128)(2,1)S(1)}, s16[368,256]{1,0:T(8,128)(2,1)S(1)}, u32[]{:S(2)}, u32[]{:S(2)}) collective-permute-start(s16[368,256]{1,0:T(8,128)(2,1)S(1)} %shard_map.72.sent), channel_id=1, source_target_pairs={{0,16},{4,20},{8,24},{12,28},{16,0},{20,4},{24,8},{28,12},{1,17},{... | collective-permute-start | bytes 565256 | tf_op jit(solution)/shard_map/ppermute | solution.py:333
  37.8 8.0 %collective-permute-done.9.got = s16[368,256]{1,0:T(8,128)(2,1)S(1)} collective-permute-done((s16[368,256]{1,0:T(8,128)(2,1)S(1)}, s16[368,256]{1,0:T(8,128)(2,1)S(1)}, u32[]{:S(2)}, u32[]{:S(2)}) %collective-permute-start.9) | collective-permute-done | bytes 188448 | tf_op jit(solution)/shard_map/ppermute | solution.py:333
  45.9 0.9 %constant_dynamic-slice_fusion.w = bf16[256,256]{1,0:T(8,128)(2,1)S(1)} fusion(bf16[1024,256]{1,0:T(8,128)(2,1)} %w.1, s32[]{:T(128)S(6)} %select_n.3), kind=kLoop, calls=%fused_computation | loop fusion | bytes 262148 | tf_op jit(solution)/shard_map/dynamic_slice | solution.py:418
  47.4 1.6 %collective-permute-start.11 = (bf16[256,256]{1,0:T(8,128)(2,1)S(1)}, bf16[256,256]{1,0:T(8,128)(2,1)S(1)}, u32[]{:S(2)}, u32[]{:S(2)}) collective-permute-start(bf16[256,256]{1,0:T(8,128)(2,1)S(1)} %shard_map.74.own), channel_id=1, source_target_pairs={{0,4},{4,0},{8,12},{12,8},{16,20},{20,16},{24,28},{28,24},{1,5},{5... | collective-permute-start | bytes 393224 | tf_op jit(solution)/shard_map/ppermute | solution.py:333
  49.0 0.7 %collective-permute-start.12 = (bf16[256,256]{1,0:T(8,128)(2,1)S(1)}, bf16[256,256]{1,0:T(8,128)(2,1)S(1)}, u32[]{:S(2)}, u32[]{:S(2)}) collective-permute-start(bf16[256,256]{1,0:T(8,128)(2,1)S(1)} %shard_map.74.own), channel_id=1, source_target_pairs={{0,8},{4,12},{8,0},{12,4},{16,24},{20,28},{24,16},{28,20},{1,9},{5... | collective-permute-start | bytes 393224 | tf_op jit(solution)/shard_map/ppermute | solution.py:333
  49.7 1.3 %collective-permute-start.13 = (bf16[256,256]{1,0:T(8,128)(2,1)S(1)}, bf16[256,256]{1,0:T(8,128)(2,1)S(1)}, u32[]{:S(2)}, u32[]{:S(2)}) collective-permute-start(bf16[256,256]{1,0:T(8,128)(2,1)S(1)} %shard_map.74.own), channel_id=1, source_target_pairs={{0,12},{4,8},{8,4},{12,0},{16,28},{20,24},{24,20},{28,16},{1,13},{... | collective-permute-start | bytes 393224 | tf_op jit(solution)/shard_map/ppermute | solution.py:333
  50.9 0.8 %shard_map.76 = bf16[256,1024]{1,0:T(8,128)(2,1)} custom-call(bf16[256,512]{1,0:T(8,128)(2,1)S(1)} %collective-permute-done.5.h, bf16[256,512]{1,0:T(8,128)(2,1)S(1)} %shard_map.66.h.h_own), custom_call_target="tpu_custom_call" | custom-call | flops 1048576 | bytes 1048576 | tf_op jit(solution)/shard_map/pallas_call | solution.py:29
  51.8 1.3 %collective-permute-done.11.one = bf16[256,256]{1,0:T(8,128)(2,1)S(1)} collective-permute-done((bf16[256,256]{1,0:T(8,128)(2,1)S(1)}, bf16[256,256]{1,0:T(8,128)(2,1)S(1)}, u32[]{:S(2)}, u32[]{:S(2)}) %collective-permute-start.11) | collective-permute-done | bytes 131104 | tf_op jit(solution)/shard_map/ppermute | solution.py:333
  53.1 2.3 %collective-permute-done.12.two = bf16[256,256]{1,0:T(8,128)(2,1)S(1)} collective-permute-done((bf16[256,256]{1,0:T(8,128)(2,1)S(1)}, bf16[256,256]{1,0:T(8,128)(2,1)S(1)}, u32[]{:S(2)}, u32[]{:S(2)}) %collective-permute-start.12) | collective-permute-done | bytes 131104 | tf_op jit(solution)/shard_map/ppermute | solution.py:333
  55.4 1.7 %collective-permute-done.13.three = bf16[256,256]{1,0:T(8,128)(2,1)S(1)} collective-permute-done((bf16[256,256]{1,0:T(8,128)(2,1)S(1)}, bf16[256,256]{1,0:T(8,128)(2,1)S(1)}, u32[]{:S(2)}, u32[]{:S(2)}) %collective-permute-start.13) | collective-permute-done | bytes 131104 | tf_op jit(solution)/shard_map/ppermute | solution.py:333
  57.1 0.8 %shard_map.75 = bf16[1024,256]{1,0:T(8,128)(2,1)} custom-call(bf16[256,256]{1,0:T(8,128)(2,1)S(1)} %shard_map.74.own, bf16[256,256]{1,0:T(8,128)(2,1)S(1)} %collective-permute-done.11.one, bf16[256,256]{1,0:T(8,128)(2,1)S(1)} %collective-permute-done.12.two, bf16[256,256]{1,0:T(8,128)(2,1)S(1)} %collective-permute-done.13.three), custom_call_target="tpu_custom_call" | custom-call | flops 1048576 | bytes 1048576 | tf_op jit(solution)/shard_map/pallas_call | solution.py:29
  (31 shorter events, 5.9 us)
Async XLA Ops:
  0.6 1.7 %copy-start = (bf16[1024,1024]{1,0:T(8,128)(2,1)S(1)}, bf16[1024,1024]{1,0:T(8,128)(2,1)}, u32[]{:S(2)}) copy-start(bf16[1024,1024]{1,0:T(8,128)(2,1)} %m.3) | copy-start | bytes 6291460
  0.6 1.2 %copy-start.2 = (bf16[1024,256]{1,0:T(8,128)(2,1)S(1)}, bf16[1024,256]{1,0:T(8,128)(2,1)}, u32[]{:S(2)}) copy-start(bf16[1024,256]{1,0:T(8,128)(2,1)} %w.1) | copy-start | bytes 1572868
  1.8 0.8 %copy-start.3 = (s32[8,8]{1,0:T(8,128)S(1)}, s32[8,8]{1,0:T(8,128)}, u32[]{:S(2)}) copy-start(s32[8,8]{1,0:T(8,128)} %pattern.3) | copy-start | bytes 772
  3.3 2.9 %collective-permute-start.1 = (f32[256,512]{1,0:T(8,128)S(1)}, f32[256,512]{1,0:T(8,128)S(1)}, u32[]{:S(2)}, u32[]{:S(2)}) collective-permute-start(f32[256,512]{1,0:T(8,128)S(1)} %get-tuple-element.17), channel_id=1, source_target_pairs={{0,1},{1,0},{2,3},{3,2},{4,5},{5,4},{6,7},{7,6},{8,9},{9,8},{10,11... | collective-permute-start | bytes 1572872 | tf_op jit(solution)/shard_map/ppermute | solution.py:333
  3.8 1.7 %collective-permute-start = (f32[96,256]{1,0:T(8,128)S(1)}, f32[96,256]{1,0:T(8,128)S(1)}, u32[]{:S(2)}, u32[]{:S(2)}) collective-permute-start(f32[96,256]{1,0:T(8,128)S(1)} %get-tuple-element.14), channel_id=1, source_target_pairs={{0,1},{1,0},{2,3},{3,2},{4,5},{5,4},{6,7},{7,6},{8,9},{9,8},{10,11... | collective-permute-start | bytes 294920 | tf_op jit(solution)/shard_map/ppermute | solution.py:333
  5.6 12.1 %copy-start.1 = (bf16[256,1024]{1,0:T(8,128)(2,1)S(1)}, bf16[256,1024]{1,0:T(8,128)(2,1)}, u32[]{:S(2)}) copy-start(bf16[256,1024]{1,0:T(8,128)(2,1)} %h.1) | copy-start | bytes 1572868
  6.5 12.5 %collective-permute-start.2 = (s16[272,512]{1,0:T(8,128)(2,1)S(1)}, s16[272,512]{1,0:T(8,128)(2,1)S(1)}, u32[]{:S(2)}, u32[]{:S(2)}) collective-permute-start(s16[272,512]{1,0:T(8,128)(2,1)S(1)} %shard_map.63.mine), channel_id=1, source_target_pairs={{0,2},{1,3},{2,0},{3,1},{4,6},{5,7},{6,4},{7,5},{8,10},{9,11},{10,... | collective-permute-start | bytes 835592 | tf_op jit(solution)/shard_map/ppermute | solution.py:333
  9.4 8.2 %collective-permute-start.3 = (s16[112,256]{1,0:T(8,128)(2,1)S(1)}, s16[112,256]{1,0:T(8,128)(2,1)S(1)}, u32[]{:S(2)}, u32[]{:S(2)}) collective-permute-start(s16[112,256]{1,0:T(8,128)(2,1)S(1)} %shard_map.61.refs_0_.a), channel_id=1, source_target_pairs={{0,2},{1,3},{2,0},{3,1},{4,6},{5,7},{6,4},{7,5},{8,10},{9,11},{10,... | collective-permute-start | bytes 172040 | tf_op jit(solution)/shard_map/ppermute | solution.py:333
  17.6 1.3 %collective-permute-start.4 = (bf16[96,256]{1,0:T(8,128)(2,1)S(1)}, bf16[96,256]{1,0:T(8,128)(2,1)S(1)}, u32[]{:S(2)}, u32[]{:S(2)}) collective-permute-start(bf16[96,256]{1,0:T(8,128)(2,1)S(1)} %shard_map.64.gram_mine), channel_id=1, source_target_pairs={{0,1},{1,0},{2,3},{3,2},{4,5},{5,4},{6,7},{7,6},{8,9},{9,8},{10,11... | collective-permute-start | bytes 147464 | tf_op jit(solution)/shard_map/ppermute | solution.py:333
  19.3 1.6 %collective-permute-start.5 = (bf16[256,512]{1,0:T(8,128)(2,1)S(1)}, bf16[256,512]{1,0:T(8,128)(2,1)S(1)}, u32[]{:S(2)}, u32[]{:S(2)}) collective-permute-start(bf16[256,512]{1,0:T(8,128)(2,1)S(1)} %shard_map.66.h.h_own), channel_id=1, source_target_pairs={{0,1},{1,0},{2,3},{3,2},{4,5},{5,4},{6,7},{7,6},{8,9},{9,8},{10,11... | collective-permute-start | bytes 786440 | tf_op jit(solution)/shard_map/ppermute | solution.py:333
  21.9 6.9 %collective-permute-start.6 = (s16[368,256]{1,0:T(8,128)(2,1)S(1)}, s16[368,256]{1,0:T(8,128)(2,1)S(1)}, u32[]{:S(2)}, u32[]{:S(2)}) collective-permute-start(s16[368,256]{1,0:T(8,128)(2,1)S(1)} %shard_map.70.own), channel_id=1, source_target_pairs={{0,4},{4,0},{8,12},{12,8},{16,20},{20,16},{24,28},{28,24},{1,5},{5... | collective-permute-start | bytes 565256 | tf_op jit(solution)/shard_map/ppermute | solution.py:333
  24.1 7.7 %collective-permute-start.7 = (s16[368,256]{1,0:T(8,128)(2,1)S(1)}, s16[368,256]{1,0:T(8,128)(2,1)S(1)}, u32[]{:S(2)}, u32[]{:S(2)}) collective-permute-start(s16[368,256]{1,0:T(8,128)(2,1)S(1)} %shard_map.71), channel_id=1, source_target_pairs={{0,8},{4,12},{8,0},{12,4},{16,24},{20,28},{24,16},{28,20},{1,9},{5... | collective-permute-start | bytes 565256 | tf_op jit(solution)/shard_map/ppermute | solution.py:333
  25.8 8.8 %collective-permute-start.8 = (s16[368,256]{1,0:T(8,128)(2,1)S(1)}, s16[368,256]{1,0:T(8,128)(2,1)S(1)}, u32[]{:S(2)}, u32[]{:S(2)}) collective-permute-start(s16[368,256]{1,0:T(8,128)(2,1)S(1)} %get-tuple-element.19), channel_id=1, source_target_pairs={{0,12},{4,8},{8,4},{12,0},{16,28},{20,24},{24,20},{28,16},{1,13},{... | collective-permute-start | bytes 565256 | tf_op jit(solution)/shard_map/ppermute | solution.py:333
  35.0 10.8 %collective-permute-start.9 = (s16[368,256]{1,0:T(8,128)(2,1)S(1)}, s16[368,256]{1,0:T(8,128)(2,1)S(1)}, u32[]{:S(2)}, u32[]{:S(2)}) collective-permute-start(s16[368,256]{1,0:T(8,128)(2,1)S(1)} %shard_map.72.sent), channel_id=1, source_target_pairs={{0,16},{4,20},{8,24},{12,28},{16,0},{20,4},{24,8},{28,12},{1,17},{... | collective-permute-start | bytes 565256 | tf_op jit(solution)/shard_map/ppermute | solution.py:333
  45.8 1.3 %collective-permute-start.10 = (bf16[96,256]{1,0:T(8,128)(2,1)S(1)}, bf16[96,256]{1,0:T(8,128)(2,1)S(1)}, u32[]{:S(2)}, u32[]{:S(2)}) collective-permute-start(bf16[96,256]{1,0:T(8,128)(2,1)S(1)} %shard_map.73.gram_mine), channel_id=1, source_target_pairs={{0,1},{1,0},{2,3},{3,2},{4,5},{5,4},{6,7},{7,6},{8,9},{9,8},{10,11... | collective-permute-start | bytes 147464 | tf_op jit(solution)/shard_map/ppermute | solution.py:333
  47.4 5.7 %collective-permute-start.11 = (bf16[256,256]{1,0:T(8,128)(2,1)S(1)}, bf16[256,256]{1,0:T(8,128)(2,1)S(1)}, u32[]{:S(2)}, u32[]{:S(2)}) collective-permute-start(bf16[256,256]{1,0:T(8,128)(2,1)S(1)} %shard_map.74.own), channel_id=1, source_target_pairs={{0,4},{4,0},{8,12},{12,8},{16,20},{20,16},{24,28},{28,24},{1,5},{5... | collective-permute-start | bytes 393224 | tf_op jit(solution)/shard_map/ppermute | solution.py:333
  49.0 6.4 %collective-permute-start.12 = (bf16[256,256]{1,0:T(8,128)(2,1)S(1)}, bf16[256,256]{1,0:T(8,128)(2,1)S(1)}, u32[]{:S(2)}, u32[]{:S(2)}) collective-permute-start(bf16[256,256]{1,0:T(8,128)(2,1)S(1)} %shard_map.74.own), channel_id=1, source_target_pairs={{0,8},{4,12},{8,0},{12,4},{16,24},{20,28},{24,16},{28,20},{1,9},{5... | collective-permute-start | bytes 393224 | tf_op jit(solution)/shard_map/ppermute | solution.py:333
  49.7 7.4 %collective-permute-start.13 = (bf16[256,256]{1,0:T(8,128)(2,1)S(1)}, bf16[256,256]{1,0:T(8,128)(2,1)S(1)}, u32[]{:S(2)}, u32[]{:S(2)}) collective-permute-start(bf16[256,256]{1,0:T(8,128)(2,1)S(1)} %shard_map.74.own), channel_id=1, source_target_pairs={{0,12},{4,8},{8,4},{12,0},{16,28},{20,24},{24,20},{28,16},{1,13},{... | collective-permute-start | bytes 393224 | tf_op jit(solution)/shard_map/ppermute | solution.py:333

commit v5 on v4

--- a/solution.py
+++ b/solution.py
@@ -225,9 +225,8 @@
     out[...] = a[...] + b[...]
 
 
-def round_sum_body(a, b, out):
-    rows = out.shape[0]
-    out[...] = (get_parts(a, (rows,))[0] + get_parts(b, (rows,))[0]).astype(BF16)
+def round_add_body(a, b, out):
+    out[...] = (a[...] + b[...]).astype(BF16)
 
 
 def code_sum_body(a, b, out):
@@ -260,21 +259,21 @@
     return part[pl.ds(start, size), :] + nt(masked[pl.ds(start, size), :], h[...])
 
 
-def first_send_body(masked, part, h, h_own, out, gram_out, *, away):
-    size = masked.shape[0] // 4
-    gram = nt(h[...], h[...]) + nt(h_own[...], h_own[...])
-    gram = pick(core_index(), pack(gram, 0), pack(gram, 1))
-    gram_out[...] = gram
-    put_parts(out, [piece_of(masked, part, h, quad_index() ^ away, size), gram])
-
-
-def send_body(masked, part, h, gram, out, *, away):
-    size = masked.shape[0] // 4
-    put_parts(out, [piece_of(masked, part, h, quad_index() ^ away, size), gram[...]])
+def send_body(masked, part, h, out, *, away):
+    put_parts(out, [piece_of(masked, part, h, quad_index() ^ away, masked.shape[0] // 4)])
 
 
 def keep_rows_body(masked, part, h, out):
     out[...] = piece_of(masked, part, h, quad_index(), out.shape[0])
+
+
+def gram_h_body(h, h_own, out):
+    gram = nt(h[...], h[...]) + nt(h_own[...], h_own[...])
+    out[...] = pick(core_index(), pack(gram, 0), pack(gram, 1))
+
+
+def gram_quad_body(own, one, two, three, out):
+    out[...] = ((own[...] + one[...]) + (two[...] + three[...])).astype(BF16)
 
 
 def new_h_out_body(h, h_own, out):
@@ -283,42 +282,29 @@
     out[:, pl.ds(pl.multiple_of(core * cols, cols), cols)] = h_own[...]
 
 
-def quad_sum_body(keep, own, one, two, three, *outs, pk, bit, last):
+def next_step_body(keep, *refs, bit, last):
     size = keep.shape[0]
-    rows, gram = zip(*[get_parts(ref, (size, pk)) for ref in (one, two, three)])
-    gram_own = get_parts(own, (size, pk))[1]
-    total = (keep[...] + rows[0]) + (rows[1] + rows[2])
-    store_step(total, (gram_own + gram[0]) + (gram[1] + gram[2]), outs, bit, last)
-
-
-def step_sum_body(keep, sent, got, *outs, pk, bit, last):
-    size = keep.shape[0]
-    rows, gram = get_parts(got, (size, pk))
-    store_step(keep[...] + rows, get_parts(sent, (size, pk))[1] + gram, outs, bit, last)
-
-
-def store_step(rows, gram, outs, bit, last):
+    outs = refs[-1:] if last else refs[-2:]
+    got = [get_parts(ref, (size,))[0] for ref in refs[: len(refs) - len(outs)]]
+    rows = keep[...] + got[0]
+    if len(got) > 1:
+        rows += got[1] + got[2]
     if last:
-        put_parts(outs[0], [rows, gram])
+        put_parts(outs[0], [rows])
         return
-    half = rows.shape[0] // 2
+    half = size // 2
     low, high = rows[:half], rows[half:]
     side = doc_bit(bit)
-    put_parts(outs[0], [pick(side, high, low), gram])
+    put_parts(outs[0], [pick(side, high, low)])
     outs[1][...] = pick(side, low, high)
-
-
-def gram_h_body(sent, got, out, *, size):
-    pk = out.shape[0]
-    out[...] = (get_parts(sent, (size, pk))[1] + get_parts(got, (size, pk))[1]).astype(BF16)
 
 
 def new_w_body(gram_mine, gram_other, w, sent, got, out):
     core = core_index()
     one, two = gram_mine[...], gram_other[...]
     gram = unpack(pick(core, one, two), pick(core, two, one))
-    size, pk = w.shape[0], one.shape[0]
-    total = get_parts(sent, (size, pk))[0] + get_parts(got, (size, pk))[0]
+    size = w.shape[0]
+    total = get_parts(sent, (size,))[0] + get_parts(got, (size,))[0]
     old = w[...]
     out[...] = (old.astype(F32) * total / nn(old, gram)).astype(BF16)
 
@@ -373,7 +359,7 @@
     for bit in range(1, term_bits - 1):
         g_keep = call(add_body, like(pk, k), (g_keep, g_got))
         g_got = over_term(g_keep, bit)
-    g_sum = call(code_sum_body, like(pk + TABLE, k, dtype=jnp.int16), (g_keep, g_got))
+    g_sum = call(add_body, like(pk, k), (g_keep, g_got))
     g_far = over_term(g_sum, term_bits - 1)
     n_keep, masked_own = numer(False, g_sum)
     h_old = call(half_h_body, like(k, half, dtype=BF16), (h,))
@@ -382,41 +368,45 @@
         n_got = over_term(n_keep, bit)
     n_sum = call(code_sum_body, like(k + TABLE, half, dtype=jnp.int16), (n_keep, n_got))
     n_far = over_term(n_sum, term_bits - 1)
-    g_mine = call(round_sum_body, like(pk, k, dtype=BF16), (g_sum, g_far))
+    g_mine = call(round_add_body, like(pk, k, dtype=BF16), (g_sum, g_far))
     g_other = over_term(g_mine, 0)
     h_own = call(new_h_body, like(k, half, dtype=BF16), (n_sum, n_far, g_mine, g_other, h_old))
     h_other = over_term(h_own, 0)
 
     part = call(first_w_body, like(terms, k), (masked_own, h_own), flops=flops, moved=moved)
     size = terms // 4
-    payload = lambda rows: like(rows + pk + TABLE, k, dtype=jnp.int16)
+    payload = lambda rows: like(rows + TABLE, k, dtype=jnp.int16)
     costs = dict(flops=flops // 4, moved=moved // 4)
-    sent, got = {}, {}
-    body = functools.partial(first_send_body, away=3)
-    sent[3], gram = call(body, (payload(size), like(pk, k)), (masked_other, part, h_other, h_own), **costs)
-    for away in (1, 2):
+    got = {}
+    for away in (3, 1, 2):
         body = functools.partial(send_body, away=away)
-        sent[away] = call(body, payload(size), (masked_other, part, h_other, gram), **costs)
-    for away in (3, 1, 2):
-        got[away] = over_doc(sent[away], away)
+        sent = call(body, payload(size), (masked_other, part, h_other), **costs)
+        got[away] = over_doc(sent, away)
+    gram = call(gram_h_body, like(pk, k), (h_other, h_own), **costs)
     keep = call(keep_rows_body, like(size, k), (masked_other, part, h_other), **costs)
     new_h = call(new_h_out_body, like(k, docs, dtype=BF16), (h_other, h_own))
-    ends = (sent[1], got[1], got[2], got[3])
+    args = (keep, got[1], got[2], got[3])
     for bit in range(2, bits):
         last = bit == bits - 1
-        body = quad_sum_body if bit == 2 else step_sum_body
         rows = size if last else size // 2
         outs = (payload(rows),) if last else (payload(rows), like(rows, k))
-        moving, *kept = call(functools.partial(body, pk=pk, bit=bit, last=last), outs, (keep, *ends))
-        keep, size = (kept[0] if kept else None), rows
-        ends = (moving, over_doc(moving, 1 << bit))
-    g_mine = call(functools.partial(gram_h_body, size=size), like(pk, k, dtype=BF16), ends)
-    g_other = over_term(g_mine, 0)
+        sent, *kept = call(functools.partial(next_step_body, bit=bit, last=last), outs, args)
+        arrived = over_doc(sent, 1 << bit)
+        size, args = rows, (*kept, arrived)
     start = quad_index() * (terms // 4)
     for bit in range(2, bits - 1):
         start += doc_bit(bit) * (terms // 4 >> (bit - 1))
     old = lax.dynamic_slice_in_dim(w, start, size, 0)
-    share = call(new_w_body, like(size, k, dtype=BF16), (g_mine, g_other, old, *ends))
+
+    for bit in range(2, bits):
+        gram_got = over_doc(gram, 1 << bit)
+        gram = call(add_body, like(pk, k), (gram, gram_got))
+    grams = {}
+    for away in (3, 1, 2):
+        grams[away] = over_doc(gram, away)
+    g_mine = call(gram_quad_body, like(pk, k, dtype=BF16), (gram, grams[1], grams[2], grams[3]))
+    g_other = over_term(g_mine, 0)
+    share = call(new_w_body, like(size, k, dtype=BF16), (g_mine, g_other, old, sent, arrived))
     for bit in reversed(range(2, bits - 1)):
         share = join(doc_bit(bit), share, over_doc(share, 1 << bit))
     shares = {away: over_doc(share, away) for away in (3, 1, 2)}

time: 58.1 us -> 54.7 us (0.941)
  waiting for transfers between devices: 33.7 us -> 26 us
  starting transfers between devices: 14 us -> 18.4 us
    ppermute x14 -> x18, waiting for transfers between devices: 33.7 us -> 26 us  [swap(): return lax.ppermute(x, axis, [(i, i ^ away) for i in range(size)])]
    ppermute x14 -> x18, starting transfers between devices: 14 us -> 18.4 us  [swap(): return lax.ppermute(x, axis, [(i, i ^ away) for i in range(size)])]
    pallas_call x18 -> x20, Pallas kernels: 6.83 us -> 6.7 us  [call(): pl.pallas_call(body, out_shape=out, in_specs=[HBM if i in hbm else VMEM f...]
  transfers between devices with their start and end apart: 14 -> 18, of which waited for: 12 -> 13; matrix products, arithmetic and copies ran while one was open for 2% -> 2% of each run, Pallas kernels for 5% -> 7%
where the time goes in v5:
time: 54.7 us; the launch traced here: 54.5 us
  waiting for transfers between devices  26 us (48%)
  starting transfers between devices  18.4 us (34%)
  Pallas kernels  6.7 us (12%)
  local copies, waits for them, and re-layouts  2.58 us (5%)
  between operations  0.82 us (1%)
    ppermute x18, waiting for transfers between devices, swap(): return lax.ppermute(x, axis, [(i, i ^ away) for i in range(size)])  26 us
    ppermute x18, starting transfers between devices, swap(): return lax.ppermute(x, axis, [(i, i ^ away) for i in range(size)])  18.4 us
    pallas_call x20, Pallas kernels, call(): pl.pallas_call(body, out_shape=out, in_specs=[HBM if i in hbm else VMEM f...  6.7 us
    unnamed x8, local copies, waits for them, and re-layouts  1.66 us
  transfers between devices with their start and end apart: 18, of which 13 were waited for; matrix products, arithmetic and copies ran while one was open for 2% of the time, Pallas kernels for 7%

profile of v5, /device:TPU:0, one launch (start us, length us, event | category | flops | bytes accessed | tf_op | source)
XLA Modules:
  0.0 54.5 jit_solution(16733418208857356259)
XLA Ops:
  0.7 1.2 %copy-done.2 = bf16[1024,256]{1,0:T(8,128)(2,1)S(1)} copy-done((bf16[1024,256]{1,0:T(8,128)(2,1)S(1)}, bf16[1024,256]{1,0:T(8,128)(2,1)}, u32[]{:S(2)}) %copy-start.2) | copy-done | bytes 524312
  3.9 1.6 %collective-permute-done.b = f32[96,256]{1,0:T(8,128)S(1)} collective-permute-done((f32[96,256]{1,0:T(8,128)S(1)}, f32[96,256]{1,0:T(8,128)S(1)}, u32[]{:S(2)}, u32[]{:S(2)}) %collective-permute-start) | collective-permute-done | bytes 98336 | tf_op jit(solution)/shard_map/ppermute | solution.py:319
  6.4 2.9 %collective-permute-start.2 = (s16[272,512]{1,0:T(8,128)(2,1)S(1)}, s16[272,512]{1,0:T(8,128)(2,1)S(1)}, u32[]{:S(2)}, u32[]{:S(2)}) collective-permute-start(s16[272,512]{1,0:T(8,128)(2,1)S(1)} %shard_map.63.mine), channel_id=1, source_target_pairs={{0,2},{1,3},{2,0},{3,1},{4,6},{5,7},{6,4},{7,5},{8,10},{9,11},{10,... | collective-permute-start | bytes 835592 | tf_op jit(solution)/shard_map/ppermute | solution.py:319
  9.4 9.0 %collective-permute-done.3.b = f32[96,256]{1,0:T(8,128)S(1)} collective-permute-done((f32[96,256]{1,0:T(8,128)S(1)}, f32[96,256]{1,0:T(8,128)S(1)}, u32[]{:S(2)}, u32[]{:S(2)}) %collective-permute-start.3) | collective-permute-done | bytes 98336 | tf_op jit(solution)/shard_map/ppermute | solution.py:319
  18.5 1.2 %collective-permute-done.4.gram_other = bf16[96,256]{1,0:T(8,128)(2,1)S(1)} collective-permute-done((bf16[96,256]{1,0:T(8,128)(2,1)S(1)}, bf16[96,256]{1,0:T(8,128)(2,1)S(1)}, u32[]{:S(2)}, u32[]{:S(2)}) %collective-permute-start.4) | collective-permute-done | bytes 49184 | tf_op jit(solution)/shard_map/ppermute | solution.py:319
  20.8 0.9 %collective-permute-done.5.h = bf16[256,512]{1,0:T(8,128)(2,1)S(1)} collective-permute-done((bf16[256,512]{1,0:T(8,128)(2,1)S(1)}, bf16[256,512]{1,0:T(8,128)(2,1)S(1)}, u32[]{:S(2)}, u32[]{:S(2)}) %collective-permute-start.5) | collective-permute-done | bytes 262176 | tf_op jit(solution)/shard_map/ppermute | solution.py:319
  22.1 1.8 %collective-permute-start.11 = (s16[272,256]{1,0:T(8,128)(2,1)S(1)}, s16[272,256]{1,0:T(8,128)(2,1)S(1)}, u32[]{:S(2)}, u32[]{:S(2)}) collective-permute-start(s16[272,256]{1,0:T(8,128)(2,1)S(1)} %shard_map.72), channel_id=1, source_target_pairs={{0,4},{4,0},{8,12},{12,8},{16,20},{20,16},{24,28},{28,24},{1,5},{5... | collective-permute-start | bytes 417800 | tf_op jit(solution)/shard_map/ppermute | solution.py:319
  24.2 2.6 %collective-permute-start.6 = (f32[96,256]{1,0:T(8,128)S(1)}, f32[96,256]{1,0:T(8,128)S(1)}, u32[]{:S(2)}, u32[]{:S(2)}) collective-permute-start(f32[96,256]{1,0:T(8,128)S(1)} %shard_map.67.a), channel_id=1, source_target_pairs={{0,16},{4,20},{8,24},{12,28},{16,0},{20,4},{24,8},{28,12},{1,17},{... | collective-permute-start | bytes 294920 | tf_op jit(solution)/shard_map/ppermute | solution.py:319
  27.3 1.6 %collective-permute-start.12 = (s16[272,256]{1,0:T(8,128)(2,1)S(1)}, s16[272,256]{1,0:T(8,128)(2,1)S(1)}, u32[]{:S(2)}, u32[]{:S(2)}) collective-permute-start(s16[272,256]{1,0:T(8,128)(2,1)S(1)} %shard_map.73), channel_id=1, source_target_pairs={{0,8},{4,12},{8,0},{12,4},{16,24},{20,28},{24,16},{28,20},{1,9},{5... | collective-permute-start | bytes 417800 | tf_op jit(solution)/shard_map/ppermute | solution.py:319
  29.7 2.1 %collective-permute-done.6.b = f32[96,256]{1,0:T(8,128)S(1)} collective-permute-done((f32[96,256]{1,0:T(8,128)S(1)}, f32[96,256]{1,0:T(8,128)S(1)}, u32[]{:S(2)}, u32[]{:S(2)}) %collective-permute-start.6) | collective-permute-done | bytes 98336 | tf_op jit(solution)/shard_map/ppermute | solution.py:319
  32.4 0.8 %collective-permute-start.8 = (f32[96,256]{1,0:T(8,128)S(1)}, f32[96,256]{1,0:T(8,128)S(1)}, u32[]{:S(2)}, u32[]{:S(2)}) collective-permute-start(f32[96,256]{1,0:T(8,128)S(1)} %shard_map.68.own), channel_id=1, source_target_pairs={{0,8},{4,12},{8,0},{12,4},{16,24},{20,28},{24,16},{28,20},{1,9},{5... | collective-permute-start | bytes 294920 | tf_op jit(solution)/shard_map/ppermute | solution.py:319
  33.2 2.2 %collective-permute-start.9 = (f32[96,256]{1,0:T(8,128)S(1)}, f32[96,256]{1,0:T(8,128)S(1)}, u32[]{:S(2)}, u32[]{:S(2)}) collective-permute-start(f32[96,256]{1,0:T(8,128)S(1)} %shard_map.68.own), channel_id=1, source_target_pairs={{0,12},{4,8},{8,4},{12,0},{16,28},{20,24},{24,20},{28,16},{1,13},{... | collective-permute-start | bytes 294920 | tf_op jit(solution)/shard_map/ppermute | solution.py:319
  35.7 1.5 %collective-permute-done.13.refs_2_ = s16[272,256]{1,0:T(8,128)(2,1)S(1)} collective-permute-done((s16[272,256]{1,0:T(8,128)(2,1)S(1)}, s16[272,256]{1,0:T(8,128)(2,1)S(1)}, u32[]{:S(2)}, u32[]{:S(2)}) %collective-permute-start.13) | collective-permute-done | bytes 139296 | tf_op jit(solution)/shard_map/ppermute | solution.py:319
  37.6 0.7 %collective-permute-start.14 = (s16[272,256]{1,0:T(8,128)(2,1)S(1)}, s16[272,256]{1,0:T(8,128)(2,1)S(1)}, u32[]{:S(2)}, u32[]{:S(2)}) collective-permute-start(s16[272,256]{1,0:T(8,128)(2,1)S(1)} %shard_map.75.sent), channel_id=1, source_target_pairs={{0,16},{4,20},{8,24},{12,28},{16,0},{20,4},{24,8},{28,12},{1,17},{... | collective-permute-start | bytes 417800 | tf_op jit(solution)/shard_map/ppermute | solution.py:319
  38.3 1.2 %collective-permute-done.8.two = f32[96,256]{1,0:T(8,128)S(1)} collective-permute-done((f32[96,256]{1,0:T(8,128)S(1)}, f32[96,256]{1,0:T(8,128)S(1)}, u32[]{:S(2)}, u32[]{:S(2)}) %collective-permute-start.8) | collective-permute-done | bytes 98336 | tf_op jit(solution)/shard_map/ppermute | solution.py:319
  39.5 1.7 %collective-permute-done.9.three = f32[96,256]{1,0:T(8,128)S(1)} collective-permute-done((f32[96,256]{1,0:T(8,128)S(1)}, f32[96,256]{1,0:T(8,128)S(1)}, u32[]{:S(2)}, u32[]{:S(2)}) %collective-permute-start.9) | collective-permute-done | bytes 98336 | tf_op jit(solution)/shard_map/ppermute | solution.py:319
  41.2 0.9 %constant_dynamic-slice_fusion.w = bf16[256,256]{1,0:T(8,128)(2,1)S(1)} fusion(bf16[1024,256]{1,0:T(8,128)(2,1)} %w.1, s32[]{:T(128)S(6)} %select_n.3), kind=kLoop, calls=%fused_computation | loop fusion | bytes 262148 | tf_op jit(solution)/shard_map/dynamic_slice | solution.py:399
  42.4 3.0 %collective-permute-done.14.got = s16[272,256]{1,0:T(8,128)(2,1)S(1)} collective-permute-done((s16[272,256]{1,0:T(8,128)(2,1)S(1)}, s16[272,256]{1,0:T(8,128)(2,1)S(1)}, u32[]{:S(2)}, u32[]{:S(2)}) %collective-permute-start.14) | collective-permute-done | bytes 139296 | tf_op jit(solution)/shard_map/ppermute | solution.py:319
  45.7 1.6 %collective-permute-start.15 = (bf16[256,256]{1,0:T(8,128)(2,1)S(1)}, bf16[256,256]{1,0:T(8,128)(2,1)S(1)}, u32[]{:S(2)}, u32[]{:S(2)}) collective-permute-start(bf16[256,256]{1,0:T(8,128)(2,1)S(1)} %shard_map.76.own), channel_id=1, source_target_pairs={{0,4},{4,0},{8,12},{12,8},{16,20},{20,16},{24,28},{28,24},{1,5},{5... | collective-permute-start | bytes 393224 | tf_op jit(solution)/shard_map/ppermute | solution.py:319
  47.3 1.9 %collective-permute-start.17 = (bf16[256,256]{1,0:T(8,128)(2,1)S(1)}, bf16[256,256]{1,0:T(8,128)(2,1)S(1)}, u32[]{:S(2)}, u32[]{:S(2)}) collective-permute-start(bf16[256,256]{1,0:T(8,128)(2,1)S(1)} %shard_map.76.own), channel_id=1, source_target_pairs={{0,12},{4,8},{8,4},{12,0},{16,28},{20,24},{24,20},{28,16},{1,13},{... | collective-permute-start | bytes 393224 | tf_op jit(solution)/shard_map/ppermute | solution.py:319
  49.3 0.8 %shard_map.78 = bf16[256,1024]{1,0:T(8,128)(2,1)} custom-call(bf16[256,512]{1,0:T(8,128)(2,1)S(1)} %collective-permute-done.5.h, bf16[256,512]{1,0:T(8,128)(2,1)S(1)} %shard_map.66.h_own.h), custom_call_target="tpu_custom_call" | custom-call | flops 1048576 | bytes 1048576 | tf_op jit(solution)/shard_map/pallas_call | solution.py:29
  50.1 1.7 %collective-permute-done.15.one = bf16[256,256]{1,0:T(8,128)(2,1)S(1)} collective-permute-done((bf16[256,256]{1,0:T(8,128)(2,1)S(1)}, bf16[256,256]{1,0:T(8,128)(2,1)S(1)}, u32[]{:S(2)}, u32[]{:S(2)}) %collective-permute-start.15) | collective-permute-done | bytes 131104 | tf_op jit(solution)/shard_map/ppermute | solution.py:319
  52.3 1.3 %collective-permute-done.17.three = bf16[256,256]{1,0:T(8,128)(2,1)S(1)} collective-permute-done((bf16[256,256]{1,0:T(8,128)(2,1)S(1)}, bf16[256,256]{1,0:T(8,128)(2,1)S(1)}, u32[]{:S(2)}, u32[]{:S(2)}) %collective-permute-start.17) | collective-permute-done | bytes 131104 | tf_op jit(solution)/shard_map/ppermute | solution.py:319
  53.6 0.8 %shard_map.77 = bf16[1024,256]{1,0:T(8,128)(2,1)} custom-call(bf16[256,256]{1,0:T(8,128)(2,1)S(1)} %shard_map.76.own, bf16[256,256]{1,0:T(8,128)(2,1)S(1)} %collective-permute-done.15.one, bf16[256,256]{1,0:T(8,128)(2,1)S(1)} %collective-permute-done.16.two, bf16[256,256]{1,0:T(8,128)(2,1)S(1)} %collective-permute-done.17.three), custom_call_target="tpu_custom_call" | custom-call | flops 1048576 | bytes 1048576 | tf_op jit(solution)/shard_map/pallas_call | solution.py:29
  (41 shorter events, 8.4 us)
Async XLA Ops:
  0.6 1.7 %copy-start = (bf16[1024,1024]{1,0:T(8,128)(2,1)S(1)}, bf16[1024,1024]{1,0:T(8,128)(2,1)}, u32[]{:S(2)}) copy-start(bf16[1024,1024]{1,0:T(8,128)(2,1)} %m.3) | copy-start | bytes 6291460
  0.6 1.2 %copy-start.2 = (bf16[1024,256]{1,0:T(8,128)(2,1)S(1)}, bf16[1024,256]{1,0:T(8,128)(2,1)}, u32[]{:S(2)}) copy-start(bf16[1024,256]{1,0:T(8,128)(2,1)} %w.1) | copy-start | bytes 1572868
  1.8 0.8 %copy-start.3 = (s32[8,8]{1,0:T(8,128)S(1)}, s32[8,8]{1,0:T(8,128)}, u32[]{:S(2)}) copy-start(s32[8,8]{1,0:T(8,128)} %pattern.3) | copy-start | bytes 772
  3.3 2.9 %collective-permute-start.1 = (f32[256,512]{1,0:T(8,128)S(1)}, f32[256,512]{1,0:T(8,128)S(1)}, u32[]{:S(2)}, u32[]{:S(2)}) collective-permute-start(f32[256,512]{1,0:T(8,128)S(1)} %get-tuple-element.13), channel_id=1, source_target_pairs={{0,1},{1,0},{2,3},{3,2},{4,5},{5,4},{6,7},{7,6},{8,9},{9,8},{10,11... | collective-permute-start | bytes 1572872 | tf_op jit(solution)/shard_map/ppermute | solution.py:319
  3.8 1.7 %collective-permute-start = (f32[96,256]{1,0:T(8,128)S(1)}, f32[96,256]{1,0:T(8,128)S(1)}, u32[]{:S(2)}, u32[]{:S(2)}) collective-permute-start(f32[96,256]{1,0:T(8,128)S(1)} %get-tuple-element.11), channel_id=1, source_target_pairs={{0,1},{1,0},{2,3},{3,2},{4,5},{5,4},{6,7},{7,6},{8,9},{9,8},{10,11... | collective-permute-start | bytes 294920 | tf_op jit(solution)/shard_map/ppermute | solution.py:319
  5.5 13.0 %copy-start.1 = (bf16[256,1024]{1,0:T(8,128)(2,1)S(1)}, bf16[256,1024]{1,0:T(8,128)(2,1)}, u32[]{:S(2)}) copy-start(bf16[256,1024]{1,0:T(8,128)(2,1)} %h.1) | copy-start | bytes 1572868
  6.4 13.3 %collective-permute-start.2 = (s16[272,512]{1,0:T(8,128)(2,1)S(1)}, s16[272,512]{1,0:T(8,128)(2,1)S(1)}, u32[]{:S(2)}, u32[]{:S(2)}) collective-permute-start(s16[272,512]{1,0:T(8,128)(2,1)S(1)} %shard_map.63.mine), channel_id=1, source_target_pairs={{0,2},{1,3},{2,0},{3,1},{4,6},{5,7},{6,4},{7,5},{8,10},{9,11},{10,... | collective-permute-start | bytes 835592 | tf_op jit(solution)/shard_map/ppermute | solution.py:319
  9.3 9.1 %collective-permute-start.3 = (f32[96,256]{1,0:T(8,128)S(1)}, f32[96,256]{1,0:T(8,128)S(1)}, u32[]{:S(2)}, u32[]{:S(2)}) collective-permute-start(f32[96,256]{1,0:T(8,128)S(1)} %shard_map.60.refs_0_.a), channel_id=1, source_target_pairs={{0,2},{1,3},{2,0},{3,1},{4,6},{5,7},{6,4},{7,5},{8,10},{9,11},{10,... | collective-permute-start | bytes 294920 | tf_op jit(solution)/shard_map/ppermute | solution.py:319
  18.4 1.3 %collective-permute-start.4 = (bf16[96,256]{1,0:T(8,128)(2,1)S(1)}, bf16[96,256]{1,0:T(8,128)(2,1)S(1)}, u32[]{:S(2)}, u32[]{:S(2)}) collective-permute-start(bf16[96,256]{1,0:T(8,128)(2,1)S(1)} %shard_map.64.gram_mine), channel_id=1, source_target_pairs={{0,1},{1,0},{2,3},{3,2},{4,5},{5,4},{6,7},{7,6},{8,9},{9,8},{10,11... | collective-permute-start | bytes 147464 | tf_op jit(solution)/shard_map/ppermute | solution.py:319
  20.1 1.6 %collective-permute-start.5 = (bf16[256,512]{1,0:T(8,128)(2,1)S(1)}, bf16[256,512]{1,0:T(8,128)(2,1)S(1)}, u32[]{:S(2)}, u32[]{:S(2)}) collective-permute-start(bf16[256,512]{1,0:T(8,128)(2,1)S(1)} %shard_map.66.h_own.h), channel_id=1, source_target_pairs={{0,1},{1,0},{2,3},{3,2},{4,5},{5,4},{6,7},{7,6},{8,9},{9,8},{10,11... | collective-permute-start | bytes 786440 | tf_op jit(solution)/shard_map/ppermute | solution.py:319
  22.1 11.1 %collective-permute-start.11 = (s16[272,256]{1,0:T(8,128)(2,1)S(1)}, s16[272,256]{1,0:T(8,128)(2,1)S(1)}, u32[]{:S(2)}, u32[]{:S(2)}) collective-permute-start(s16[272,256]{1,0:T(8,128)(2,1)S(1)} %shard_map.72), channel_id=1, source_target_pairs={{0,4},{4,0},{8,12},{12,8},{16,20},{20,16},{24,28},{28,24},{1,5},{5... | collective-permute-start | bytes 417800 | tf_op jit(solution)/shard_map/ppermute | solution.py:319
  24.2 7.6 %collective-permute-start.6 = (f32[96,256]{1,0:T(8,128)S(1)}, f32[96,256]{1,0:T(8,128)S(1)}, u32[]{:S(2)}, u32[]{:S(2)}) collective-permute-start(f32[96,256]{1,0:T(8,128)S(1)} %shard_map.67.a), channel_id=1, source_target_pairs={{0,16},{4,20},{8,24},{12,28},{16,0},{20,4},{24,8},{28,12},{1,17},{... | collective-permute-start | bytes 294920 | tf_op jit(solution)/shard_map/ppermute | solution.py:319
  27.3 8.4 %collective-permute-start.12 = (s16[272,256]{1,0:T(8,128)(2,1)S(1)}, s16[272,256]{1,0:T(8,128)(2,1)S(1)}, u32[]{:S(2)}, u32[]{:S(2)}) collective-permute-start(s16[272,256]{1,0:T(8,128)(2,1)S(1)} %shard_map.73), channel_id=1, source_target_pairs={{0,8},{4,12},{8,0},{12,4},{16,24},{20,28},{24,16},{28,20},{1,9},{5... | collective-permute-start | bytes 417800 | tf_op jit(solution)/shard_map/ppermute | solution.py:319
  29.3 8.0 %collective-permute-start.13 = (s16[272,256]{1,0:T(8,128)(2,1)S(1)}, s16[272,256]{1,0:T(8,128)(2,1)S(1)}, u32[]{:S(2)}, u32[]{:S(2)}) collective-permute-start(s16[272,256]{1,0:T(8,128)(2,1)S(1)} %shard_map.74), channel_id=1, source_target_pairs={{0,12},{4,8},{8,4},{12,0},{16,28},{20,24},{24,20},{28,16},{1,13},{... | collective-permute-start | bytes 417800 | tf_op jit(solution)/shard_map/ppermute | solution.py:319
  31.9 6.4 %collective-permute-start.7 = (f32[96,256]{1,0:T(8,128)S(1)}, f32[96,256]{1,0:T(8,128)S(1)}, u32[]{:S(2)}, u32[]{:S(2)}) collective-permute-start(f32[96,256]{1,0:T(8,128)S(1)} %shard_map.68.own), channel_id=1, source_target_pairs={{0,4},{4,0},{8,12},{12,8},{16,20},{20,16},{24,28},{28,24},{1,5},{5... | collective-permute-start | bytes 294920 | tf_op jit(solution)/shard_map/ppermute | solution.py:319
  32.4 7.1 %collective-permute-start.8 = (f32[96,256]{1,0:T(8,128)S(1)}, f32[96,256]{1,0:T(8,128)S(1)}, u32[]{:S(2)}, u32[]{:S(2)}) collective-permute-start(f32[96,256]{1,0:T(8,128)S(1)} %shard_map.68.own), channel_id=1, source_target_pairs={{0,8},{4,12},{8,0},{12,4},{16,24},{20,28},{24,16},{28,20},{1,9},{5... | collective-permute-start | bytes 294920 | tf_op jit(solution)/shard_map/ppermute | solution.py:319
  33.2 7.9 %collective-permute-start.9 = (f32[96,256]{1,0:T(8,128)S(1)}, f32[96,256]{1,0:T(8,128)S(1)}, u32[]{:S(2)}, u32[]{:S(2)}) collective-permute-start(f32[96,256]{1,0:T(8,128)S(1)} %shard_map.68.own), channel_id=1, source_target_pairs={{0,12},{4,8},{8,4},{12,0},{16,28},{20,24},{24,20},{28,16},{1,13},{... | collective-permute-start | bytes 294920 | tf_op jit(solution)/shard_map/ppermute | solution.py:319
  37.6 7.9 %collective-permute-start.14 = (s16[272,256]{1,0:T(8,128)(2,1)S(1)}, s16[272,256]{1,0:T(8,128)(2,1)S(1)}, u32[]{:S(2)}, u32[]{:S(2)}) collective-permute-start(s16[272,256]{1,0:T(8,128)(2,1)S(1)} %shard_map.75.sent), channel_id=1, source_target_pairs={{0,16},{4,20},{8,24},{12,28},{16,0},{20,4},{24,8},{28,12},{1,17},{... | collective-permute-start | bytes 417800 | tf_op jit(solution)/shard_map/ppermute | solution.py:319
  41.1 1.3 %collective-permute-start.10 = (bf16[96,256]{1,0:T(8,128)(2,1)S(1)}, bf16[96,256]{1,0:T(8,128)(2,1)S(1)}, u32[]{:S(2)}, u32[]{:S(2)}) collective-permute-start(bf16[96,256]{1,0:T(8,128)(2,1)S(1)} %shard_map.69.gram_mine), channel_id=1, source_target_pairs={{0,1},{1,0},{2,3},{3,2},{4,5},{5,4},{6,7},{7,6},{8,9},{9,8},{10,11... | collective-permute-start | bytes 147464 | tf_op jit(solution)/shard_map/ppermute | solution.py:319
  45.7 6.1 %collective-permute-start.15 = (bf16[256,256]{1,0:T(8,128)(2,1)S(1)}, bf16[256,256]{1,0:T(8,128)(2,1)S(1)}, u32[]{:S(2)}, u32[]{:S(2)}) collective-permute-start(bf16[256,256]{1,0:T(8,128)(2,1)S(1)} %shard_map.76.own), channel_id=1, source_target_pairs={{0,4},{4,0},{8,12},{12,8},{16,20},{20,16},{24,28},{28,24},{1,5},{5... | collective-permute-start | bytes 393224 | tf_op jit(solution)/shard_map/ppermute | solution.py:319
  47.3 5.0 %collective-permute-start.16 = (bf16[256,256]{1,0:T(8,128)(2,1)S(1)}, bf16[256,256]{1,0:T(8,128)(2,1)S(1)}, u32[]{:S(2)}, u32[]{:S(2)}) collective-permute-start(bf16[256,256]{1,0:T(8,128)(2,1)S(1)} %shard_map.76.own), channel_id=1, source_target_pairs={{0,8},{4,12},{8,0},{12,4},{16,24},{20,28},{24,16},{28,20},{1,9},{5... | collective-permute-start | bytes 393224 | tf_op jit(solution)/shard_map/ppermute | solution.py:319
  47.3 6.3 %collective-permute-start.17 = (bf16[256,256]{1,0:T(8,128)(2,1)S(1)}, bf16[256,256]{1,0:T(8,128)(2,1)S(1)}, u32[]{:S(2)}, u32[]{:S(2)}) collective-permute-start(bf16[256,256]{1,0:T(8,128)(2,1)S(1)} %shard_map.76.own), channel_id=1, source_target_pairs={{0,12},{4,8},{8,4},{12,0},{16,28},{20,24},{24,20},{28,16},{1,13},{... | collective-permute-start | bytes 393224 | tf_op jit(solution)/shard_map/ppermute | solution.py:319

commit v6 on v5

--- a/solution.py
+++ b/solution.py
@@ -124,6 +124,10 @@
 
 def core_index():
     return lax.axis_index("term") & 1
+
+
+def term_bit(bit):
+    return (lax.axis_index("term") >> bit) & 1
 
 
 def quad_index():
@@ -267,9 +271,19 @@
     out[...] = piece_of(masked, part, h, quad_index(), out.shape[0])
 
 
-def gram_h_body(h, h_own, out):
+def gram_h_body(h, h_own, out, *, side_bit):
     gram = nt(h[...], h[...]) + nt(h_own[...], h_own[...])
-    out[...] = pick(core_index(), pack(gram, 0), pack(gram, 1))
+    part = pick(core_index(), pack(gram, 0), pack(gram, 1))
+    rows = out.shape[0]
+    out[...] = pick(term_bit(side_bit), part[:rows], part[rows:])
+
+
+def join_body(mine, other, out, *, side_bit):
+    rows = mine.shape[0]
+    a, b = mine[...], other[...]
+    side = term_bit(side_bit)
+    out[:rows, :] = pick(side, a, b)
+    out[rows:, :] = pick(side, b, a)
 
 
 def gram_quad_body(own, one, two, three, out):
@@ -299,20 +313,22 @@
     outs[1][...] = pick(side, low, high)
 
 
-def new_w_body(gram_mine, gram_other, w, sent, got, out):
+def total_body(sent, got, out):
+    size = sent.shape[0] - TABLE
+    put_parts(out.at[0], [get_parts(sent, (size,))[0] + get_parts(got, (size,))[0]])
+
+
+def new_w_body(gram_mine, gram_other, w, own, one, two, three, out):
     core = core_index()
-    one, two = gram_mine[...], gram_other[...]
-    gram = unpack(pick(core, one, two), pick(core, two, one))
-    size = w.shape[0]
-    total = get_parts(sent, (size,))[0] + get_parts(got, (size,))[0]
-    old = w[...]
-    out[...] = (old.astype(F32) * total / nn(old, gram)).astype(BF16)
-
-
-def new_w_out_body(own, one, two, three, out):
-    size = own.shape[0]
+    a, b = gram_mine[...], gram_other[...]
+    gram = unpack(pick(core, a, b), pick(core, b, a))
+    pieces, size = own.shape[0], own.shape[1] - TABLE
     for away, ref in enumerate((own, one, two, three)):
-        out[pl.ds(pl.multiple_of((quad_index() ^ away) * size, size), size), :] = ref[...]
+        for i in range(pieces):
+            start = pl.multiple_of(((quad_index() ^ away) * pieces + i) * size, size)
+            old = w[pl.ds(start, size), :]
+            total = get_parts(ref.at[i], (size,))[0]
+            out[pl.ds(start, size), :] = (old.astype(F32) * total / nn(old, gram)).astype(BF16)
 
 
 def swap(x, axis, size, away):
@@ -382,7 +398,8 @@
         body = functools.partial(send_body, away=away)
         sent = call(body, payload(size), (masked_other, part, h_other), **costs)
         got[away] = over_doc(sent, away)
-    gram = call(gram_h_body, like(pk, k), (h_other, h_own), **costs)
+    body = functools.partial(gram_h_body, side_bit=term_bits - 1)
+    gram = call(body, like(pk // 2, k), (h_other, h_own), **costs)
     keep = call(keep_rows_body, like(size, k), (masked_other, part, h_other), **costs)
     new_h = call(new_h_out_body, like(k, docs, dtype=BF16), (h_other, h_own))
     args = (keep, got[1], got[2], got[3])
@@ -393,24 +410,26 @@
         sent, *kept = call(functools.partial(next_step_body, bit=bit, last=last), outs, args)
         arrived = over_doc(sent, 1 << bit)
         size, args = rows, (*kept, arrived)
-    start = quad_index() * (terms // 4)
-    for bit in range(2, bits - 1):
-        start += doc_bit(bit) * (terms // 4 >> (bit - 1))
-    old = lax.dynamic_slice_in_dim(w, start, size, 0)
+    share = call(total_body, like(1, size + TABLE, k, dtype=jnp.int16), (sent, arrived))
+    for bit in reversed(range(2, bits - 1)):
+        share = join(doc_bit(bit), share, over_doc(share, 1 << bit))
+    shares = {}
+    for away in (3, 1, 2):
+        shares[away] = over_doc(share, away)
 
     for bit in range(2, bits):
         gram_got = over_doc(gram, 1 << bit)
-        gram = call(add_body, like(pk, k), (gram, gram_got))
+        gram = call(add_body, like(pk // 2, k), (gram, gram_got))
     grams = {}
     for away in (3, 1, 2):
         grams[away] = over_doc(gram, away)
-    g_mine = call(gram_quad_body, like(pk, k, dtype=BF16), (gram, grams[1], grams[2], grams[3]))
+    g_half = call(gram_quad_body, like(pk // 2, k, dtype=BF16), (gram, grams[1], grams[2], grams[3]))
+    g_far = over_term(g_half, term_bits - 1)
+    body = functools.partial(join_body, side_bit=term_bits - 1)
+    g_mine = call(body, like(pk, k, dtype=BF16), (g_half, g_far))
     g_other = over_term(g_mine, 0)
-    share = call(new_w_body, like(size, k, dtype=BF16), (g_mine, g_other, old, sent, arrived))
-    for bit in reversed(range(2, bits - 1)):
-        share = join(doc_bit(bit), share, over_doc(share, 1 << bit))
-    shares = {away: over_doc(share, away) for away in (3, 1, 2)}
-    new_w = call(new_w_out_body, like(terms, k, dtype=BF16), (share, shares[1], shares[2], shares[3]))
+    ends = (share, shares[1], shares[2], shares[3])
+    new_w = call(new_w_body, like(terms, k, dtype=BF16), (g_mine, g_other, w, *ends), flops=flops // 4)
     return new_w, new_h
 
 

time: 54.7 us -> 62.9 us (1.15)
  waiting for transfers between devices: 26 us -> 33.6 us
  starting transfers between devices: 18.4 us -> 19.5 us
  local copies, waits for them, and re-layouts: 2.58 us -> 1.67 us
    ppermute x18 -> x19, waiting for transfers between devices: 26 us -> 33.6 us  [swap(): return lax.ppermute(x, axis, [(i, i ^ away) for i in range(size)])]
    ppermute x18 -> x19, starting transfers between devices: 18.4 us -> 19.5 us  [swap(): return lax.ppermute(x, axis, [(i, i ^ away) for i in range(size)])]
    dynamic_slice x1 -> x0, local copies, waits for them, and re-layouts: 0.92 us -> none  [update(): old = lax.dynamic_slice_in_dim(w, start, size, 0)]
    pallas_call x20 -> x21, Pallas kernels: 6.7 us -> 7.14 us  [call(): pl.pallas_call(body, out_shape=out, in_specs=[HBM if i in hbm else VMEM f...]
    unnamed x8 -> x10, local copies, waits for them, and re-layouts: 1.66 us -> 1.67 us
  transfers between devices with their start and end apart: 18 -> 19, of which waited for: 13 -> 12; matrix products, arithmetic and copies ran while one was open for 2% -> 0% of each run, Pallas kernels for 7% -> 6%
where the time goes in v6:
time: 62.9 us; the launch traced here: 62.7 us
  waiting for transfers between devices  33.6 us (53%)
  starting transfers between devices  19.5 us (31%)
  Pallas kernels  7.14 us (11%)
  local copies, waits for them, and re-layouts  1.67 us (3%)
  between operations  0.83 us (1%)
    ppermute x19, waiting for transfers between devices, swap(): return lax.ppermute(x, axis, [(i, i ^ away) for i in range(size)])  33.6 us
    ppermute x19, starting transfers between devices, swap(): return lax.ppermute(x, axis, [(i, i ^ away) for i in range(size)])  19.5 us
    pallas_call x21, Pallas kernels, call(): pl.pallas_call(body, out_shape=out, in_specs=[HBM if i in hbm else VMEM f...  7.14 us
    unnamed x10, local copies, waits for them, and re-layouts  1.67 us
  transfers between devices with their start and end apart: 19, of which 12 were waited for; matrix products, arithmetic and copies ran while one was open for 0% of the time, Pallas kernels for 6%

profile of v6, /device:TPU:0, one launch (start us, length us, event | category | flops | bytes accessed | tf_op | source)
XLA Modules:
  0.0 62.7 jit_solution(18298760192401792557)
XLA Ops:
  0.7 1.2 %copy-done.2 = bf16[1024,256]{1,0:T(8,128)(2,1)S(1)} copy-done((bf16[1024,256]{1,0:T(8,128)(2,1)S(1)}, bf16[1024,256]{1,0:T(8,128)(2,1)}, u32[]{:S(2)}) %copy-start.2) | copy-done | bytes 524312
  3.9 1.6 %collective-permute-done.b = f32[96,256]{1,0:T(8,128)S(1)} collective-permute-done((f32[96,256]{1,0:T(8,128)S(1)}, f32[96,256]{1,0:T(8,128)S(1)}, u32[]{:S(2)}, u32[]{:S(2)}) %collective-permute-start) | collective-permute-done | bytes 98336 | tf_op jit(solution)/shard_map/ppermute | solution.py:335
  6.4 2.9 %collective-permute-start.2 = (s16[272,512]{1,0:T(8,128)(2,1)S(1)}, s16[272,512]{1,0:T(8,128)(2,1)S(1)}, u32[]{:S(2)}, u32[]{:S(2)}) collective-permute-start(s16[272,512]{1,0:T(8,128)(2,1)S(1)} %shard_map.63.mine), channel_id=1, source_target_pairs={{0,2},{1,3},{2,0},{3,1},{4,6},{5,7},{6,4},{7,5},{8,10},{9,11},{10,... | collective-permute-start | bytes 835592 | tf_op jit(solution)/shard_map/ppermute | solution.py:335
  9.4 9.0 %collective-permute-done.3.b = f32[96,256]{1,0:T(8,128)S(1)} collective-permute-done((f32[96,256]{1,0:T(8,128)S(1)}, f32[96,256]{1,0:T(8,128)S(1)}, u32[]{:S(2)}, u32[]{:S(2)}) %collective-permute-start.3) | collective-permute-done | bytes 98336 | tf_op jit(solution)/shard_map/ppermute | solution.py:335
  18.5 1.2 %collective-permute-done.4.gram_other = bf16[96,256]{1,0:T(8,128)(2,1)S(1)} collective-permute-done((bf16[96,256]{1,0:T(8,128)(2,1)S(1)}, bf16[96,256]{1,0:T(8,128)(2,1)S(1)}, u32[]{:S(2)}, u32[]{:S(2)}) %collective-permute-start.4) | collective-permute-done | bytes 49184 | tf_op jit(solution)/shard_map/ppermute | solution.py:335
  20.8 0.9 %collective-permute-done.5.h = bf16[256,512]{1,0:T(8,128)(2,1)S(1)} collective-permute-done((bf16[256,512]{1,0:T(8,128)(2,1)S(1)}, bf16[256,512]{1,0:T(8,128)(2,1)S(1)}, u32[]{:S(2)}, u32[]{:S(2)}) %collective-permute-start.5) | collective-permute-done | bytes 262176 | tf_op jit(solution)/shard_map/ppermute | solution.py:335
  22.1 1.8 %collective-permute-start.12 = (s16[272,256]{1,0:T(8,128)(2,1)S(1)}, s16[272,256]{1,0:T(8,128)(2,1)S(1)}, u32[]{:S(2)}, u32[]{:S(2)}) collective-permute-start(s16[272,256]{1,0:T(8,128)(2,1)S(1)} %shard_map.73), channel_id=1, source_target_pairs={{0,4},{4,0},{8,12},{12,8},{16,20},{20,16},{24,28},{28,24},{1,5},{5... | collective-permute-start | bytes 417800 | tf_op jit(solution)/shard_map/ppermute | solution.py:335
  24.3 1.6 %collective-permute-start.13 = (s16[272,256]{1,0:T(8,128)(2,1)S(1)}, s16[272,256]{1,0:T(8,128)(2,1)S(1)}, u32[]{:S(2)}, u32[]{:S(2)}) collective-permute-start(s16[272,256]{1,0:T(8,128)(2,1)S(1)} %shard_map.74), channel_id=1, source_target_pairs={{0,8},{4,12},{8,0},{12,4},{16,24},{20,28},{24,16},{28,20},{1,9},{5... | collective-permute-start | bytes 417800 | tf_op jit(solution)/shard_map/ppermute | solution.py:335
  26.8 1.1 %collective-permute-done.12.refs_0_ = s16[272,256]{1,0:T(8,128)(2,1)S(1)} collective-permute-done((s16[272,256]{1,0:T(8,128)(2,1)S(1)}, s16[272,256]{1,0:T(8,128)(2,1)S(1)}, u32[]{:S(2)}, u32[]{:S(2)}) %collective-permute-start.12) | collective-permute-done | bytes 139296 | tf_op jit(solution)/shard_map/ppermute | solution.py:335
  27.9 3.0 %collective-permute-done.13.refs_1_ = s16[272,256]{1,0:T(8,128)(2,1)S(1)} collective-permute-done((s16[272,256]{1,0:T(8,128)(2,1)S(1)}, s16[272,256]{1,0:T(8,128)(2,1)S(1)}, u32[]{:S(2)}, u32[]{:S(2)}) %collective-permute-start.13) | collective-permute-done | bytes 139296 | tf_op jit(solution)/shard_map/ppermute | solution.py:335
  30.9 1.7 %collective-permute-done.14.refs_2_ = s16[272,256]{1,0:T(8,128)(2,1)S(1)} collective-permute-done((s16[272,256]{1,0:T(8,128)(2,1)S(1)}, s16[272,256]{1,0:T(8,128)(2,1)S(1)}, u32[]{:S(2)}, u32[]{:S(2)}) %collective-permute-start.14) | collective-permute-done | bytes 139296 | tf_op jit(solution)/shard_map/ppermute | solution.py:335
  32.9 2.8 %collective-permute-start.15 = (s16[272,256]{1,0:T(8,128)(2,1)S(1)}, s16[272,256]{1,0:T(8,128)(2,1)S(1)}, u32[]{:S(2)}, u32[]{:S(2)}) collective-permute-start(s16[272,256]{1,0:T(8,128)(2,1)S(1)} %shard_map.76.sent), channel_id=1, source_target_pairs={{0,16},{4,20},{8,24},{12,28},{16,0},{20,4},{24,8},{28,12},{1,17},{... | collective-permute-start | bytes 417800 | tf_op jit(solution)/shard_map/ppermute | solution.py:335
  36.3 7.4 %collective-permute-done.6.b = f32[48,256]{1,0:T(8,128)S(1)} collective-permute-done((f32[48,256]{1,0:T(8,128)S(1)}, f32[48,256]{1,0:T(8,128)S(1)}, u32[]{:S(2)}, u32[]{:S(2)}) %collective-permute-start.6) | collective-permute-done | bytes 49184 | tf_op jit(solution)/shard_map/ppermute | solution.py:335
  43.7 1.6 %collective-permute-start.7 = (f32[48,256]{1,0:T(8,128)S(1)}, f32[48,256]{1,0:T(8,128)S(1)}, u32[]{:S(2)}, u32[]{:S(2)}) collective-permute-start(f32[48,256]{1,0:T(8,128)S(1)} %shard_map.68.own), channel_id=1, source_target_pairs={{0,4},{4,0},{8,12},{12,8},{16,20},{20,16},{24,28},{28,24},{1,5},{5... | collective-permute-start | bytes 147464 | tf_op jit(solution)/shard_map/ppermute | solution.py:335
  46.1 0.7 %collective-permute-start.17 = (s16[1,272,256]{2,1,0:T(8,128)(2,1)S(1)}, s16[1,272,256]{2,1,0:T(8,128)(2,1)S(1)}, u32[]{:S(2)}, u32[]{:S(2)}) collective-permute-start(s16[1,272,256]{2,1,0:T(8,128)(2,1)S(1)} %shard_map.77.own), channel_id=1, source_target_pairs={{0,8},{4,12},{8,0},{12,4},{16,24},{20,28},{24,16},{28,20},{1,9},{5... | collective-permute-start | bytes 417800 | tf_op jit(solution)/shard_map/ppermute | solution.py:335
  46.7 2.3 %collective-permute-start.18 = (s16[1,272,256]{2,1,0:T(8,128)(2,1)S(1)}, s16[1,272,256]{2,1,0:T(8,128)(2,1)S(1)}, u32[]{:S(2)}, u32[]{:S(2)}) collective-permute-start(s16[1,272,256]{2,1,0:T(8,128)(2,1)S(1)} %shard_map.77.own), channel_id=1, source_target_pairs={{0,12},{4,8},{8,4},{12,0},{16,28},{20,24},{24,20},{28,16},{1,13},{... | collective-permute-start | bytes 417800 | tf_op jit(solution)/shard_map/ppermute | solution.py:335
  49.1 0.6 %collective-permute-start.8 = (f32[48,256]{1,0:T(8,128)S(1)}, f32[48,256]{1,0:T(8,128)S(1)}, u32[]{:S(2)}, u32[]{:S(2)}) collective-permute-start(f32[48,256]{1,0:T(8,128)S(1)} %shard_map.68.own), channel_id=1, source_target_pairs={{0,8},{4,12},{8,0},{12,4},{16,24},{20,28},{24,16},{28,20},{1,9},{5... | collective-permute-start | bytes 147464 | tf_op jit(solution)/shard_map/ppermute | solution.py:335
  49.7 1.3 %collective-permute-start.9 = (f32[48,256]{1,0:T(8,128)S(1)}, f32[48,256]{1,0:T(8,128)S(1)}, u32[]{:S(2)}, u32[]{:S(2)}) collective-permute-start(f32[48,256]{1,0:T(8,128)S(1)} %shard_map.68.own), channel_id=1, source_target_pairs={{0,12},{4,8},{8,4},{12,0},{16,28},{20,24},{24,20},{28,16},{1,13},{... | collective-permute-start | bytes 147464 | tf_op jit(solution)/shard_map/ppermute | solution.py:335
  51.0 4.5 %collective-permute-done.8.two = f32[48,256]{1,0:T(8,128)S(1)} collective-permute-done((f32[48,256]{1,0:T(8,128)S(1)}, f32[48,256]{1,0:T(8,128)S(1)}, u32[]{:S(2)}, u32[]{:S(2)}) %collective-permute-start.8) | collective-permute-done | bytes 49184 | tf_op jit(solution)/shard_map/ppermute | solution.py:335
  55.5 0.7 %collective-permute-done.9.three = f32[48,256]{1,0:T(8,128)S(1)} collective-permute-done((f32[48,256]{1,0:T(8,128)S(1)}, f32[48,256]{1,0:T(8,128)S(1)}, u32[]{:S(2)}, u32[]{:S(2)}) %collective-permute-start.9) | collective-permute-done | bytes 49184 | tf_op jit(solution)/shard_map/ppermute | solution.py:335
  56.2 1.6 %collective-permute-start.10 = (bf16[48,256]{1,0:T(8,128)(2,1)S(1)}, bf16[48,256]{1,0:T(8,128)(2,1)S(1)}, u32[]{:S(2)}, u32[]{:S(2)}) collective-permute-start(bf16[48,256]{1,0:T(8,128)(2,1)S(1)} %shard_map.69.mine), channel_id=1, source_target_pairs={{0,2},{1,3},{2,0},{3,1},{4,6},{5,7},{6,4},{7,5},{8,10},{9,11},{10,... | collective-permute-start | bytes 73736 | tf_op jit(solution)/shard_map/ppermute | solution.py:335
  57.8 2.3 %collective-permute-done.10.other = bf16[48,256]{1,0:T(8,128)(2,1)S(1)} collective-permute-done((bf16[48,256]{1,0:T(8,128)(2,1)S(1)}, bf16[48,256]{1,0:T(8,128)(2,1)S(1)}, u32[]{:S(2)}, u32[]{:S(2)}) %collective-permute-start.10) | collective-permute-done | bytes 24608 | tf_op jit(solution)/shard_map/ppermute | solution.py:335
  60.2 0.8 %shard_map.79 = bf16[256,1024]{1,0:T(8,128)(2,1)} custom-call(bf16[256,512]{1,0:T(8,128)(2,1)S(1)} %collective-permute-done.5.h, bf16[256,512]{1,0:T(8,128)(2,1)S(1)} %shard_map.66.h_own.h), custom_call_target="tpu_custom_call" | custom-call | flops 1048576 | bytes 1048576 | tf_op jit(solution)/shard_map/pallas_call | solution.py:29
  61.4 1.3 %shard_map.78 = bf16[1024,256]{1,0:T(8,128)(2,1)} custom-call(bf16[96,256]{1,0:T(8,128)(2,1)S(1)} %shard_map.70.gram_mine, bf16[96,256]{1,0:T(8,128)(2,1)S(1)} %collective-permute-done.11.gram_other, bf16[1024,256]{1,0:T(8,128)(2,1)S(1)} %copy-done.3, s16[1,272,256]{2,1,0:T(8,128)(2,1)S(1)} %shard_map.77.own, ...), custom_call_target="tpu_custom_call" | custom-call | flops 67108864 | bytes 1048576 | tf_op jit(solution)/shard_map/pallas_call | solution.py:29
  (45 shorter events, 8.0 us)
Async XLA Ops:
  0.6 1.7 %copy-start = (bf16[1024,1024]{1,0:T(8,128)(2,1)S(1)}, bf16[1024,1024]{1,0:T(8,128)(2,1)}, u32[]{:S(2)}) copy-start(bf16[1024,1024]{1,0:T(8,128)(2,1)} %m.3) | copy-start | bytes 6291460
  0.6 1.2 %copy-start.2 = (bf16[1024,256]{1,0:T(8,128)(2,1)S(1)}, bf16[1024,256]{1,0:T(8,128)(2,1)}, u32[]{:S(2)}) copy-start(bf16[1024,256]{1,0:T(8,128)(2,1)} %w.3) | copy-start | bytes 1572868
  1.8 0.8 %copy-start.4 = (s32[8,8]{1,0:T(8,128)S(1)}, s32[8,8]{1,0:T(8,128)}, u32[]{:S(2)}) copy-start(s32[8,8]{1,0:T(8,128)} %pattern.3) | copy-start | bytes 772
  3.3 2.9 %collective-permute-start.1 = (f32[256,512]{1,0:T(8,128)S(1)}, f32[256,512]{1,0:T(8,128)S(1)}, u32[]{:S(2)}, u32[]{:S(2)}) collective-permute-start(f32[256,512]{1,0:T(8,128)S(1)} %get-tuple-element.13), channel_id=1, source_target_pairs={{0,1},{1,0},{2,3},{3,2},{4,5},{5,4},{6,7},{7,6},{8,9},{9,8},{10,11... | collective-permute-start | bytes 1572872 | tf_op jit(solution)/shard_map/ppermute | solution.py:335
  3.8 1.7 %collective-permute-start = (f32[96,256]{1,0:T(8,128)S(1)}, f32[96,256]{1,0:T(8,128)S(1)}, u32[]{:S(2)}, u32[]{:S(2)}) collective-permute-start(f32[96,256]{1,0:T(8,128)S(1)} %get-tuple-element.11), channel_id=1, source_target_pairs={{0,1},{1,0},{2,3},{3,2},{4,5},{5,4},{6,7},{7,6},{8,9},{9,8},{10,11... | collective-permute-start | bytes 294920 | tf_op jit(solution)/shard_map/ppermute | solution.py:335
  5.5 13.0 %copy-start.1 = (bf16[256,1024]{1,0:T(8,128)(2,1)S(1)}, bf16[256,1024]{1,0:T(8,128)(2,1)}, u32[]{:S(2)}) copy-start(bf16[256,1024]{1,0:T(8,128)(2,1)} %h.1) | copy-start | bytes 1572868
  6.4 13.3 %collective-permute-start.2 = (s16[272,512]{1,0:T(8,128)(2,1)S(1)}, s16[272,512]{1,0:T(8,128)(2,1)S(1)}, u32[]{:S(2)}, u32[]{:S(2)}) collective-permute-start(s16[272,512]{1,0:T(8,128)(2,1)S(1)} %shard_map.63.mine), channel_id=1, source_target_pairs={{0,2},{1,3},{2,0},{3,1},{4,6},{5,7},{6,4},{7,5},{8,10},{9,11},{10,... | collective-permute-start | bytes 835592 | tf_op jit(solution)/shard_map/ppermute | solution.py:335
  9.3 9.1 %collective-permute-start.3 = (f32[96,256]{1,0:T(8,128)S(1)}, f32[96,256]{1,0:T(8,128)S(1)}, u32[]{:S(2)}, u32[]{:S(2)}) collective-permute-start(f32[96,256]{1,0:T(8,128)S(1)} %shard_map.60.refs_0_.a), channel_id=1, source_target_pairs={{0,2},{1,3},{2,0},{3,1},{4,6},{5,7},{6,4},{7,5},{8,10},{9,11},{10,... | collective-permute-start | bytes 294920 | tf_op jit(solution)/shard_map/ppermute | solution.py:335
  18.4 1.3 %collective-permute-start.4 = (bf16[96,256]{1,0:T(8,128)(2,1)S(1)}, bf16[96,256]{1,0:T(8,128)(2,1)S(1)}, u32[]{:S(2)}, u32[]{:S(2)}) collective-permute-start(bf16[96,256]{1,0:T(8,128)(2,1)S(1)} %shard_map.64.gram_mine), channel_id=1, source_target_pairs={{0,1},{1,0},{2,3},{3,2},{4,5},{5,4},{6,7},{7,6},{8,9},{9,8},{10,11... | collective-permute-start | bytes 147464 | tf_op jit(solution)/shard_map/ppermute | solution.py:335
  20.1 1.6 %collective-permute-start.5 = (bf16[256,512]{1,0:T(8,128)(2,1)S(1)}, bf16[256,512]{1,0:T(8,128)(2,1)S(1)}, u32[]{:S(2)}, u32[]{:S(2)}) collective-permute-start(bf16[256,512]{1,0:T(8,128)(2,1)S(1)} %shard_map.66.h_own.h), channel_id=1, source_target_pairs={{0,1},{1,0},{2,3},{3,2},{4,5},{5,4},{6,7},{7,6},{8,9},{9,8},{10,11... | collective-permute-start | bytes 786440 | tf_op jit(solution)/shard_map/ppermute | solution.py:335
  22.1 5.8 %collective-permute-start.12 = (s16[272,256]{1,0:T(8,128)(2,1)S(1)}, s16[272,256]{1,0:T(8,128)(2,1)S(1)}, u32[]{:S(2)}, u32[]{:S(2)}) collective-permute-start(s16[272,256]{1,0:T(8,128)(2,1)S(1)} %shard_map.73), channel_id=1, source_target_pairs={{0,4},{4,0},{8,12},{12,8},{16,20},{20,16},{24,28},{28,24},{1,5},{5... | collective-permute-start | bytes 417800 | tf_op jit(solution)/shard_map/ppermute | solution.py:335
  24.3 6.6 %collective-permute-start.13 = (s16[272,256]{1,0:T(8,128)(2,1)S(1)}, s16[272,256]{1,0:T(8,128)(2,1)S(1)}, u32[]{:S(2)}, u32[]{:S(2)}) collective-permute-start(s16[272,256]{1,0:T(8,128)(2,1)S(1)} %shard_map.74), channel_id=1, source_target_pairs={{0,8},{4,12},{8,0},{12,4},{16,24},{20,28},{24,16},{28,20},{1,9},{5... | collective-permute-start | bytes 417800 | tf_op jit(solution)/shard_map/ppermute | solution.py:335
  26.3 6.3 %collective-permute-start.14 = (s16[272,256]{1,0:T(8,128)(2,1)S(1)}, s16[272,256]{1,0:T(8,128)(2,1)S(1)}, u32[]{:S(2)}, u32[]{:S(2)}) collective-permute-start(s16[272,256]{1,0:T(8,128)(2,1)S(1)} %shard_map.75), channel_id=1, source_target_pairs={{0,12},{4,8},{8,4},{12,0},{16,28},{20,24},{24,20},{28,16},{1,13},{... | collective-permute-start | bytes 417800 | tf_op jit(solution)/shard_map/ppermute | solution.py:335
  26.8 34.6 %copy-start.3 = (bf16[1024,256]{1,0:T(8,128)(2,1)S(1)}, bf16[1024,256]{1,0:T(8,128)(2,1)}, u32[]{:S(2)}) copy-start(bf16[1024,256]{1,0:T(8,128)(2,1)} %w.3) | copy-start | bytes 1572868
  32.9 12.4 %collective-permute-start.15 = (s16[272,256]{1,0:T(8,128)(2,1)S(1)}, s16[272,256]{1,0:T(8,128)(2,1)S(1)}, u32[]{:S(2)}, u32[]{:S(2)}) collective-permute-start(s16[272,256]{1,0:T(8,128)(2,1)S(1)} %shard_map.76.sent), channel_id=1, source_target_pairs={{0,16},{4,20},{8,24},{12,28},{16,0},{20,4},{24,8},{28,12},{1,17},{... | collective-permute-start | bytes 417800 | tf_op jit(solution)/shard_map/ppermute | solution.py:335
  36.0 7.6 %collective-permute-start.6 = (f32[48,256]{1,0:T(8,128)S(1)}, f32[48,256]{1,0:T(8,128)S(1)}, u32[]{:S(2)}, u32[]{:S(2)}) collective-permute-start(f32[48,256]{1,0:T(8,128)S(1)} %shard_map.67.a), channel_id=1, source_target_pairs={{0,16},{4,20},{8,24},{12,28},{16,0},{20,4},{24,8},{28,12},{1,17},{... | collective-permute-start | bytes 147464 | tf_op jit(solution)/shard_map/ppermute | solution.py:335
  43.7 6.0 %collective-permute-start.7 = (f32[48,256]{1,0:T(8,128)S(1)}, f32[48,256]{1,0:T(8,128)S(1)}, u32[]{:S(2)}, u32[]{:S(2)}) collective-permute-start(f32[48,256]{1,0:T(8,128)S(1)} %shard_map.68.own), channel_id=1, source_target_pairs={{0,4},{4,0},{8,12},{12,8},{16,20},{20,16},{24,28},{28,24},{1,5},{5... | collective-permute-start | bytes 147464 | tf_op jit(solution)/shard_map/ppermute | solution.py:335
  45.5 15.9 %collective-permute-start.16 = (s16[1,272,256]{2,1,0:T(8,128)(2,1)S(1)}, s16[1,272,256]{2,1,0:T(8,128)(2,1)S(1)}, u32[]{:S(2)}, u32[]{:S(2)}) collective-permute-start(s16[1,272,256]{2,1,0:T(8,128)(2,1)S(1)} %shard_map.77.own), channel_id=1, source_target_pairs={{0,4},{4,0},{8,12},{12,8},{16,20},{20,16},{24,28},{28,24},{1,5},{5... | collective-permute-start | bytes 417800 | tf_op jit(solution)/shard_map/ppermute | solution.py:335
  46.1 15.3 %collective-permute-start.17 = (s16[1,272,256]{2,1,0:T(8,128)(2,1)S(1)}, s16[1,272,256]{2,1,0:T(8,128)(2,1)S(1)}, u32[]{:S(2)}, u32[]{:S(2)}) collective-permute-start(s16[1,272,256]{2,1,0:T(8,128)(2,1)S(1)} %shard_map.77.own), channel_id=1, source_target_pairs={{0,8},{4,12},{8,0},{12,4},{16,24},{20,28},{24,16},{28,20},{1,9},{5... | collective-permute-start | bytes 417800 | tf_op jit(solution)/shard_map/ppermute | solution.py:335
  46.7 14.6 %collective-permute-start.18 = (s16[1,272,256]{2,1,0:T(8,128)(2,1)S(1)}, s16[1,272,256]{2,1,0:T(8,128)(2,1)S(1)}, u32[]{:S(2)}, u32[]{:S(2)}) collective-permute-start(s16[1,272,256]{2,1,0:T(8,128)(2,1)S(1)} %shard_map.77.own), channel_id=1, source_target_pairs={{0,12},{4,8},{8,4},{12,0},{16,28},{20,24},{24,20},{28,16},{1,13},{... | collective-permute-start | bytes 417800 | tf_op jit(solution)/shard_map/ppermute | solution.py:335
  49.1 6.4 %collective-permute-start.8 = (f32[48,256]{1,0:T(8,128)S(1)}, f32[48,256]{1,0:T(8,128)S(1)}, u32[]{:S(2)}, u32[]{:S(2)}) collective-permute-start(f32[48,256]{1,0:T(8,128)S(1)} %shard_map.68.own), channel_id=1, source_target_pairs={{0,8},{4,12},{8,0},{12,4},{16,24},{20,28},{24,16},{28,20},{1,9},{5... | collective-permute-start | bytes 147464 | tf_op jit(solution)/shard_map/ppermute | solution.py:335
  49.7 6.5 %collective-permute-start.9 = (f32[48,256]{1,0:T(8,128)S(1)}, f32[48,256]{1,0:T(8,128)S(1)}, u32[]{:S(2)}, u32[]{:S(2)}) collective-permute-start(f32[48,256]{1,0:T(8,128)S(1)} %shard_map.68.own), channel_id=1, source_target_pairs={{0,12},{4,8},{8,4},{12,0},{16,28},{20,24},{24,20},{28,16},{1,13},{... | collective-permute-start | bytes 147464 | tf_op jit(solution)/shard_map/ppermute | solution.py:335
  56.2 3.9 %collective-permute-start.10 = (bf16[48,256]{1,0:T(8,128)(2,1)S(1)}, bf16[48,256]{1,0:T(8,128)(2,1)S(1)}, u32[]{:S(2)}, u32[]{:S(2)}) collective-permute-start(bf16[48,256]{1,0:T(8,128)(2,1)S(1)} %shard_map.69.mine), channel_id=1, source_target_pairs={{0,2},{1,3},{2,0},{3,1},{4,6},{5,7},{6,4},{7,5},{8,10},{9,11},{10,... | collective-permute-start | bytes 73736 | tf_op jit(solution)/shard_map/ppermute | solution.py:335
  60.1 1.3 %collective-permute-start.11 = (bf16[96,256]{1,0:T(8,128)(2,1)S(1)}, bf16[96,256]{1,0:T(8,128)(2,1)S(1)}, u32[]{:S(2)}, u32[]{:S(2)}) collective-permute-start(bf16[96,256]{1,0:T(8,128)(2,1)S(1)} %shard_map.70.gram_mine), channel_id=1, source_target_pairs={{0,1},{1,0},{2,3},{3,2},{4,5},{5,4},{6,7},{7,6},{8,9},{9,8},{10,11... | collective-permute-start | bytes 147464 | tf_op jit(solution)/shard_map/ppermute | solution.py:335

commit v7 on v6

--- a/solution.py
+++ b/solution.py
@@ -14,7 +14,7 @@
 VMEM = pl.BlockSpec(memory_space=pltpu.VMEM)
 HBM = pl.BlockSpec(memory_space=pltpu.HBM)
 PIECES = 4
-TABLE = 16
+TABLE = 8
 
 
 def nt(a, b):
@@ -25,12 +25,12 @@
     return lax.dot_general(a, b, (((1,), (0,)), ((), ())), preferred_element_type=F32)
 
 
-def call(body, out, args, hbm=(), scratch=(), flops=1 << 20, moved=1 << 20, limit=24 << 20):
+def call(body, out, args, spec=None, scratch=(), flops=1 << 20, moved=1 << 20, limit=24 << 20):
     return pl.pallas_call(
         body,
         out_shape=out,
-        in_specs=[HBM if i in hbm else VMEM for i in range(len(args))],
-        out_specs=jax.tree.map(lambda _: VMEM, out),
+        in_specs=[VMEM] * len(args),
+        out_specs=jax.tree.map(lambda _: spec or VMEM, out),
         scratch_shapes=list(scratch),
         compiler_params=pltpu.CompilerParams(vmem_limit_bytes=limit),
         cost_estimate=pl.CostEstimate(flops=flops, bytes_accessed=moved, transcendentals=0),
@@ -318,17 +318,27 @@
     put_parts(out.at[0], [get_parts(sent, (size,))[0] + get_parts(got, (size,))[0]])
 
 
-def new_w_body(gram_mine, gram_other, w, own, one, two, three, out):
+def ratio_body(gram_mine, gram_other, w, out):
     core = core_index()
     a, b = gram_mine[...], gram_other[...]
     gram = unpack(pick(core, a, b), pick(core, b, a))
+    old = w[...]
+    out[...] = old.astype(F32) / nn(old, gram)
+
+
+def new_w_body(ratio, own, one, two, three, out, held, sems):
     pieces, size = own.shape[0], own.shape[1] - TABLE
+    copies = []
     for away, ref in enumerate((own, one, two, three)):
+        first = (quad_index() ^ away) * pieces
         for i in range(pieces):
-            start = pl.multiple_of(((quad_index() ^ away) * pieces + i) * size, size)
-            old = w[pl.ds(start, size), :]
-            total = get_parts(ref.at[i], (size,))[0]
-            out[pl.ds(start, size), :] = (old.astype(F32) * total / nn(old, gram)).astype(BF16)
+            rows = pl.ds(pl.multiple_of((first + i) * size, size), size)
+            held[rows, :] = (ratio[rows, :] * get_parts(ref.at[i], (size,))[0]).astype(BF16)
+        rows = pl.ds(pl.multiple_of(first * size, pieces * size), pieces * size)
+        copies.append(pltpu.make_async_copy(held.at[rows, :], out.at[rows, :], sems.at[away]))
+        copies[-1].start()
+    for copy in copies:
+        copy.wait()
 
 
 def swap(x, axis, size, away):
@@ -428,8 +438,14 @@
     body = functools.partial(join_body, side_bit=term_bits - 1)
     g_mine = call(body, like(pk, k, dtype=BF16), (g_half, g_far))
     g_other = over_term(g_mine, 0)
-    ends = (share, shares[1], shares[2], shares[3])
-    new_w = call(new_w_body, like(terms, k, dtype=BF16), (g_mine, g_other, w, *ends), flops=flops // 4)
+    ratio = call(ratio_body, like(terms, k), (g_mine, g_other, w), flops=flops // 4)
+    new_w = call(
+        new_w_body,
+        like(terms, k, dtype=BF16),
+        (ratio, share, shares[1], shares[2], shares[3]),
+        spec=HBM,
+        scratch=(pltpu.VMEM((terms, k), BF16), pltpu.SemaphoreType.DMA((4,))),
+    )
     return new_w, new_h
 
 

time: 62.9 us -> 61.9 us (0.984)
  waiting for transfers between devices: 33.6 us -> 32.7 us
    ppermute x19, waiting for transfers between devices: 33.6 us -> 32.7 us  [swap(): return lax.ppermute(x, axis, [(i, i ^ away) for i in range(size)])]
    pallas_call x21 -> x22, Pallas kernels: 7.14 us -> 7.1 us  [call(): pl.pallas_call(body, out_shape=out, in_specs=[VMEM] * len(args), out_spec...]
where the time goes in v7:
time: 61.9 us; the launch traced here: 61.7 us
  waiting for transfers between devices  32.7 us (53%)
  starting transfers between devices  19.4 us (31%)
  Pallas kernels  7.1 us (11%)
  local copies, waits for them, and re-layouts  1.67 us (3%)
  between operations  0.85 us (1%)
    ppermute x19, waiting for transfers between devices, swap(): return lax.ppermute(x, axis, [(i, i ^ away) for i in range(size)])  32.7 us
    ppermute x19, starting transfers between devices, swap(): return lax.ppermute(x, axis, [(i, i ^ away) for i in range(size)])  19.4 us
    pallas_call x22, Pallas kernels, call(): pl.pallas_call(body, out_shape=out, in_specs=[VMEM] * len(args), out_spec...  7.1 us
    unnamed x10, local copies, waits for them, and re-layouts  1.67 us
  transfers between devices with their start and end apart: 19, of which 12 were waited for; matrix products, arithmetic and copies ran while one was open for 0% of the time, Pallas kernels for 6%

profile of v7, /device:TPU:0, one launch (start us, length us, event | category | flops | bytes accessed | tf_op | source)
XLA Modules:
  0.0 61.7 jit_solution(15483632767927687770)
XLA Ops:
  0.7 1.2 %copy-done.1 = bf16[1024,256]{1,0:T(8,128)(2,1)S(1)} copy-done((bf16[1024,256]{1,0:T(8,128)(2,1)S(1)}, bf16[1024,256]{1,0:T(8,128)(2,1)}, u32[]{:S(2)}) %copy-start.1) | copy-done | bytes 524312
  3.9 1.6 %collective-permute-done.b = f32[96,256]{1,0:T(8,128)S(1)} collective-permute-done((f32[96,256]{1,0:T(8,128)S(1)}, f32[96,256]{1,0:T(8,128)S(1)}, u32[]{:S(2)}, u32[]{:S(2)}) %collective-permute-start) | collective-permute-done | bytes 98336 | tf_op jit(solution)/shard_map/ppermute | solution.py:345
  5.5 0.6 shard_map.61
  6.4 2.9 %collective-permute-start.2 = (s16[264,512]{1,0:T(8,128)(2,1)S(1)}, s16[264,512]{1,0:T(8,128)(2,1)S(1)}, u32[]{:S(2)}, u32[]{:S(2)}) collective-permute-start(s16[264,512]{1,0:T(8,128)(2,1)S(1)} %shard_map.63.mine), channel_id=1, source_target_pairs={{0,2},{1,3},{2,0},{3,1},{4,6},{5,7},{6,4},{7,5},{8,10},{9,11},{10,... | collective-permute-start | bytes 811016 | tf_op jit(solution)/shard_map/ppermute | solution.py:345
  9.4 8.8 %collective-permute-done.3.b = f32[96,256]{1,0:T(8,128)S(1)} collective-permute-done((f32[96,256]{1,0:T(8,128)S(1)}, f32[96,256]{1,0:T(8,128)S(1)}, u32[]{:S(2)}, u32[]{:S(2)}) %collective-permute-start.3) | collective-permute-done | bytes 98336 | tf_op jit(solution)/shard_map/ppermute | solution.py:345
  18.4 1.2 %collective-permute-done.4.gram_other = bf16[96,256]{1,0:T(8,128)(2,1)S(1)} collective-permute-done((bf16[96,256]{1,0:T(8,128)(2,1)S(1)}, bf16[96,256]{1,0:T(8,128)(2,1)S(1)}, u32[]{:S(2)}, u32[]{:S(2)}) %collective-permute-start.4) | collective-permute-done | bytes 49184 | tf_op jit(solution)/shard_map/ppermute | solution.py:345
  20.6 0.9 %collective-permute-done.5.h = bf16[256,512]{1,0:T(8,128)(2,1)S(1)} collective-permute-done((bf16[256,512]{1,0:T(8,128)(2,1)S(1)}, bf16[256,512]{1,0:T(8,128)(2,1)S(1)}, u32[]{:S(2)}, u32[]{:S(2)}) %collective-permute-start.5) | collective-permute-done | bytes 262176 | tf_op jit(solution)/shard_map/ppermute | solution.py:345
  21.9 1.8 %collective-permute-start.12 = (s16[264,256]{1,0:T(8,128)(2,1)S(1)}, s16[264,256]{1,0:T(8,128)(2,1)S(1)}, u32[]{:S(2)}, u32[]{:S(2)}) collective-permute-start(s16[264,256]{1,0:T(8,128)(2,1)S(1)} %shard_map.74), channel_id=1, source_target_pairs={{0,4},{4,0},{8,12},{12,8},{16,20},{20,16},{24,28},{28,24},{1,5},{5... | collective-permute-start | bytes 405512 | tf_op jit(solution)/shard_map/ppermute | solution.py:345
  24.1 1.6 %collective-permute-start.13 = (s16[264,256]{1,0:T(8,128)(2,1)S(1)}, s16[264,256]{1,0:T(8,128)(2,1)S(1)}, u32[]{:S(2)}, u32[]{:S(2)}) collective-permute-start(s16[264,256]{1,0:T(8,128)(2,1)S(1)} %shard_map.75), channel_id=1, source_target_pairs={{0,8},{4,12},{8,0},{12,4},{16,24},{20,28},{24,16},{28,20},{1,9},{5... | collective-permute-start | bytes 405512 | tf_op jit(solution)/shard_map/ppermute | solution.py:345
  26.6 1.0 %collective-permute-done.12.refs_0_ = s16[264,256]{1,0:T(8,128)(2,1)S(1)} collective-permute-done((s16[264,256]{1,0:T(8,128)(2,1)S(1)}, s16[264,256]{1,0:T(8,128)(2,1)S(1)}, u32[]{:S(2)}, u32[]{:S(2)}) %collective-permute-start.12) | collective-permute-done | bytes 135200 | tf_op jit(solution)/shard_map/ppermute | solution.py:345
  27.6 3.0 %collective-permute-done.13.refs_1_ = s16[264,256]{1,0:T(8,128)(2,1)S(1)} collective-permute-done((s16[264,256]{1,0:T(8,128)(2,1)S(1)}, s16[264,256]{1,0:T(8,128)(2,1)S(1)}, u32[]{:S(2)}, u32[]{:S(2)}) %collective-permute-start.13) | collective-permute-done | bytes 135200 | tf_op jit(solution)/shard_map/ppermute | solution.py:345
  30.6 1.6 %collective-permute-done.14.refs_2_ = s16[264,256]{1,0:T(8,128)(2,1)S(1)} collective-permute-done((s16[264,256]{1,0:T(8,128)(2,1)S(1)}, s16[264,256]{1,0:T(8,128)(2,1)S(1)}, u32[]{:S(2)}, u32[]{:S(2)}) %collective-permute-start.14) | collective-permute-done | bytes 135200 | tf_op jit(solution)/shard_map/ppermute | solution.py:345
  32.5 2.8 %collective-permute-start.15 = (s16[264,256]{1,0:T(8,128)(2,1)S(1)}, s16[264,256]{1,0:T(8,128)(2,1)S(1)}, u32[]{:S(2)}, u32[]{:S(2)}) collective-permute-start(s16[264,256]{1,0:T(8,128)(2,1)S(1)} %shard_map.77.sent), channel_id=1, source_target_pairs={{0,16},{4,20},{8,24},{12,28},{16,0},{20,4},{24,8},{28,12},{1,17},{... | collective-permute-start | bytes 405512 | tf_op jit(solution)/shard_map/ppermute | solution.py:345
  35.9 7.1 %collective-permute-done.6.b = f32[48,256]{1,0:T(8,128)S(1)} collective-permute-done((f32[48,256]{1,0:T(8,128)S(1)}, f32[48,256]{1,0:T(8,128)S(1)}, u32[]{:S(2)}, u32[]{:S(2)}) %collective-permute-start.6) | collective-permute-done | bytes 49184 | tf_op jit(solution)/shard_map/ppermute | solution.py:345
  43.0 1.8 %collective-permute-start.9 = (f32[48,256]{1,0:T(8,128)S(1)}, f32[48,256]{1,0:T(8,128)S(1)}, u32[]{:S(2)}, u32[]{:S(2)}) collective-permute-start(f32[48,256]{1,0:T(8,128)S(1)} %shard_map.68.own), channel_id=1, source_target_pairs={{0,12},{4,8},{8,4},{12,0},{16,28},{20,24},{24,20},{28,16},{1,13},{... | collective-permute-start | bytes 147464 | tf_op jit(solution)/shard_map/ppermute | solution.py:345
  45.0 1.3 %collective-permute-start.18 = (s16[1,264,256]{2,1,0:T(8,128)(2,1)S(1)}, s16[1,264,256]{2,1,0:T(8,128)(2,1)S(1)}, u32[]{:S(2)}, u32[]{:S(2)}) collective-permute-start(s16[1,264,256]{2,1,0:T(8,128)(2,1)S(1)} %shard_map.78.own), channel_id=1, source_target_pairs={{0,12},{4,8},{8,4},{12,0},{16,28},{20,24},{24,20},{28,16},{1,13},{... | collective-permute-start | bytes 405512 | tf_op jit(solution)/shard_map/ppermute | solution.py:345
  46.3 0.7 %collective-permute-start.17 = (s16[1,264,256]{2,1,0:T(8,128)(2,1)S(1)}, s16[1,264,256]{2,1,0:T(8,128)(2,1)S(1)}, u32[]{:S(2)}, u32[]{:S(2)}) collective-permute-start(s16[1,264,256]{2,1,0:T(8,128)(2,1)S(1)} %shard_map.78.own), channel_id=1, source_target_pairs={{0,8},{4,12},{8,0},{12,4},{16,24},{20,28},{24,16},{28,20},{1,9},{5... | collective-permute-start | bytes 405512 | tf_op jit(solution)/shard_map/ppermute | solution.py:345
  47.0 1.6 %collective-permute-start.16 = (s16[1,264,256]{2,1,0:T(8,128)(2,1)S(1)}, s16[1,264,256]{2,1,0:T(8,128)(2,1)S(1)}, u32[]{:S(2)}, u32[]{:S(2)}) collective-permute-start(s16[1,264,256]{2,1,0:T(8,128)(2,1)S(1)} %shard_map.78.own), channel_id=1, source_target_pairs={{0,4},{4,0},{8,12},{12,8},{16,20},{20,16},{24,28},{28,24},{1,5},{5... | collective-permute-start | bytes 405512 | tf_op jit(solution)/shard_map/ppermute | solution.py:345
  48.6 1.4 %collective-permute-start.8 = (f32[48,256]{1,0:T(8,128)S(1)}, f32[48,256]{1,0:T(8,128)S(1)}, u32[]{:S(2)}, u32[]{:S(2)}) collective-permute-start(f32[48,256]{1,0:T(8,128)S(1)} %shard_map.68.own), channel_id=1, source_target_pairs={{0,8},{4,12},{8,0},{12,4},{16,24},{20,28},{24,16},{28,20},{1,9},{5... | collective-permute-start | bytes 147464 | tf_op jit(solution)/shard_map/ppermute | solution.py:345
  50.4 4.3 %collective-permute-done.8.two = f32[48,256]{1,0:T(8,128)S(1)} collective-permute-done((f32[48,256]{1,0:T(8,128)S(1)}, f32[48,256]{1,0:T(8,128)S(1)}, u32[]{:S(2)}, u32[]{:S(2)}) %collective-permute-start.8) | collective-permute-done | bytes 49184 | tf_op jit(solution)/shard_map/ppermute | solution.py:345
  55.2 1.6 %collective-permute-start.10 = (bf16[48,256]{1,0:T(8,128)(2,1)S(1)}, bf16[48,256]{1,0:T(8,128)(2,1)S(1)}, u32[]{:S(2)}, u32[]{:S(2)}) collective-permute-start(bf16[48,256]{1,0:T(8,128)(2,1)S(1)} %shard_map.69.mine), channel_id=1, source_target_pairs={{0,2},{1,3},{2,0},{3,1},{4,6},{5,7},{6,4},{7,5},{8,10},{9,11},{10,... | collective-permute-start | bytes 73736 | tf_op jit(solution)/shard_map/ppermute | solution.py:345
  56.8 2.3 %collective-permute-done.10.other = bf16[48,256]{1,0:T(8,128)(2,1)S(1)} collective-permute-done((bf16[48,256]{1,0:T(8,128)(2,1)S(1)}, bf16[48,256]{1,0:T(8,128)(2,1)S(1)}, u32[]{:S(2)}, u32[]{:S(2)}) %collective-permute-start.10) | collective-permute-done | bytes 24608 | tf_op jit(solution)/shard_map/ppermute | solution.py:345
  59.2 0.8 %shard_map.80 = bf16[256,1024]{1,0:T(8,128)(2,1)} custom-call(bf16[256,512]{1,0:T(8,128)(2,1)S(1)} %collective-permute-done.5.h, bf16[256,512]{1,0:T(8,128)(2,1)S(1)} %shard_map.66.h_own.h), custom_call_target="tpu_custom_call" | custom-call | flops 1048576 | bytes 1048576 | tf_op jit(solution)/shard_map/pallas_call | solution.py:29
  60.8 0.9 %shard_map.79 = bf16[1024,256]{1,0:T(8,128)(2,1)} custom-call(f32[1024,256]{1,0:T(8,128)S(1)} %shard_map.71.ratio, s16[1,264,256]{2,1,0:T(8,128)(2,1)S(1)} %shard_map.78.own, s16[1,264,256]{2,1,0:T(8,128)(2,1)S(1)} %collective-permute-done.16.one, s16[1,264,256]{2,1,0:T(8,128)(2,1)S(1)} %collective-permute-done.17.two, ...), custom_call_target="tpu_custom_call" | custom-call | flops 1048576 | bytes 1048576 | tf_op jit(solution)/shard_map/pallas_call | solution.py:29
  (46 shorter events, 8.0 us)
Async XLA Ops:
  0.6 1.7 %copy-start = (bf16[1024,1024]{1,0:T(8,128)(2,1)S(1)}, bf16[1024,1024]{1,0:T(8,128)(2,1)}, u32[]{:S(2)}) copy-start(bf16[1024,1024]{1,0:T(8,128)(2,1)} %m.3) | copy-start | bytes 6291460
  0.6 1.2 %copy-start.1 = (bf16[1024,256]{1,0:T(8,128)(2,1)S(1)}, bf16[1024,256]{1,0:T(8,128)(2,1)}, u32[]{:S(2)}) copy-start(bf16[1024,256]{1,0:T(8,128)(2,1)} %w.3) | copy-start | bytes 1572868
  1.8 0.8 %copy-start.4 = (s32[8,8]{1,0:T(8,128)S(1)}, s32[8,8]{1,0:T(8,128)}, u32[]{:S(2)}) copy-start(s32[8,8]{1,0:T(8,128)} %pattern.3) | copy-start | bytes 772
  3.3 2.9 %collective-permute-start.1 = (f32[256,512]{1,0:T(8,128)S(1)}, f32[256,512]{1,0:T(8,128)S(1)}, u32[]{:S(2)}, u32[]{:S(2)}) collective-permute-start(f32[256,512]{1,0:T(8,128)S(1)} %get-tuple-element.13), channel_id=1, source_target_pairs={{0,1},{1,0},{2,3},{3,2},{4,5},{5,4},{6,7},{7,6},{8,9},{9,8},{10,11... | collective-permute-start | bytes 1572872 | tf_op jit(solution)/shard_map/ppermute | solution.py:345
  3.8 1.7 %collective-permute-start = (f32[96,256]{1,0:T(8,128)S(1)}, f32[96,256]{1,0:T(8,128)S(1)}, u32[]{:S(2)}, u32[]{:S(2)}) collective-permute-start(f32[96,256]{1,0:T(8,128)S(1)} %get-tuple-element.11), channel_id=1, source_target_pairs={{0,1},{1,0},{2,3},{3,2},{4,5},{5,4},{6,7},{7,6},{8,9},{9,8},{10,11... | collective-permute-start | bytes 294920 | tf_op jit(solution)/shard_map/ppermute | solution.py:345
  5.5 12.8 %copy-start.3 = (bf16[256,1024]{1,0:T(8,128)(2,1)S(1)}, bf16[256,1024]{1,0:T(8,128)(2,1)}, u32[]{:S(2)}) copy-start(bf16[256,1024]{1,0:T(8,128)(2,1)} %h.1) | copy-start | bytes 1572868
  6.4 13.1 %collective-permute-start.2 = (s16[264,512]{1,0:T(8,128)(2,1)S(1)}, s16[264,512]{1,0:T(8,128)(2,1)S(1)}, u32[]{:S(2)}, u32[]{:S(2)}) collective-permute-start(s16[264,512]{1,0:T(8,128)(2,1)S(1)} %shard_map.63.mine), channel_id=1, source_target_pairs={{0,2},{1,3},{2,0},{3,1},{4,6},{5,7},{6,4},{7,5},{8,10},{9,11},{10,... | collective-permute-start | bytes 811016 | tf_op jit(solution)/shard_map/ppermute | solution.py:345
  9.3 8.9 %collective-permute-start.3 = (f32[96,256]{1,0:T(8,128)S(1)}, f32[96,256]{1,0:T(8,128)S(1)}, u32[]{:S(2)}, u32[]{:S(2)}) collective-permute-start(f32[96,256]{1,0:T(8,128)S(1)} %shard_map.60.refs_0_.a), channel_id=1, source_target_pairs={{0,2},{1,3},{2,0},{3,1},{4,6},{5,7},{6,4},{7,5},{8,10},{9,11},{10,... | collective-permute-start | bytes 294920 | tf_op jit(solution)/shard_map/ppermute | solution.py:345
  18.2 1.3 %collective-permute-start.4 = (bf16[96,256]{1,0:T(8,128)(2,1)S(1)}, bf16[96,256]{1,0:T(8,128)(2,1)S(1)}, u32[]{:S(2)}, u32[]{:S(2)}) collective-permute-start(bf16[96,256]{1,0:T(8,128)(2,1)S(1)} %shard_map.64.gram_mine), channel_id=1, source_target_pairs={{0,1},{1,0},{2,3},{3,2},{4,5},{5,4},{6,7},{7,6},{8,9},{9,8},{10,11... | collective-permute-start | bytes 147464 | tf_op jit(solution)/shard_map/ppermute | solution.py:345
  19.9 1.6 %collective-permute-start.5 = (bf16[256,512]{1,0:T(8,128)(2,1)S(1)}, bf16[256,512]{1,0:T(8,128)(2,1)S(1)}, u32[]{:S(2)}, u32[]{:S(2)}) collective-permute-start(bf16[256,512]{1,0:T(8,128)(2,1)S(1)} %shard_map.66.h_own.h), channel_id=1, source_target_pairs={{0,1},{1,0},{2,3},{3,2},{4,5},{5,4},{6,7},{7,6},{8,9},{9,8},{10,11... | collective-permute-start | bytes 786440 | tf_op jit(solution)/shard_map/ppermute | solution.py:345
  21.9 5.7 %collective-permute-start.12 = (s16[264,256]{1,0:T(8,128)(2,1)S(1)}, s16[264,256]{1,0:T(8,128)(2,1)S(1)}, u32[]{:S(2)}, u32[]{:S(2)}) collective-permute-start(s16[264,256]{1,0:T(8,128)(2,1)S(1)} %shard_map.74), channel_id=1, source_target_pairs={{0,4},{4,0},{8,12},{12,8},{16,20},{20,16},{24,28},{28,24},{1,5},{5... | collective-permute-start | bytes 405512 | tf_op jit(solution)/shard_map/ppermute | solution.py:345
  24.1 6.5 %collective-permute-start.13 = (s16[264,256]{1,0:T(8,128)(2,1)S(1)}, s16[264,256]{1,0:T(8,128)(2,1)S(1)}, u32[]{:S(2)}, u32[]{:S(2)}) collective-permute-start(s16[264,256]{1,0:T(8,128)(2,1)S(1)} %shard_map.75), channel_id=1, source_target_pairs={{0,8},{4,12},{8,0},{12,4},{16,24},{20,28},{24,16},{28,20},{1,9},{5... | collective-permute-start | bytes 405512 | tf_op jit(solution)/shard_map/ppermute | solution.py:345
  26.1 6.1 %collective-permute-start.14 = (s16[264,256]{1,0:T(8,128)(2,1)S(1)}, s16[264,256]{1,0:T(8,128)(2,1)S(1)}, u32[]{:S(2)}, u32[]{:S(2)}) collective-permute-start(s16[264,256]{1,0:T(8,128)(2,1)S(1)} %shard_map.76), channel_id=1, source_target_pairs={{0,12},{4,8},{8,4},{12,0},{16,28},{20,24},{24,20},{28,16},{1,13},{... | collective-permute-start | bytes 405512 | tf_op jit(solution)/shard_map/ppermute | solution.py:345
  26.6 33.8 %copy-start.2 = (bf16[1024,256]{1,0:T(8,128)(2,1)S(1)}, bf16[1024,256]{1,0:T(8,128)(2,1)}, u32[]{:S(2)}) copy-start(bf16[1024,256]{1,0:T(8,128)(2,1)} %w.3) | copy-start | bytes 1572868
  32.5 12.3 %collective-permute-start.15 = (s16[264,256]{1,0:T(8,128)(2,1)S(1)}, s16[264,256]{1,0:T(8,128)(2,1)S(1)}, u32[]{:S(2)}, u32[]{:S(2)}) collective-permute-start(s16[264,256]{1,0:T(8,128)(2,1)S(1)} %shard_map.77.sent), channel_id=1, source_target_pairs={{0,16},{4,20},{8,24},{12,28},{16,0},{20,4},{24,8},{28,12},{1,17},{... | collective-permute-start | bytes 405512 | tf_op jit(solution)/shard_map/ppermute | solution.py:345
  35.7 7.3 %collective-permute-start.6 = (f32[48,256]{1,0:T(8,128)S(1)}, f32[48,256]{1,0:T(8,128)S(1)}, u32[]{:S(2)}, u32[]{:S(2)}) collective-permute-start(f32[48,256]{1,0:T(8,128)S(1)} %shard_map.67.a), channel_id=1, source_target_pairs={{0,16},{4,20},{8,24},{12,28},{16,0},{20,4},{24,8},{28,12},{1,17},{... | collective-permute-start | bytes 147464 | tf_op jit(solution)/shard_map/ppermute | solution.py:345
  43.0 7.0 %collective-permute-start.9 = (f32[48,256]{1,0:T(8,128)S(1)}, f32[48,256]{1,0:T(8,128)S(1)}, u32[]{:S(2)}, u32[]{:S(2)}) collective-permute-start(f32[48,256]{1,0:T(8,128)S(1)} %shard_map.68.own), channel_id=1, source_target_pairs={{0,12},{4,8},{8,4},{12,0},{16,28},{20,24},{24,20},{28,16},{1,13},{... | collective-permute-start | bytes 147464 | tf_op jit(solution)/shard_map/ppermute | solution.py:345
  45.0 15.7 %collective-permute-start.18 = (s16[1,264,256]{2,1,0:T(8,128)(2,1)S(1)}, s16[1,264,256]{2,1,0:T(8,128)(2,1)S(1)}, u32[]{:S(2)}, u32[]{:S(2)}) collective-permute-start(s16[1,264,256]{2,1,0:T(8,128)(2,1)S(1)} %shard_map.78.own), channel_id=1, source_target_pairs={{0,12},{4,8},{8,4},{12,0},{16,28},{20,24},{24,20},{28,16},{1,13},{... | collective-permute-start | bytes 405512 | tf_op jit(solution)/shard_map/ppermute | solution.py:345
  46.3 14.4 %collective-permute-start.17 = (s16[1,264,256]{2,1,0:T(8,128)(2,1)S(1)}, s16[1,264,256]{2,1,0:T(8,128)(2,1)S(1)}, u32[]{:S(2)}, u32[]{:S(2)}) collective-permute-start(s16[1,264,256]{2,1,0:T(8,128)(2,1)S(1)} %shard_map.78.own), channel_id=1, source_target_pairs={{0,8},{4,12},{8,0},{12,4},{16,24},{20,28},{24,16},{28,20},{1,9},{5... | collective-permute-start | bytes 405512 | tf_op jit(solution)/shard_map/ppermute | solution.py:345
  47.0 13.8 %collective-permute-start.16 = (s16[1,264,256]{2,1,0:T(8,128)(2,1)S(1)}, s16[1,264,256]{2,1,0:T(8,128)(2,1)S(1)}, u32[]{:S(2)}, u32[]{:S(2)}) collective-permute-start(s16[1,264,256]{2,1,0:T(8,128)(2,1)S(1)} %shard_map.78.own), channel_id=1, source_target_pairs={{0,4},{4,0},{8,12},{12,8},{16,20},{20,16},{24,28},{28,24},{1,5},{5... | collective-permute-start | bytes 405512 | tf_op jit(solution)/shard_map/ppermute | solution.py:345
  48.6 6.1 %collective-permute-start.8 = (f32[48,256]{1,0:T(8,128)S(1)}, f32[48,256]{1,0:T(8,128)S(1)}, u32[]{:S(2)}, u32[]{:S(2)}) collective-permute-start(f32[48,256]{1,0:T(8,128)S(1)} %shard_map.68.own), channel_id=1, source_target_pairs={{0,8},{4,12},{8,0},{12,4},{16,24},{20,28},{24,16},{28,20},{1,9},{5... | collective-permute-start | bytes 147464 | tf_op jit(solution)/shard_map/ppermute | solution.py:345
  50.0 5.2 %collective-permute-start.7 = (f32[48,256]{1,0:T(8,128)S(1)}, f32[48,256]{1,0:T(8,128)S(1)}, u32[]{:S(2)}, u32[]{:S(2)}) collective-permute-start(f32[48,256]{1,0:T(8,128)S(1)} %shard_map.68.own), channel_id=1, source_target_pairs={{0,4},{4,0},{8,12},{12,8},{16,20},{20,16},{24,28},{28,24},{1,5},{5... | collective-permute-start | bytes 147464 | tf_op jit(solution)/shard_map/ppermute | solution.py:345
  55.2 3.9 %collective-permute-start.10 = (bf16[48,256]{1,0:T(8,128)(2,1)S(1)}, bf16[48,256]{1,0:T(8,128)(2,1)S(1)}, u32[]{:S(2)}, u32[]{:S(2)}) collective-permute-start(bf16[48,256]{1,0:T(8,128)(2,1)S(1)} %shard_map.69.mine), channel_id=1, source_target_pairs={{0,2},{1,3},{2,0},{3,1},{4,6},{5,7},{6,4},{7,5},{8,10},{9,11},{10,... | collective-permute-start | bytes 73736 | tf_op jit(solution)/shard_map/ppermute | solution.py:345
  59.1 1.3 %collective-permute-start.11 = (bf16[96,256]{1,0:T(8,128)(2,1)S(1)}, bf16[96,256]{1,0:T(8,128)(2,1)S(1)}, u32[]{:S(2)}, u32[]{:S(2)}) collective-permute-start(bf16[96,256]{1,0:T(8,128)(2,1)S(1)} %shard_map.70.gram_mine), channel_id=1, source_target_pairs={{0,1},{1,0},{2,3},{3,2},{4,5},{5,4},{6,7},{7,6},{8,9},{9,8},{10,11... | collective-permute-start | bytes 147464 | tf_op jit(solution)/shard_map/ppermute | solution.py:345

commit v8 on v7

--- a/solution.py
+++ b/solution.py
@@ -13,7 +13,7 @@
 BF16 = jnp.bfloat16
 VMEM = pl.BlockSpec(memory_space=pltpu.VMEM)
 HBM = pl.BlockSpec(memory_space=pltpu.HBM)
-PIECES = 4
+PIECES = 2
 TABLE = 8
 
 
@@ -54,6 +54,7 @@
 
 
 def encode(x):
+    x = x * lax.rsqrt(jnp.maximum(x, 1e-30))
     least = jnp.min(x, axis=0, keepdims=True)
     most = jnp.max(x, axis=0, keepdims=True)
     octave = lambda v: jnp.log2(jnp.maximum(v, 1e-18)) * PER_OCTAVE
@@ -68,7 +69,8 @@
 
 def decode(code, low, high):
     base, step = limits(low, high)
-    return base + (code.astype(jnp.int32) + LEVELS // 2).astype(F32) * step
+    root = base + (code.astype(jnp.int32) + LEVELS // 2).astype(F32) * step
+    return root * root
 
 
 def put_codes(ref, first, groups):
@@ -278,14 +280,6 @@
     out[...] = pick(term_bit(side_bit), part[:rows], part[rows:])
 
 
-def join_body(mine, other, out, *, side_bit):
-    rows = mine.shape[0]
-    a, b = mine[...], other[...]
-    side = term_bit(side_bit)
-    out[:rows, :] = pick(side, a, b)
-    out[rows:, :] = pick(side, b, a)
-
-
 def gram_quad_body(own, one, two, three, out):
     out[...] = ((own[...] + one[...]) + (two[...] + three[...])).astype(BF16)
 
@@ -318,10 +312,14 @@
     put_parts(out.at[0], [get_parts(sent, (size,))[0] + get_parts(got, (size,))[0]])
 
 
-def ratio_body(gram_mine, gram_other, w, out):
-    core = core_index()
-    a, b = gram_mine[...], gram_other[...]
-    gram = unpack(pick(core, a, b), pick(core, b, a))
+def ratio_body(here, near, far, across, w, out, *, side_bit):
+    core, side = core_index(), term_bit(side_bit)
+
+    def both(one, two):
+        return jnp.concatenate([pick(side, one, two), pick(side, two, one)], axis=0)
+
+    mine, other = both(here[...], far[...]), both(near[...], across[...])
+    gram = unpack(pick(core, mine, other), pick(core, other, mine))
     old = w[...]
     out[...] = old.astype(F32) / nn(old, gram)
 
@@ -404,7 +402,7 @@
     payload = lambda rows: like(rows + TABLE, k, dtype=jnp.int16)
     costs = dict(flops=flops // 4, moved=moved // 4)
     got = {}
-    for away in (3, 1, 2):
+    for away in (3, 2, 1):
         body = functools.partial(send_body, away=away)
         sent = call(body, payload(size), (masked_other, part, h_other), **costs)
         got[away] = over_doc(sent, away)
@@ -434,11 +432,12 @@
     for away in (3, 1, 2):
         grams[away] = over_doc(gram, away)
     g_half = call(gram_quad_body, like(pk // 2, k, dtype=BF16), (gram, grams[1], grams[2], grams[3]))
-    g_far = over_term(g_half, term_bits - 1)
-    body = functools.partial(join_body, side_bit=term_bits - 1)
-    g_mine = call(body, like(pk, k, dtype=BF16), (g_half, g_far))
-    g_other = over_term(g_mine, 0)
-    ratio = call(ratio_body, like(terms, k), (g_mine, g_other, w), flops=flops // 4)
+    far = term_bits - 1
+    g_far = over_term(g_half, far)
+    g_across = swap(g_half, "term", n_term, 1 | (1 << far))
+    g_near = over_term(g_half, 0)
+    body = functools.partial(ratio_body, side_bit=far)
+    ratio = call(body, like(terms, k), (g_half, g_near, g_far, g_across, w), flops=flops // 4)
     new_w = call(
         new_w_body,
         like(terms, k, dtype=BF16),

time: 61.9 us -> 61.8 us (level)
    ppermute x19 -> x20, waiting for transfers between devices: 32.7 us -> 32.3 us  [swap(): return lax.ppermute(x, axis, [(i, i ^ away) for i in range(size)])]
    pallas_call x22 -> x21, Pallas kernels: 7.1 us -> 7.36 us  [call(): pl.pallas_call(body, out_shape=out, in_specs=[VMEM] * len(args), out_spec...]
    ppermute x19 -> x20, starting transfers between devices: 19.4 us -> 19.5 us  [swap(): return lax.ppermute(x, axis, [(i, i ^ away) for i in range(size)])]
  transfers between devices with their start and end apart: 19 -> 20, of which waited for: 12 -> 12; matrix products, arithmetic and copies ran while one was open for 0% -> 0% of each run, Pallas kernels for 6% -> 6%
where the time goes in v8:
time: 61.8 us; the launch traced here: 61.6 us
  waiting for transfers between devices  32.3 us (52%)
  starting transfers between devices  19.5 us (32%)
  Pallas kernels  7.36 us (12%)
  local copies, waits for them, and re-layouts  1.67 us (3%)
  between operations  0.84 us (1%)
    ppermute x20, waiting for transfers between devices, swap(): return lax.ppermute(x, axis, [(i, i ^ away) for i in range(size)])  32.3 us
    ppermute x20, starting transfers between devices, swap(): return lax.ppermute(x, axis, [(i, i ^ away) for i in range(size)])  19.5 us
    pallas_call x21, Pallas kernels, call(): pl.pallas_call(body, out_shape=out, in_specs=[VMEM] * len(args), out_spec...  7.36 us
    unnamed x10, local copies, waits for them, and re-layouts  1.67 us
  transfers between devices with their start and end apart: 20, of which 12 were waited for; matrix products, arithmetic and copies ran while one was open for 0% of the time, Pallas kernels for 6%

profile of v8, /device:TPU:0, one launch (start us, length us, event | category | flops | bytes accessed | tf_op | source)
XLA Modules:
  0.0 61.6 jit_solution(15291356386105262152)
XLA Ops:
  0.7 1.2 %copy-done.1 = bf16[1024,256]{1,0:T(8,128)(2,1)S(1)} copy-done((bf16[1024,256]{1,0:T(8,128)(2,1)S(1)}, bf16[1024,256]{1,0:T(8,128)(2,1)}, u32[]{:S(2)}) %copy-start.1) | copy-done | bytes 524312
  3.9 1.6 %collective-permute-done.b = f32[96,256]{1,0:T(8,128)S(1)} collective-permute-done((f32[96,256]{1,0:T(8,128)S(1)}, f32[96,256]{1,0:T(8,128)S(1)}, u32[]{:S(2)}, u32[]{:S(2)}) %collective-permute-start) | collective-permute-done | bytes 98336 | tf_op jit(solution)/shard_map/ppermute | solution.py:343
  6.5 2.9 %collective-permute-start.2 = (s16[264,512]{1,0:T(8,128)(2,1)S(1)}, s16[264,512]{1,0:T(8,128)(2,1)S(1)}, u32[]{:S(2)}, u32[]{:S(2)}) collective-permute-start(s16[264,512]{1,0:T(8,128)(2,1)S(1)} %shard_map.63.mine), channel_id=1, source_target_pairs={{0,2},{1,3},{2,0},{3,1},{4,6},{5,7},{6,4},{7,5},{8,10},{9,11},{10,... | collective-permute-start | bytes 811016 | tf_op jit(solution)/shard_map/ppermute | solution.py:343
  9.5 8.8 %collective-permute-done.3.b = f32[96,256]{1,0:T(8,128)S(1)} collective-permute-done((f32[96,256]{1,0:T(8,128)S(1)}, f32[96,256]{1,0:T(8,128)S(1)}, u32[]{:S(2)}, u32[]{:S(2)}) %collective-permute-start.3) | collective-permute-done | bytes 98336 | tf_op jit(solution)/shard_map/ppermute | solution.py:343
  18.4 1.2 %collective-permute-done.4.gram_other = bf16[96,256]{1,0:T(8,128)(2,1)S(1)} collective-permute-done((bf16[96,256]{1,0:T(8,128)(2,1)S(1)}, bf16[96,256]{1,0:T(8,128)(2,1)S(1)}, u32[]{:S(2)}, u32[]{:S(2)}) %collective-permute-start.4) | collective-permute-done | bytes 49184 | tf_op jit(solution)/shard_map/ppermute | solution.py:343
  20.7 0.9 %collective-permute-done.5.h = bf16[256,512]{1,0:T(8,128)(2,1)S(1)} collective-permute-done((bf16[256,512]{1,0:T(8,128)(2,1)S(1)}, bf16[256,512]{1,0:T(8,128)(2,1)S(1)}, u32[]{:S(2)}, u32[]{:S(2)}) %collective-permute-start.5) | collective-permute-done | bytes 262176 | tf_op jit(solution)/shard_map/ppermute | solution.py:343
  22.0 1.8 %collective-permute-start.13 = (s16[264,256]{1,0:T(8,128)(2,1)S(1)}, s16[264,256]{1,0:T(8,128)(2,1)S(1)}, u32[]{:S(2)}, u32[]{:S(2)}) collective-permute-start(s16[264,256]{1,0:T(8,128)(2,1)S(1)} %shard_map.73), channel_id=1, source_target_pairs={{0,4},{4,0},{8,12},{12,8},{16,20},{20,16},{24,28},{28,24},{1,5},{5... | collective-permute-start | bytes 405512 | tf_op jit(solution)/shard_map/ppermute | solution.py:343
  24.2 1.6 %collective-permute-start.14 = (s16[264,256]{1,0:T(8,128)(2,1)S(1)}, s16[264,256]{1,0:T(8,128)(2,1)S(1)}, u32[]{:S(2)}, u32[]{:S(2)}) collective-permute-start(s16[264,256]{1,0:T(8,128)(2,1)S(1)} %shard_map.74), channel_id=1, source_target_pairs={{0,8},{4,12},{8,0},{12,4},{16,24},{20,28},{24,16},{28,20},{1,9},{5... | collective-permute-start | bytes 405512 | tf_op jit(solution)/shard_map/ppermute | solution.py:343
  26.8 1.0 %collective-permute-done.13.refs_0_ = s16[264,256]{1,0:T(8,128)(2,1)S(1)} collective-permute-done((s16[264,256]{1,0:T(8,128)(2,1)S(1)}, s16[264,256]{1,0:T(8,128)(2,1)S(1)}, u32[]{:S(2)}, u32[]{:S(2)}) %collective-permute-start.13) | collective-permute-done | bytes 135200 | tf_op jit(solution)/shard_map/ppermute | solution.py:343
  27.8 3.0 %collective-permute-done.14.refs_1_ = s16[264,256]{1,0:T(8,128)(2,1)S(1)} collective-permute-done((s16[264,256]{1,0:T(8,128)(2,1)S(1)}, s16[264,256]{1,0:T(8,128)(2,1)S(1)}, u32[]{:S(2)}, u32[]{:S(2)}) %collective-permute-start.14) | collective-permute-done | bytes 135200 | tf_op jit(solution)/shard_map/ppermute | solution.py:343
  30.8 1.6 %collective-permute-done.15.refs_2_ = s16[264,256]{1,0:T(8,128)(2,1)S(1)} collective-permute-done((s16[264,256]{1,0:T(8,128)(2,1)S(1)}, s16[264,256]{1,0:T(8,128)(2,1)S(1)}, u32[]{:S(2)}, u32[]{:S(2)}) %collective-permute-start.15) | collective-permute-done | bytes 135200 | tf_op jit(solution)/shard_map/ppermute | solution.py:343
  32.7 2.8 %collective-permute-start.16 = (s16[264,256]{1,0:T(8,128)(2,1)S(1)}, s16[264,256]{1,0:T(8,128)(2,1)S(1)}, u32[]{:S(2)}, u32[]{:S(2)}) collective-permute-start(s16[264,256]{1,0:T(8,128)(2,1)S(1)} %shard_map.76.sent), channel_id=1, source_target_pairs={{0,16},{4,20},{8,24},{12,28},{16,0},{20,4},{24,8},{28,12},{1,17},{... | collective-permute-start | bytes 405512 | tf_op jit(solution)/shard_map/ppermute | solution.py:343
  36.1 7.1 %collective-permute-done.6.b = f32[48,256]{1,0:T(8,128)S(1)} collective-permute-done((f32[48,256]{1,0:T(8,128)S(1)}, f32[48,256]{1,0:T(8,128)S(1)}, u32[]{:S(2)}, u32[]{:S(2)}) %collective-permute-start.6) | collective-permute-done | bytes 49184 | tf_op jit(solution)/shard_map/ppermute | solution.py:343
  43.2 1.8 %collective-permute-start.9 = (f32[48,256]{1,0:T(8,128)S(1)}, f32[48,256]{1,0:T(8,128)S(1)}, u32[]{:S(2)}, u32[]{:S(2)}) collective-permute-start(f32[48,256]{1,0:T(8,128)S(1)} %shard_map.68.own), channel_id=1, source_target_pairs={{0,12},{4,8},{8,4},{12,0},{16,28},{20,24},{24,20},{28,16},{1,13},{... | collective-permute-start | bytes 147464 | tf_op jit(solution)/shard_map/ppermute | solution.py:343
  45.3 1.3 %collective-permute-start.19 = (s16[1,264,256]{2,1,0:T(8,128)(2,1)S(1)}, s16[1,264,256]{2,1,0:T(8,128)(2,1)S(1)}, u32[]{:S(2)}, u32[]{:S(2)}) collective-permute-start(s16[1,264,256]{2,1,0:T(8,128)(2,1)S(1)} %shard_map.77.own), channel_id=1, source_target_pairs={{0,12},{4,8},{8,4},{12,0},{16,28},{20,24},{24,20},{28,16},{1,13},{... | collective-permute-start | bytes 405512 | tf_op jit(solution)/shard_map/ppermute | solution.py:343
  46.6 0.7 %collective-permute-start.18 = (s16[1,264,256]{2,1,0:T(8,128)(2,1)S(1)}, s16[1,264,256]{2,1,0:T(8,128)(2,1)S(1)}, u32[]{:S(2)}, u32[]{:S(2)}) collective-permute-start(s16[1,264,256]{2,1,0:T(8,128)(2,1)S(1)} %shard_map.77.own), channel_id=1, source_target_pairs={{0,8},{4,12},{8,0},{12,4},{16,24},{20,28},{24,16},{28,20},{1,9},{5... | collective-permute-start | bytes 405512 | tf_op jit(solution)/shard_map/ppermute | solution.py:343
  47.2 1.6 %collective-permute-start.17 = (s16[1,264,256]{2,1,0:T(8,128)(2,1)S(1)}, s16[1,264,256]{2,1,0:T(8,128)(2,1)S(1)}, u32[]{:S(2)}, u32[]{:S(2)}) collective-permute-start(s16[1,264,256]{2,1,0:T(8,128)(2,1)S(1)} %shard_map.77.own), channel_id=1, source_target_pairs={{0,4},{4,0},{8,12},{12,8},{16,20},{20,16},{24,28},{28,24},{1,5},{5... | collective-permute-start | bytes 405512 | tf_op jit(solution)/shard_map/ppermute | solution.py:343
  48.8 1.4 %collective-permute-start.8 = (f32[48,256]{1,0:T(8,128)S(1)}, f32[48,256]{1,0:T(8,128)S(1)}, u32[]{:S(2)}, u32[]{:S(2)}) collective-permute-start(f32[48,256]{1,0:T(8,128)S(1)} %shard_map.68.own), channel_id=1, source_target_pairs={{0,8},{4,12},{8,0},{12,4},{16,24},{20,28},{24,16},{28,20},{1,9},{5... | collective-permute-start | bytes 147464 | tf_op jit(solution)/shard_map/ppermute | solution.py:343
  50.6 4.3 %collective-permute-done.8.two = f32[48,256]{1,0:T(8,128)S(1)} collective-permute-done((f32[48,256]{1,0:T(8,128)S(1)}, f32[48,256]{1,0:T(8,128)S(1)}, u32[]{:S(2)}, u32[]{:S(2)}) %collective-permute-start.8) | collective-permute-done | bytes 49184 | tf_op jit(solution)/shard_map/ppermute | solution.py:343
  55.5 1.0 %collective-permute-start.12 = (bf16[48,256]{1,0:T(8,128)(2,1)S(1)}, bf16[48,256]{1,0:T(8,128)(2,1)S(1)}, u32[]{:S(2)}, u32[]{:S(2)}) collective-permute-start(bf16[48,256]{1,0:T(8,128)(2,1)S(1)} %shard_map.69.here), channel_id=1, source_target_pairs={{0,3},{1,2},{2,1},{3,0},{4,7},{5,6},{6,5},{7,4},{8,11},{9,10},{10,... | collective-permute-start | bytes 73736 | tf_op jit(solution)/shard_map/ppermute | solution.py:343
  56.4 0.6 %collective-permute-start.11 = (bf16[48,256]{1,0:T(8,128)(2,1)S(1)}, bf16[48,256]{1,0:T(8,128)(2,1)S(1)}, u32[]{:S(2)}, u32[]{:S(2)}) collective-permute-start(bf16[48,256]{1,0:T(8,128)(2,1)S(1)} %shard_map.69.here), channel_id=1, source_target_pairs={{0,2},{1,3},{2,0},{3,1},{4,6},{5,7},{6,4},{7,5},{8,10},{9,11},{10,... | collective-permute-start | bytes 73736 | tf_op jit(solution)/shard_map/ppermute | solution.py:343
  57.1 1.9 %collective-permute-done.12.across = bf16[48,256]{1,0:T(8,128)(2,1)S(1)} collective-permute-done((bf16[48,256]{1,0:T(8,128)(2,1)S(1)}, bf16[48,256]{1,0:T(8,128)(2,1)S(1)}, u32[]{:S(2)}, u32[]{:S(2)}) %collective-permute-start.12) | collective-permute-done | bytes 24608 | tf_op jit(solution)/shard_map/ppermute | solution.py:343
  59.1 0.8 %shard_map.79 = bf16[256,1024]{1,0:T(8,128)(2,1)} custom-call(bf16[256,512]{1,0:T(8,128)(2,1)S(1)} %collective-permute-done.5.h, bf16[256,512]{1,0:T(8,128)(2,1)S(1)} %shard_map.66.h_own.h), custom_call_target="tpu_custom_call" | custom-call | flops 1048576 | bytes 1048576 | tf_op jit(solution)/shard_map/pallas_call | solution.py:29
  60.7 1.0 %shard_map.78 = bf16[1024,256]{1,0:T(8,128)(2,1)} custom-call(f32[1024,256]{1,0:T(8,128)S(1)} %shard_map.70.ratio, s16[1,264,256]{2,1,0:T(8,128)(2,1)S(1)} %shard_map.77.own, s16[1,264,256]{2,1,0:T(8,128)(2,1)S(1)} %collective-permute-done.17.one, s16[1,264,256]{2,1,0:T(8,128)(2,1)S(1)} %collective-permute-done.18.two, ...), custom_call_target="tpu_custom_call" | custom-call | flops 1048576 | bytes 1048576 | tf_op jit(solution)/shard_map/pallas_call | solution.py:29
  (47 shorter events, 8.8 us)
Async XLA Ops:
  0.6 1.7 %copy-start = (bf16[1024,1024]{1,0:T(8,128)(2,1)S(1)}, bf16[1024,1024]{1,0:T(8,128)(2,1)}, u32[]{:S(2)}) copy-start(bf16[1024,1024]{1,0:T(8,128)(2,1)} %m.3) | copy-start | bytes 6291460
  0.6 1.2 %copy-start.1 = (bf16[1024,256]{1,0:T(8,128)(2,1)S(1)}, bf16[1024,256]{1,0:T(8,128)(2,1)}, u32[]{:S(2)}) copy-start(bf16[1024,256]{1,0:T(8,128)(2,1)} %w.3) | copy-start | bytes 1572868
  3.3 2.9 %collective-permute-start.1 = (f32[256,512]{1,0:T(8,128)S(1)}, f32[256,512]{1,0:T(8,128)S(1)}, u32[]{:S(2)}, u32[]{:S(2)}) collective-permute-start(f32[256,512]{1,0:T(8,128)S(1)} %get-tuple-element.13), channel_id=1, source_target_pairs={{0,1},{1,0},{2,3},{3,2},{4,5},{5,4},{6,7},{7,6},{8,9},{9,8},{10,11... | collective-permute-start | bytes 1572872 | tf_op jit(solution)/shard_map/ppermute | solution.py:343
  3.8 1.7 %collective-permute-start = (f32[96,256]{1,0:T(8,128)S(1)}, f32[96,256]{1,0:T(8,128)S(1)}, u32[]{:S(2)}, u32[]{:S(2)}) collective-permute-start(f32[96,256]{1,0:T(8,128)S(1)} %get-tuple-element.11), channel_id=1, source_target_pairs={{0,1},{1,0},{2,3},{3,2},{4,5},{5,4},{6,7},{7,6},{8,9},{9,8},{10,11... | collective-permute-start | bytes 294920 | tf_op jit(solution)/shard_map/ppermute | solution.py:343
  5.5 12.9 %copy-start.3 = (bf16[256,1024]{1,0:T(8,128)(2,1)S(1)}, bf16[256,1024]{1,0:T(8,128)(2,1)}, u32[]{:S(2)}) copy-start(bf16[256,1024]{1,0:T(8,128)(2,1)} %h.1) | copy-start | bytes 1572868
  6.5 13.1 %collective-permute-start.2 = (s16[264,512]{1,0:T(8,128)(2,1)S(1)}, s16[264,512]{1,0:T(8,128)(2,1)S(1)}, u32[]{:S(2)}, u32[]{:S(2)}) collective-permute-start(s16[264,512]{1,0:T(8,128)(2,1)S(1)} %shard_map.63.mine), channel_id=1, source_target_pairs={{0,2},{1,3},{2,0},{3,1},{4,6},{5,7},{6,4},{7,5},{8,10},{9,11},{10,... | collective-permute-start | bytes 811016 | tf_op jit(solution)/shard_map/ppermute | solution.py:343
  9.4 8.9 %collective-permute-start.3 = (f32[96,256]{1,0:T(8,128)S(1)}, f32[96,256]{1,0:T(8,128)S(1)}, u32[]{:S(2)}, u32[]{:S(2)}) collective-permute-start(f32[96,256]{1,0:T(8,128)S(1)} %shard_map.60.refs_0_.a), channel_id=1, source_target_pairs={{0,2},{1,3},{2,0},{3,1},{4,6},{5,7},{6,4},{7,5},{8,10},{9,11},{10,... | collective-permute-start | bytes 294920 | tf_op jit(solution)/shard_map/ppermute | solution.py:343
  18.3 1.3 %collective-permute-start.4 = (bf16[96,256]{1,0:T(8,128)(2,1)S(1)}, bf16[96,256]{1,0:T(8,128)(2,1)S(1)}, u32[]{:S(2)}, u32[]{:S(2)}) collective-permute-start(bf16[96,256]{1,0:T(8,128)(2,1)S(1)} %shard_map.64.gram_mine), channel_id=1, source_target_pairs={{0,1},{1,0},{2,3},{3,2},{4,5},{5,4},{6,7},{7,6},{8,9},{9,8},{10,11... | collective-permute-start | bytes 147464 | tf_op jit(solution)/shard_map/ppermute | solution.py:343
  20.0 1.6 %collective-permute-start.5 = (bf16[256,512]{1,0:T(8,128)(2,1)S(1)}, bf16[256,512]{1,0:T(8,128)(2,1)S(1)}, u32[]{:S(2)}, u32[]{:S(2)}) collective-permute-start(bf16[256,512]{1,0:T(8,128)(2,1)S(1)} %shard_map.66.h_own.h), channel_id=1, source_target_pairs={{0,1},{1,0},{2,3},{3,2},{4,5},{5,4},{6,7},{7,6},{8,9},{9,8},{10,11... | collective-permute-start | bytes 786440 | tf_op jit(solution)/shard_map/ppermute | solution.py:343
  22.0 5.7 %collective-permute-start.13 = (s16[264,256]{1,0:T(8,128)(2,1)S(1)}, s16[264,256]{1,0:T(8,128)(2,1)S(1)}, u32[]{:S(2)}, u32[]{:S(2)}) collective-permute-start(s16[264,256]{1,0:T(8,128)(2,1)S(1)} %shard_map.73), channel_id=1, source_target_pairs={{0,4},{4,0},{8,12},{12,8},{16,20},{20,16},{24,28},{28,24},{1,5},{5... | collective-permute-start | bytes 405512 | tf_op jit(solution)/shard_map/ppermute | solution.py:343
  24.2 6.5 %collective-permute-start.14 = (s16[264,256]{1,0:T(8,128)(2,1)S(1)}, s16[264,256]{1,0:T(8,128)(2,1)S(1)}, u32[]{:S(2)}, u32[]{:S(2)}) collective-permute-start(s16[264,256]{1,0:T(8,128)(2,1)S(1)} %shard_map.74), channel_id=1, source_target_pairs={{0,8},{4,12},{8,0},{12,4},{16,24},{20,28},{24,16},{28,20},{1,9},{5... | collective-permute-start | bytes 405512 | tf_op jit(solution)/shard_map/ppermute | solution.py:343
  26.3 6.1 %collective-permute-start.15 = (s16[264,256]{1,0:T(8,128)(2,1)S(1)}, s16[264,256]{1,0:T(8,128)(2,1)S(1)}, u32[]{:S(2)}, u32[]{:S(2)}) collective-permute-start(s16[264,256]{1,0:T(8,128)(2,1)S(1)} %shard_map.75), channel_id=1, source_target_pairs={{0,12},{4,8},{8,4},{12,0},{16,28},{20,24},{24,20},{28,16},{1,13},{... | collective-permute-start | bytes 405512 | tf_op jit(solution)/shard_map/ppermute | solution.py:343
  26.8 33.5 %copy-start.2 = (bf16[1024,256]{1,0:T(8,128)(2,1)S(1)}, bf16[1024,256]{1,0:T(8,128)(2,1)}, u32[]{:S(2)}) copy-start(bf16[1024,256]{1,0:T(8,128)(2,1)} %w.3) | copy-start | bytes 1572868
  32.7 12.3 %collective-permute-start.16 = (s16[264,256]{1,0:T(8,128)(2,1)S(1)}, s16[264,256]{1,0:T(8,128)(2,1)S(1)}, u32[]{:S(2)}, u32[]{:S(2)}) collective-permute-start(s16[264,256]{1,0:T(8,128)(2,1)S(1)} %shard_map.76.sent), channel_id=1, source_target_pairs={{0,16},{4,20},{8,24},{12,28},{16,0},{20,4},{24,8},{28,12},{1,17},{... | collective-permute-start | bytes 405512 | tf_op jit(solution)/shard_map/ppermute | solution.py:343
  35.9 7.3 %collective-permute-start.6 = (f32[48,256]{1,0:T(8,128)S(1)}, f32[48,256]{1,0:T(8,128)S(1)}, u32[]{:S(2)}, u32[]{:S(2)}) collective-permute-start(f32[48,256]{1,0:T(8,128)S(1)} %shard_map.67.a), channel_id=1, source_target_pairs={{0,16},{4,20},{8,24},{12,28},{16,0},{20,4},{24,8},{28,12},{1,17},{... | collective-permute-start | bytes 147464 | tf_op jit(solution)/shard_map/ppermute | solution.py:343
  43.2 7.0 %collective-permute-start.9 = (f32[48,256]{1,0:T(8,128)S(1)}, f32[48,256]{1,0:T(8,128)S(1)}, u32[]{:S(2)}, u32[]{:S(2)}) collective-permute-start(f32[48,256]{1,0:T(8,128)S(1)} %shard_map.68.own), channel_id=1, source_target_pairs={{0,12},{4,8},{8,4},{12,0},{16,28},{20,24},{24,20},{28,16},{1,13},{... | collective-permute-start | bytes 147464 | tf_op jit(solution)/shard_map/ppermute | solution.py:343
  45.3 15.3 %collective-permute-start.19 = (s16[1,264,256]{2,1,0:T(8,128)(2,1)S(1)}, s16[1,264,256]{2,1,0:T(8,128)(2,1)S(1)}, u32[]{:S(2)}, u32[]{:S(2)}) collective-permute-start(s16[1,264,256]{2,1,0:T(8,128)(2,1)S(1)} %shard_map.77.own), channel_id=1, source_target_pairs={{0,12},{4,8},{8,4},{12,0},{16,28},{20,24},{24,20},{28,16},{1,13},{... | collective-permute-start | bytes 405512 | tf_op jit(solution)/shard_map/ppermute | solution.py:343
  46.6 14.1 %collective-permute-start.18 = (s16[1,264,256]{2,1,0:T(8,128)(2,1)S(1)}, s16[1,264,256]{2,1,0:T(8,128)(2,1)S(1)}, u32[]{:S(2)}, u32[]{:S(2)}) collective-permute-start(s16[1,264,256]{2,1,0:T(8,128)(2,1)S(1)} %shard_map.77.own), channel_id=1, source_target_pairs={{0,8},{4,12},{8,0},{12,4},{16,24},{20,28},{24,16},{28,20},{1,9},{5... | collective-permute-start | bytes 405512 | tf_op jit(solution)/shard_map/ppermute | solution.py:343
  47.2 13.4 %collective-permute-start.17 = (s16[1,264,256]{2,1,0:T(8,128)(2,1)S(1)}, s16[1,264,256]{2,1,0:T(8,128)(2,1)S(1)}, u32[]{:S(2)}, u32[]{:S(2)}) collective-permute-start(s16[1,264,256]{2,1,0:T(8,128)(2,1)S(1)} %shard_map.77.own), channel_id=1, source_target_pairs={{0,4},{4,0},{8,12},{12,8},{16,20},{20,16},{24,28},{28,24},{1,5},{5... | collective-permute-start | bytes 405512 | tf_op jit(solution)/shard_map/ppermute | solution.py:343
  48.8 6.1 %collective-permute-start.8 = (f32[48,256]{1,0:T(8,128)S(1)}, f32[48,256]{1,0:T(8,128)S(1)}, u32[]{:S(2)}, u32[]{:S(2)}) collective-permute-start(f32[48,256]{1,0:T(8,128)S(1)} %shard_map.68.own), channel_id=1, source_target_pairs={{0,8},{4,12},{8,0},{12,4},{16,24},{20,28},{24,16},{28,20},{1,9},{5... | collective-permute-start | bytes 147464 | tf_op jit(solution)/shard_map/ppermute | solution.py:343
  50.3 5.2 %collective-permute-start.7 = (f32[48,256]{1,0:T(8,128)S(1)}, f32[48,256]{1,0:T(8,128)S(1)}, u32[]{:S(2)}, u32[]{:S(2)}) collective-permute-start(f32[48,256]{1,0:T(8,128)S(1)} %shard_map.68.own), channel_id=1, source_target_pairs={{0,4},{4,0},{8,12},{12,8},{16,20},{20,16},{24,28},{28,24},{1,5},{5... | collective-permute-start | bytes 147464 | tf_op jit(solution)/shard_map/ppermute | solution.py:343
  55.5 3.5 %collective-permute-start.12 = (bf16[48,256]{1,0:T(8,128)(2,1)S(1)}, bf16[48,256]{1,0:T(8,128)(2,1)S(1)}, u32[]{:S(2)}, u32[]{:S(2)}) collective-permute-start(bf16[48,256]{1,0:T(8,128)(2,1)S(1)} %shard_map.69.here), channel_id=1, source_target_pairs={{0,3},{1,2},{2,1},{3,0},{4,7},{5,6},{6,5},{7,4},{8,11},{9,10},{10,... | collective-permute-start | bytes 73736 | tf_op jit(solution)/shard_map/ppermute | solution.py:343
  56.4 3.8 %collective-permute-start.11 = (bf16[48,256]{1,0:T(8,128)(2,1)S(1)}, bf16[48,256]{1,0:T(8,128)(2,1)S(1)}, u32[]{:S(2)}, u32[]{:S(2)}) collective-permute-start(bf16[48,256]{1,0:T(8,128)(2,1)S(1)} %shard_map.69.here), channel_id=1, source_target_pairs={{0,2},{1,3},{2,0},{3,1},{4,6},{5,7},{6,4},{7,5},{8,10},{9,11},{10,... | collective-permute-start | bytes 73736 | tf_op jit(solution)/shard_map/ppermute | solution.py:343
  59.0 1.3 %collective-permute-start.10 = (bf16[48,256]{1,0:T(8,128)(2,1)S(1)}, bf16[48,256]{1,0:T(8,128)(2,1)S(1)}, u32[]{:S(2)}, u32[]{:S(2)}) collective-permute-start(bf16[48,256]{1,0:T(8,128)(2,1)S(1)} %shard_map.69.here), channel_id=1, source_target_pairs={{0,1},{1,0},{2,3},{3,2},{4,5},{5,4},{6,7},{7,6},{8,9},{9,8},{10,11... | collective-permute-start | bytes 73736 | tf_op jit(solution)/shard_map/ppermute | solution.py:343
  (1 other events, 0.8 us)

commit v9 on v8

--- a/solution.py
+++ b/solution.py
@@ -13,7 +13,7 @@
 BF16 = jnp.bfloat16
 VMEM = pl.BlockSpec(memory_space=pltpu.VMEM)
 HBM = pl.BlockSpec(memory_space=pltpu.HBM)
-PIECES = 2
+PIECES = 1
 TABLE = 8
 
 
@@ -125,7 +125,8 @@
 
 
 def core_index():
-    return lax.axis_index("term") & 1
+    term = lax.axis_index("term")
+    return (term ^ (term >> (lax.axis_size("term").bit_length() - 2))) & 1
 
 
 def term_bit(bit):
@@ -384,14 +385,14 @@
         g_keep = call(add_body, like(pk, k), (g_keep, g_got))
         g_got = over_term(g_keep, bit)
     g_sum = call(add_body, like(pk, k), (g_keep, g_got))
-    g_far = over_term(g_sum, term_bits - 1)
+    g_far = swap(g_sum, "term", n_term, 1 | (1 << (term_bits - 1)))
     n_keep, masked_own = numer(False, g_sum)
     h_old = call(half_h_body, like(k, half, dtype=BF16), (h,))
     for bit in range(1, term_bits - 1):
         n_keep = call(add_body, like(k, half), (n_keep, n_got))
         n_got = over_term(n_keep, bit)
     n_sum = call(code_sum_body, like(k + TABLE, half, dtype=jnp.int16), (n_keep, n_got))
-    n_far = over_term(n_sum, term_bits - 1)
+    n_far = swap(n_sum, "term", n_term, 1 | (1 << (term_bits - 1)))
     g_mine = call(round_add_body, like(pk, k, dtype=BF16), (g_sum, g_far))
     g_other = over_term(g_mine, 0)
     h_own = call(new_h_body, like(k, half, dtype=BF16), (n_sum, n_far, g_mine, g_other, h_old))
@@ -433,8 +434,8 @@
         grams[away] = over_doc(gram, away)
     g_half = call(gram_quad_body, like(pk // 2, k, dtype=BF16), (gram, grams[1], grams[2], grams[3]))
     far = term_bits - 1
-    g_far = over_term(g_half, far)
-    g_across = swap(g_half, "term", n_term, 1 | (1 << far))
+    g_far = swap(g_half, "term", n_term, 1 | (1 << far))
+    g_across = over_term(g_half, far)
     g_near = over_term(g_half, 0)
     body = functools.partial(ratio_body, side_bit=far)
     ratio = call(body, like(terms, k), (g_half, g_near, g_far, g_across, w), flops=flops // 4)

time: 61.8 us -> 62 us (level)
  transfers between devices with their start and end apart: 20 -> 20, of which waited for: 12 -> 13; matrix products, arithmetic and copies ran while one was open for 0% -> 0% of each run, Pallas kernels for 6% -> 6%
where the time goes in v9:
time: 62 us; the launch traced here: 61.8 us
  waiting for transfers between devices  32.1 us (52%)
  starting transfers between devices  19.8 us (32%)
  Pallas kernels  7.36 us (12%)
  local copies, waits for them, and re-layouts  1.67 us (3%)
  between operations  0.82 us (1%)
    ppermute x20, waiting for transfers between devices, swap(): return lax.ppermute(x, axis, [(i, i ^ away) for i in range(size)])  32.1 us
    ppermute x20, starting transfers between devices, swap(): return lax.ppermute(x, axis, [(i, i ^ away) for i in range(size)])  19.8 us
    pallas_call x21, Pallas kernels, call(): pl.pallas_call(body, out_shape=out, in_specs=[VMEM] * len(args), out_spec...  7.36 us
    unnamed x10, local copies, waits for them, and re-layouts  1.67 us
  transfers between devices with their start and end apart: 20, of which 13 were waited for; matrix products, arithmetic and copies ran while one was open for 0% of the time, Pallas kernels for 6%

profile of v9, /device:TPU:0, one launch (start us, length us, event | category | flops | bytes accessed | tf_op | source)
XLA Modules:
  0.0 61.8 jit_solution(7850022331050852496)
XLA Ops:
  0.7 1.2 %copy-done.1 = bf16[1024,256]{1,0:T(8,128)(2,1)S(1)} copy-done((bf16[1024,256]{1,0:T(8,128)(2,1)S(1)}, bf16[1024,256]{1,0:T(8,128)(2,1)}, u32[]{:S(2)}) %copy-start.1) | copy-done | bytes 524312
  3.9 1.6 %collective-permute-done.b = f32[96,256]{1,0:T(8,128)S(1)} collective-permute-done((f32[96,256]{1,0:T(8,128)S(1)}, f32[96,256]{1,0:T(8,128)S(1)}, u32[]{:S(2)}, u32[]{:S(2)}) %collective-permute-start) | collective-permute-done | bytes 98336 | tf_op jit(solution)/shard_map/ppermute | solution.py:344
  5.5 0.6 shard_map.61
  6.5 2.7 %collective-permute-start.2 = (s16[264,512]{1,0:T(8,128)(2,1)S(1)}, s16[264,512]{1,0:T(8,128)(2,1)S(1)}, u32[]{:S(2)}, u32[]{:S(2)}) collective-permute-start(s16[264,512]{1,0:T(8,128)(2,1)S(1)} %shard_map.63.mine), channel_id=1, source_target_pairs={{0,3},{1,2},{2,1},{3,0},{4,7},{5,6},{6,5},{7,4},{8,11},{9,10},{10,... | collective-permute-start | bytes 811016 | tf_op jit(solution)/shard_map/ppermute | solution.py:344
  9.2 8.6 %collective-permute-done.3.b = f32[96,256]{1,0:T(8,128)S(1)} collective-permute-done((f32[96,256]{1,0:T(8,128)S(1)}, f32[96,256]{1,0:T(8,128)S(1)}, u32[]{:S(2)}, u32[]{:S(2)}) %collective-permute-start.3) | collective-permute-done | bytes 98336 | tf_op jit(solution)/shard_map/ppermute | solution.py:344
  18.2 0.9 %collective-permute-done.4.gram_other = bf16[96,256]{1,0:T(8,128)(2,1)S(1)} collective-permute-done((bf16[96,256]{1,0:T(8,128)(2,1)S(1)}, bf16[96,256]{1,0:T(8,128)(2,1)S(1)}, u32[]{:S(2)}, u32[]{:S(2)}) %collective-permute-start.4) | collective-permute-done | bytes 49184 | tf_op jit(solution)/shard_map/ppermute | solution.py:344
  20.4 0.8 %collective-permute-done.5.h = bf16[256,512]{1,0:T(8,128)(2,1)S(1)} collective-permute-done((bf16[256,512]{1,0:T(8,128)(2,1)S(1)}, bf16[256,512]{1,0:T(8,128)(2,1)S(1)}, u32[]{:S(2)}, u32[]{:S(2)}) %collective-permute-start.5) | collective-permute-done | bytes 262176 | tf_op jit(solution)/shard_map/ppermute | solution.py:344
  21.5 2.3 %collective-permute-start.13 = (s16[264,256]{1,0:T(8,128)(2,1)S(1)}, s16[264,256]{1,0:T(8,128)(2,1)S(1)}, u32[]{:S(2)}, u32[]{:S(2)}) collective-permute-start(s16[264,256]{1,0:T(8,128)(2,1)S(1)} %shard_map.73), channel_id=1, source_target_pairs={{0,4},{4,0},{8,12},{12,8},{16,20},{20,16},{24,28},{28,24},{1,5},{5... | collective-permute-start | bytes 405512 | tf_op jit(solution)/shard_map/ppermute | solution.py:344
  24.2 1.7 %collective-permute-start.14 = (s16[264,256]{1,0:T(8,128)(2,1)S(1)}, s16[264,256]{1,0:T(8,128)(2,1)S(1)}, u32[]{:S(2)}, u32[]{:S(2)}) collective-permute-start(s16[264,256]{1,0:T(8,128)(2,1)S(1)} %shard_map.74), channel_id=1, source_target_pairs={{0,8},{4,12},{8,0},{12,4},{16,24},{20,28},{24,16},{28,20},{1,9},{5... | collective-permute-start | bytes 405512 | tf_op jit(solution)/shard_map/ppermute | solution.py:344
  26.6 1.1 %collective-permute-done.13.refs_0_ = s16[264,256]{1,0:T(8,128)(2,1)S(1)} collective-permute-done((s16[264,256]{1,0:T(8,128)(2,1)S(1)}, s16[264,256]{1,0:T(8,128)(2,1)S(1)}, u32[]{:S(2)}, u32[]{:S(2)}) %collective-permute-start.13) | collective-permute-done | bytes 135200 | tf_op jit(solution)/shard_map/ppermute | solution.py:344
  27.7 3.0 %collective-permute-done.14.refs_1_ = s16[264,256]{1,0:T(8,128)(2,1)S(1)} collective-permute-done((s16[264,256]{1,0:T(8,128)(2,1)S(1)}, s16[264,256]{1,0:T(8,128)(2,1)S(1)}, u32[]{:S(2)}, u32[]{:S(2)}) %collective-permute-start.14) | collective-permute-done | bytes 135200 | tf_op jit(solution)/shard_map/ppermute | solution.py:344
  30.7 1.6 %collective-permute-done.15.refs_2_ = s16[264,256]{1,0:T(8,128)(2,1)S(1)} collective-permute-done((s16[264,256]{1,0:T(8,128)(2,1)S(1)}, s16[264,256]{1,0:T(8,128)(2,1)S(1)}, u32[]{:S(2)}, u32[]{:S(2)}) %collective-permute-start.15) | collective-permute-done | bytes 135200 | tf_op jit(solution)/shard_map/ppermute | solution.py:344
  32.6 2.8 %collective-permute-start.16 = (s16[264,256]{1,0:T(8,128)(2,1)S(1)}, s16[264,256]{1,0:T(8,128)(2,1)S(1)}, u32[]{:S(2)}, u32[]{:S(2)}) collective-permute-start(s16[264,256]{1,0:T(8,128)(2,1)S(1)} %shard_map.76.sent), channel_id=1, source_target_pairs={{0,16},{4,20},{8,24},{12,28},{16,0},{20,4},{24,8},{28,12},{1,17},{... | collective-permute-start | bytes 405512 | tf_op jit(solution)/shard_map/ppermute | solution.py:344
  36.0 7.1 %collective-permute-done.6.b = f32[48,256]{1,0:T(8,128)S(1)} collective-permute-done((f32[48,256]{1,0:T(8,128)S(1)}, f32[48,256]{1,0:T(8,128)S(1)}, u32[]{:S(2)}, u32[]{:S(2)}) %collective-permute-start.6) | collective-permute-done | bytes 49184 | tf_op jit(solution)/shard_map/ppermute | solution.py:344
  43.1 1.8 %collective-permute-start.9 = (f32[48,256]{1,0:T(8,128)S(1)}, f32[48,256]{1,0:T(8,128)S(1)}, u32[]{:S(2)}, u32[]{:S(2)}) collective-permute-start(f32[48,256]{1,0:T(8,128)S(1)} %shard_map.68.own), channel_id=1, source_target_pairs={{0,12},{4,8},{8,4},{12,0},{16,28},{20,24},{24,20},{28,16},{1,13},{... | collective-permute-start | bytes 147464 | tf_op jit(solution)/shard_map/ppermute | solution.py:344
  45.2 1.3 %collective-permute-start.19 = (s16[1,264,256]{2,1,0:T(8,128)(2,1)S(1)}, s16[1,264,256]{2,1,0:T(8,128)(2,1)S(1)}, u32[]{:S(2)}, u32[]{:S(2)}) collective-permute-start(s16[1,264,256]{2,1,0:T(8,128)(2,1)S(1)} %shard_map.77.own), channel_id=1, source_target_pairs={{0,12},{4,8},{8,4},{12,0},{16,28},{20,24},{24,20},{28,16},{1,13},{... | collective-permute-start | bytes 405512 | tf_op jit(solution)/shard_map/ppermute | solution.py:344
  46.5 0.7 %collective-permute-start.18 = (s16[1,264,256]{2,1,0:T(8,128)(2,1)S(1)}, s16[1,264,256]{2,1,0:T(8,128)(2,1)S(1)}, u32[]{:S(2)}, u32[]{:S(2)}) collective-permute-start(s16[1,264,256]{2,1,0:T(8,128)(2,1)S(1)} %shard_map.77.own), channel_id=1, source_target_pairs={{0,8},{4,12},{8,0},{12,4},{16,24},{20,28},{24,16},{28,20},{1,9},{5... | collective-permute-start | bytes 405512 | tf_op jit(solution)/shard_map/ppermute | solution.py:344
  47.1 1.6 %collective-permute-start.17 = (s16[1,264,256]{2,1,0:T(8,128)(2,1)S(1)}, s16[1,264,256]{2,1,0:T(8,128)(2,1)S(1)}, u32[]{:S(2)}, u32[]{:S(2)}) collective-permute-start(s16[1,264,256]{2,1,0:T(8,128)(2,1)S(1)} %shard_map.77.own), channel_id=1, source_target_pairs={{0,4},{4,0},{8,12},{12,8},{16,20},{20,16},{24,28},{28,24},{1,5},{5... | collective-permute-start | bytes 405512 | tf_op jit(solution)/shard_map/ppermute | solution.py:344
  48.8 1.4 %collective-permute-start.8 = (f32[48,256]{1,0:T(8,128)S(1)}, f32[48,256]{1,0:T(8,128)S(1)}, u32[]{:S(2)}, u32[]{:S(2)}) collective-permute-start(f32[48,256]{1,0:T(8,128)S(1)} %shard_map.68.own), channel_id=1, source_target_pairs={{0,8},{4,12},{8,0},{12,4},{16,24},{20,28},{24,16},{28,20},{1,9},{5... | collective-permute-start | bytes 147464 | tf_op jit(solution)/shard_map/ppermute | solution.py:344
  50.5 4.3 %collective-permute-done.8.two = f32[48,256]{1,0:T(8,128)S(1)} collective-permute-done((f32[48,256]{1,0:T(8,128)S(1)}, f32[48,256]{1,0:T(8,128)S(1)}, u32[]{:S(2)}, u32[]{:S(2)}) %collective-permute-start.8) | collective-permute-done | bytes 49184 | tf_op jit(solution)/shard_map/ppermute | solution.py:344
  55.4 1.6 %collective-permute-start.12 = (bf16[48,256]{1,0:T(8,128)(2,1)S(1)}, bf16[48,256]{1,0:T(8,128)(2,1)S(1)}, u32[]{:S(2)}, u32[]{:S(2)}) collective-permute-start(bf16[48,256]{1,0:T(8,128)(2,1)S(1)} %shard_map.69.here), channel_id=1, source_target_pairs={{0,2},{1,3},{2,0},{3,1},{4,6},{5,7},{6,4},{7,5},{8,10},{9,11},{10,... | collective-permute-start | bytes 73736 | tf_op jit(solution)/shard_map/ppermute | solution.py:344
  56.9 2.3 %collective-permute-done.12.across = bf16[48,256]{1,0:T(8,128)(2,1)S(1)} collective-permute-done((bf16[48,256]{1,0:T(8,128)(2,1)S(1)}, bf16[48,256]{1,0:T(8,128)(2,1)S(1)}, u32[]{:S(2)}, u32[]{:S(2)}) %collective-permute-start.12) | collective-permute-done | bytes 24608 | tf_op jit(solution)/shard_map/ppermute | solution.py:344
  59.3 0.8 %shard_map.79 = bf16[256,1024]{1,0:T(8,128)(2,1)} custom-call(bf16[256,512]{1,0:T(8,128)(2,1)S(1)} %collective-permute-done.5.h, bf16[256,512]{1,0:T(8,128)(2,1)S(1)} %shard_map.66.h_own.h), custom_call_target="tpu_custom_call" | custom-call | flops 1048576 | bytes 1048576 | tf_op jit(solution)/shard_map/pallas_call | solution.py:29
  60.8 1.0 %shard_map.78 = bf16[1024,256]{1,0:T(8,128)(2,1)} custom-call(f32[1024,256]{1,0:T(8,128)S(1)} %shard_map.70.ratio, s16[1,264,256]{2,1,0:T(8,128)(2,1)S(1)} %shard_map.77.own, s16[1,264,256]{2,1,0:T(8,128)(2,1)S(1)} %collective-permute-done.17.one, s16[1,264,256]{2,1,0:T(8,128)(2,1)S(1)} %collective-permute-done.18.two, ...), custom_call_target="tpu_custom_call" | custom-call | flops 1048576 | bytes 1048576 | tf_op jit(solution)/shard_map/pallas_call | solution.py:29
  (47 shorter events, 8.4 us)
Async XLA Ops:
  0.6 1.7 %copy-start = (bf16[1024,1024]{1,0:T(8,128)(2,1)S(1)}, bf16[1024,1024]{1,0:T(8,128)(2,1)}, u32[]{:S(2)}) copy-start(bf16[1024,1024]{1,0:T(8,128)(2,1)} %m.3) | copy-start | bytes 6291460
  0.6 1.2 %copy-start.1 = (bf16[1024,256]{1,0:T(8,128)(2,1)S(1)}, bf16[1024,256]{1,0:T(8,128)(2,1)}, u32[]{:S(2)}) copy-start(bf16[1024,256]{1,0:T(8,128)(2,1)} %w.3) | copy-start | bytes 1572868
  3.3 2.9 %collective-permute-start.1 = (f32[256,512]{1,0:T(8,128)S(1)}, f32[256,512]{1,0:T(8,128)S(1)}, u32[]{:S(2)}, u32[]{:S(2)}) collective-permute-start(f32[256,512]{1,0:T(8,128)S(1)} %get-tuple-element.13), channel_id=1, source_target_pairs={{0,1},{1,0},{2,3},{3,2},{4,5},{5,4},{6,7},{7,6},{8,9},{9,8},{10,11... | collective-permute-start | bytes 1572872 | tf_op jit(solution)/shard_map/ppermute | solution.py:344
  3.8 1.7 %collective-permute-start = (f32[96,256]{1,0:T(8,128)S(1)}, f32[96,256]{1,0:T(8,128)S(1)}, u32[]{:S(2)}, u32[]{:S(2)}) collective-permute-start(f32[96,256]{1,0:T(8,128)S(1)} %get-tuple-element.11), channel_id=1, source_target_pairs={{0,1},{1,0},{2,3},{3,2},{4,5},{5,4},{6,7},{7,6},{8,9},{9,8},{10,11... | collective-permute-start | bytes 294920 | tf_op jit(solution)/shard_map/ppermute | solution.py:344
  5.5 12.7 %copy-start.3 = (bf16[256,1024]{1,0:T(8,128)(2,1)S(1)}, bf16[256,1024]{1,0:T(8,128)(2,1)}, u32[]{:S(2)}) copy-start(bf16[256,1024]{1,0:T(8,128)(2,1)} %h.1) | copy-start | bytes 1572868
  6.5 12.6 %collective-permute-start.2 = (s16[264,512]{1,0:T(8,128)(2,1)S(1)}, s16[264,512]{1,0:T(8,128)(2,1)S(1)}, u32[]{:S(2)}, u32[]{:S(2)}) collective-permute-start(s16[264,512]{1,0:T(8,128)(2,1)S(1)} %shard_map.63.mine), channel_id=1, source_target_pairs={{0,3},{1,2},{2,1},{3,0},{4,7},{5,6},{6,5},{7,4},{8,11},{9,10},{10,... | collective-permute-start | bytes 811016 | tf_op jit(solution)/shard_map/ppermute | solution.py:344
  9.1 8.7 %collective-permute-start.3 = (f32[96,256]{1,0:T(8,128)S(1)}, f32[96,256]{1,0:T(8,128)S(1)}, u32[]{:S(2)}, u32[]{:S(2)}) collective-permute-start(f32[96,256]{1,0:T(8,128)S(1)} %shard_map.60.refs_0_.a), channel_id=1, source_target_pairs={{0,3},{1,2},{2,1},{3,0},{4,7},{5,6},{6,5},{7,4},{8,11},{9,10},{10,... | collective-permute-start | bytes 294920 | tf_op jit(solution)/shard_map/ppermute | solution.py:344
  17.8 1.3 %collective-permute-start.4 = (bf16[96,256]{1,0:T(8,128)(2,1)S(1)}, bf16[96,256]{1,0:T(8,128)(2,1)S(1)}, u32[]{:S(2)}, u32[]{:S(2)}) collective-permute-start(bf16[96,256]{1,0:T(8,128)(2,1)S(1)} %shard_map.64.gram_mine), channel_id=1, source_target_pairs={{0,1},{1,0},{2,3},{3,2},{4,5},{5,4},{6,7},{7,6},{8,9},{9,8},{10,11... | collective-permute-start | bytes 147464 | tf_op jit(solution)/shard_map/ppermute | solution.py:344
  19.5 1.6 %collective-permute-start.5 = (bf16[256,512]{1,0:T(8,128)(2,1)S(1)}, bf16[256,512]{1,0:T(8,128)(2,1)S(1)}, u32[]{:S(2)}, u32[]{:S(2)}) collective-permute-start(bf16[256,512]{1,0:T(8,128)(2,1)S(1)} %shard_map.66.h_own.h), channel_id=1, source_target_pairs={{0,1},{1,0},{2,3},{3,2},{4,5},{5,4},{6,7},{7,6},{8,9},{9,8},{10,11... | collective-permute-start | bytes 786440 | tf_op jit(solution)/shard_map/ppermute | solution.py:344
  21.5 6.2 %collective-permute-start.13 = (s16[264,256]{1,0:T(8,128)(2,1)S(1)}, s16[264,256]{1,0:T(8,128)(2,1)S(1)}, u32[]{:S(2)}, u32[]{:S(2)}) collective-permute-start(s16[264,256]{1,0:T(8,128)(2,1)S(1)} %shard_map.73), channel_id=1, source_target_pairs={{0,4},{4,0},{8,12},{12,8},{16,20},{20,16},{24,28},{28,24},{1,5},{5... | collective-permute-start | bytes 405512 | tf_op jit(solution)/shard_map/ppermute | solution.py:344
  24.2 6.5 %collective-permute-start.14 = (s16[264,256]{1,0:T(8,128)(2,1)S(1)}, s16[264,256]{1,0:T(8,128)(2,1)S(1)}, u32[]{:S(2)}, u32[]{:S(2)}) collective-permute-start(s16[264,256]{1,0:T(8,128)(2,1)S(1)} %shard_map.74), channel_id=1, source_target_pairs={{0,8},{4,12},{8,0},{12,4},{16,24},{20,28},{24,16},{28,20},{1,9},{5... | collective-permute-start | bytes 405512 | tf_op jit(solution)/shard_map/ppermute | solution.py:344
  26.2 6.0 %collective-permute-start.15 = (s16[264,256]{1,0:T(8,128)(2,1)S(1)}, s16[264,256]{1,0:T(8,128)(2,1)S(1)}, u32[]{:S(2)}, u32[]{:S(2)}) collective-permute-start(s16[264,256]{1,0:T(8,128)(2,1)S(1)} %shard_map.75), channel_id=1, source_target_pairs={{0,12},{4,8},{8,4},{12,0},{16,28},{20,24},{24,20},{28,16},{1,13},{... | collective-permute-start | bytes 405512 | tf_op jit(solution)/shard_map/ppermute | solution.py:344
  26.6 33.9 %copy-start.2 = (bf16[1024,256]{1,0:T(8,128)(2,1)S(1)}, bf16[1024,256]{1,0:T(8,128)(2,1)}, u32[]{:S(2)}) copy-start(bf16[1024,256]{1,0:T(8,128)(2,1)} %w.3) | copy-start | bytes 1572868
  32.6 12.3 %collective-permute-start.16 = (s16[264,256]{1,0:T(8,128)(2,1)S(1)}, s16[264,256]{1,0:T(8,128)(2,1)S(1)}, u32[]{:S(2)}, u32[]{:S(2)}) collective-permute-start(s16[264,256]{1,0:T(8,128)(2,1)S(1)} %shard_map.76.sent), channel_id=1, source_target_pairs={{0,16},{4,20},{8,24},{12,28},{16,0},{20,4},{24,8},{28,12},{1,17},{... | collective-permute-start | bytes 405512 | tf_op jit(solution)/shard_map/ppermute | solution.py:344
  35.8 7.3 %collective-permute-start.6 = (f32[48,256]{1,0:T(8,128)S(1)}, f32[48,256]{1,0:T(8,128)S(1)}, u32[]{:S(2)}, u32[]{:S(2)}) collective-permute-start(f32[48,256]{1,0:T(8,128)S(1)} %shard_map.67.a), channel_id=1, source_target_pairs={{0,16},{4,20},{8,24},{12,28},{16,0},{20,4},{24,8},{28,12},{1,17},{... | collective-permute-start | bytes 147464 | tf_op jit(solution)/shard_map/ppermute | solution.py:344
  43.1 7.0 %collective-permute-start.9 = (f32[48,256]{1,0:T(8,128)S(1)}, f32[48,256]{1,0:T(8,128)S(1)}, u32[]{:S(2)}, u32[]{:S(2)}) collective-permute-start(f32[48,256]{1,0:T(8,128)S(1)} %shard_map.68.own), channel_id=1, source_target_pairs={{0,12},{4,8},{8,4},{12,0},{16,28},{20,24},{24,20},{28,16},{1,13},{... | collective-permute-start | bytes 147464 | tf_op jit(solution)/shard_map/ppermute | solution.py:344
  45.2 15.6 %collective-permute-start.19 = (s16[1,264,256]{2,1,0:T(8,128)(2,1)S(1)}, s16[1,264,256]{2,1,0:T(8,128)(2,1)S(1)}, u32[]{:S(2)}, u32[]{:S(2)}) collective-permute-start(s16[1,264,256]{2,1,0:T(8,128)(2,1)S(1)} %shard_map.77.own), channel_id=1, source_target_pairs={{0,12},{4,8},{8,4},{12,0},{16,28},{20,24},{24,20},{28,16},{1,13},{... | collective-permute-start | bytes 405512 | tf_op jit(solution)/shard_map/ppermute | solution.py:344
  46.5 14.3 %collective-permute-start.18 = (s16[1,264,256]{2,1,0:T(8,128)(2,1)S(1)}, s16[1,264,256]{2,1,0:T(8,128)(2,1)S(1)}, u32[]{:S(2)}, u32[]{:S(2)}) collective-permute-start(s16[1,264,256]{2,1,0:T(8,128)(2,1)S(1)} %shard_map.77.own), channel_id=1, source_target_pairs={{0,8},{4,12},{8,0},{12,4},{16,24},{20,28},{24,16},{28,20},{1,9},{5... | collective-permute-start | bytes 405512 | tf_op jit(solution)/shard_map/ppermute | solution.py:344
  47.1 13.7 %collective-permute-start.17 = (s16[1,264,256]{2,1,0:T(8,128)(2,1)S(1)}, s16[1,264,256]{2,1,0:T(8,128)(2,1)S(1)}, u32[]{:S(2)}, u32[]{:S(2)}) collective-permute-start(s16[1,264,256]{2,1,0:T(8,128)(2,1)S(1)} %shard_map.77.own), channel_id=1, source_target_pairs={{0,4},{4,0},{8,12},{12,8},{16,20},{20,16},{24,28},{28,24},{1,5},{5... | collective-permute-start | bytes 405512 | tf_op jit(solution)/shard_map/ppermute | solution.py:344
  48.8 6.1 %collective-permute-start.8 = (f32[48,256]{1,0:T(8,128)S(1)}, f32[48,256]{1,0:T(8,128)S(1)}, u32[]{:S(2)}, u32[]{:S(2)}) collective-permute-start(f32[48,256]{1,0:T(8,128)S(1)} %shard_map.68.own), channel_id=1, source_target_pairs={{0,8},{4,12},{8,0},{12,4},{16,24},{20,28},{24,16},{28,20},{1,9},{5... | collective-permute-start | bytes 147464 | tf_op jit(solution)/shard_map/ppermute | solution.py:344
  50.2 5.2 %collective-permute-start.7 = (f32[48,256]{1,0:T(8,128)S(1)}, f32[48,256]{1,0:T(8,128)S(1)}, u32[]{:S(2)}, u32[]{:S(2)}) collective-permute-start(f32[48,256]{1,0:T(8,128)S(1)} %shard_map.68.own), channel_id=1, source_target_pairs={{0,4},{4,0},{8,12},{12,8},{16,20},{20,16},{24,28},{28,24},{1,5},{5... | collective-permute-start | bytes 147464 | tf_op jit(solution)/shard_map/ppermute | solution.py:344
  55.4 3.9 %collective-permute-start.12 = (bf16[48,256]{1,0:T(8,128)(2,1)S(1)}, bf16[48,256]{1,0:T(8,128)(2,1)S(1)}, u32[]{:S(2)}, u32[]{:S(2)}) collective-permute-start(bf16[48,256]{1,0:T(8,128)(2,1)S(1)} %shard_map.69.here), channel_id=1, source_target_pairs={{0,2},{1,3},{2,0},{3,1},{4,6},{5,7},{6,4},{7,5},{8,10},{9,11},{10,... | collective-permute-start | bytes 73736 | tf_op jit(solution)/shard_map/ppermute | solution.py:344
  56.9 3.3 %collective-permute-start.11 = (bf16[48,256]{1,0:T(8,128)(2,1)S(1)}, bf16[48,256]{1,0:T(8,128)(2,1)S(1)}, u32[]{:S(2)}, u32[]{:S(2)}) collective-permute-start(bf16[48,256]{1,0:T(8,128)(2,1)S(1)} %shard_map.69.here), channel_id=1, source_target_pairs={{0,3},{1,2},{2,1},{3,0},{4,7},{5,6},{6,5},{7,4},{8,11},{9,10},{10,... | collective-permute-start | bytes 73736 | tf_op jit(solution)/shard_map/ppermute | solution.py:344
  59.3 1.2 %collective-permute-start.10 = (bf16[48,256]{1,0:T(8,128)(2,1)S(1)}, bf16[48,256]{1,0:T(8,128)(2,1)S(1)}, u32[]{:S(2)}, u32[]{:S(2)}) collective-permute-start(bf16[48,256]{1,0:T(8,128)(2,1)S(1)} %shard_map.69.here), channel_id=1, source_target_pairs={{0,1},{1,0},{2,3},{3,2},{4,5},{5,4},{6,7},{7,6},{8,9},{9,8},{10,11... | collective-permute-start | bytes 73736 | tf_op jit(solution)/shard_map/ppermute | solution.py:344
  (1 other events, 0.8 us)
